TPU v7x, 32 devices: a whole 2x2x4 slice. The times are simulated.
32 devices in a mesh: groups: 2 (over x), mp: 16 (over z, y, core).
Axes of the slice: x: 2, y: 2, z: 4, core: 2. Of those that a mesh axis runs over, the one named last changes fastest.
Arguments:
- tokens: bfloat16 [256, 4096], P('groups'), parts along dimension 0, may hold values from -6 to 6
- up_values: bfloat16 [4096, 16384], P(None, 'mp'), may hold values from -0.09375 to 0.09375
- up_scale: int32 [32, 128], P(None, 'mp'), may hold values from -1 to 1
- diag_blocks: bfloat16 [128, 128, 128], P('mp'), may hold values from -0.5 to 0.5
- partner_blocks: bfloat16 [7, 128, 128, 128], P(None, 'mp'), may hold values from -0.1875 to 0.1875
- pattern: int32 [7, 128], P(None, 'mp'), may hold values 0 or 1
- down_values: bfloat16 [16384, 4096], P('mp'), may hold values from -0.046875 to 0.046875
- down_scale: int32 [128, 32], P('mp'), may hold values from -1 to 1
- norm_gain: float32 [4096], replicated, may hold values from 0.5 to 1.5
- vocab_table: bfloat16 [32768, 4096], P('mp'), may hold values from -0.359375 to 0.359375
- teacher_ids: int32 [256, 8], P('groups'), parts along dimension 0, may hold values from 0 to 32767, as said below
- teacher_logits: float32 [256, 8], P('groups'), parts along dimension 0, may hold values from -12 to 12
Outputs:
- mean_loss: float32 [2], P('groups'), parts along dimension 0
- grad_up: float32 [8192, 16384], P('groups', 'mp'), parts along dimension 0
- grad_down: float32 [32768, 4096], P(('groups', 'mp')), parts along dimension 0
- grad_diag: float32 [256, 128, 128], P(('groups', 'mp')), parts along dimension 0
- grad_partner: float32 [14, 128, 128, 128], P('groups', 'mp'), parts along dimension 0
There are 2 independent parts, one for each index of `groups`. A program takes and returns all parts, laid end to end along the dimension named above; an argument that names none is the same for every part. Nothing has to cross between parts.
Inputs may be any that keep to these rules, and one draw needn't show every extreme that they name: `teacher_ids`: the 8 ids of one token are distinct.
All inputs are finite; a program needn't handle non-finite values. No bound on the sum of `pattern` on one device may be relied on, other than what follows from the above.
Results may differ from a plain program's by a relative error of at most 0.012.
Values may be sent and summed in bfloat16 or wider, within the bound.
No kernel may reach another device: no remote copies, remote signals or barrier semaphores. Data moves between devices by JAX's collectives and lax.ppermute only.
A program may use at most 192 MiB of HBM per device.

v0:
```python
import jax
import jax.numpy as jnp
from jax import lax
from jax.sharding import PartitionSpec as P


def swapped(block, axis, stride):
    count = lax.axis_size(axis)
    route = []
    for low in range(count):
        high = low | 1 << stride
        if high != low and high < count:
            route += [(low, high), (high, low)]
    return lax.ppermute(block, axis, route)


def scaled_weight(values, exponents, block_width):
    factors = jnp.exp2(exponents.astype(jnp.float32))
    factors = jnp.repeat(jnp.repeat(factors, block_width, axis=0), block_width, axis=1)
    return (values.astype(jnp.float32) * factors).astype(jnp.bfloat16)


def flip_blocks(blocks, bit_level, position):
    old_shape = blocks.shape
    block_count = old_shape[position]
    split_shape = (
        old_shape[:position]
        + (block_count >> bit_level + 1, 2, 1 << bit_level)
        + old_shape[position + 1 :]
    )
    return jnp.flip(blocks.reshape(split_shape), position + 1).reshape(old_shape)


def silu_slope(pre_value):
    sigmoid_value = jax.nn.sigmoid(pre_value)
    return sigmoid_value * (1.0 + pre_value * (1.0 - sigmoid_value))


def normalize(stream, norm_gain):
    values = stream.astype(jnp.float32)
    inverse = lax.rsqrt(jnp.mean(values * values, axis=1, keepdims=True) + 1e-05)
    return (values * inverse * norm_gain).astype(jnp.bfloat16)


def normalize_back(stream, norm_gain, upstream):
    values = stream.astype(jnp.float32)
    inverse = lax.rsqrt(jnp.mean(values * values, axis=1, keepdims=True) + 1e-05)
    unit_rows = values * inverse
    scaled = upstream * norm_gain
    return (
        inverse * (scaled - unit_rows * jnp.mean(scaled * unit_rows, axis=1, keepdims=True))
    ).astype(jnp.bfloat16)


def fetch_acts(blocks, bit_level, local_bits):
    if bit_level < local_bits:
        return flip_blocks(blocks, bit_level, 1)
    return swapped(blocks, "mp", bit_level - local_bits)


def fetch_terms(blocks, bit_level, local_bits):
    if bit_level < local_bits:
        return flip_blocks(blocks, bit_level, 1)
    return swapped(blocks.astype(jnp.bfloat16), "mp", bit_level - local_bits).astype(blocks.dtype)


def on_device(
    tokens,
    up_values,
    up_scale,
    diag_blocks,
    partner_blocks,
    pattern,
    down_values,
    down_scale,
    norm_gain,
    vocab_table,
    teacher_ids,
    teacher_logits,
):
    block_width = diag_blocks.shape[-1]
    token_count = tokens.shape[0]
    local_blocks = diag_blocks.shape[0]
    levels = partner_blocks.shape[0]
    local_bits = local_blocks.bit_length() - 1
    up_eff = scaled_weight(up_values, up_scale, block_width)
    down_eff = scaled_weight(down_values, down_scale, block_width)
    masked = (
        partner_blocks.astype(jnp.float32) * pattern.astype(jnp.float32)[:, :, None, None]
    ).astype(jnp.bfloat16)
    pre_act = jnp.dot(tokens, up_eff, preferred_element_type=jnp.float32)
    activated = jax.nn.silu(pre_act).astype(jnp.bfloat16)
    act_blocks = activated.reshape(token_count, local_blocks, block_width)
    mixed_blocks = jnp.einsum(
        "tlb,lbc->tlc", act_blocks, diag_blocks, preferred_element_type=jnp.float32
    )
    partners = []
    for bit_level in range(levels):
        partner = fetch_acts(act_blocks, bit_level, local_bits)
        partners.append(partner)
        mixed_blocks = mixed_blocks + jnp.einsum(
            "tlb,lbc->tlc", partner, masked[bit_level], preferred_element_type=jnp.float32
        )
    mixed = mixed_blocks.astype(jnp.bfloat16).reshape(token_count, -1)
    shard_rows = token_count // lax.axis_size("mp")
    shard_start = lax.axis_index("mp") * shard_rows
    delta_rows = lax.psum_scatter(
        jnp.dot(mixed, down_eff, preferred_element_type=jnp.float32),
        "mp",
        scatter_dimension=0,
        tiled=True,
    )
    own_tokens = lax.dynamic_slice_in_dim(tokens, shard_start, shard_rows, 0)
    stream_rows = (own_tokens.astype(jnp.float32) + delta_rows).astype(jnp.bfloat16)
    stream = lax.all_gather(stream_rows, "mp", axis=0, tiled=True)
    normed = normalize(stream, norm_gain)
    vocab_rows = vocab_table.shape[0]
    offset = teacher_ids - lax.axis_index("mp") * vocab_rows
    row_numbers = lax.broadcasted_iota(jnp.int32, (1, 1, vocab_rows), 2)
    hits = offset[:, :, None] == row_numbers
    local_scores = jnp.einsum("td,vd->tv", normed, vocab_table, preferred_element_type=jnp.float32)
    picked_scores = jnp.sum(jnp.where(hits, local_scores[:, None, :], 0.0), axis=2)
    scores = lax.psum(picked_scores, "mp")
    log_student = scores - jnp.log(jnp.sum(jnp.exp(scores), axis=1, keepdims=True))
    teacher_exp = jnp.exp(teacher_logits)
    teacher = teacher_exp / jnp.sum(teacher_exp, axis=1, keepdims=True)
    mean_loss = (-jnp.sum(teacher * log_student) / token_count).reshape(1)
    score_grad = (jnp.exp(log_student) - teacher).astype(jnp.bfloat16)
    spread_grad = jnp.sum(
        jnp.where(hits, score_grad.astype(jnp.float32)[:, :, None], 0.0), axis=1
    ).astype(jnp.bfloat16)
    local_upstream = jnp.dot(spread_grad, vocab_table, preferred_element_type=jnp.float32)
    upstream = lax.psum(local_upstream, "mp")
    stream_grad = normalize_back(stream, norm_gain, upstream)
    grad_down = jnp.einsum("th,td->hd", mixed, stream_grad, preferred_element_type=jnp.float32)
    mixed_grad = jnp.einsum(
        "td,hd->th", stream_grad, down_eff, preferred_element_type=jnp.float32
    ).astype(jnp.bfloat16)
    grad_blocks = mixed_grad.reshape(token_count, local_blocks, block_width)
    grad_diag = jnp.einsum(
        "tlb,tlc->lbc", act_blocks, grad_blocks, preferred_element_type=jnp.float32
    )
    act_grad = jnp.einsum(
        "tlc,lbc->tlb", grad_blocks, diag_blocks, preferred_element_type=jnp.float32
    )
    partner_grads = []
    for bit_level in range(levels):
        partner_grads.append(
            jnp.einsum(
                "tlb,tlc->lbc", partners[bit_level], grad_blocks, preferred_element_type=jnp.float32
            )
            * pattern[bit_level].astype(jnp.float32)[:, None, None]
        )
        outgoing = jnp.einsum(
            "tlc,lbc->tlb", grad_blocks, masked[bit_level], preferred_element_type=jnp.float32
        )
        act_grad = act_grad + fetch_terms(outgoing, bit_level, local_bits)
    pre_grad = (act_grad.reshape(token_count, -1) * silu_slope(pre_act)).astype(jnp.bfloat16)
    grad_up = jnp.einsum("td,th->dh", tokens, pre_grad, preferred_element_type=jnp.float32)
    return (mean_loss, grad_up, grad_down, grad_diag, jnp.stack(partner_grads))


def solution(mesh):
    return jax.shard_map(
        on_device,
        mesh=mesh,
        in_specs=(
            P("groups", None),
            P(None, "mp"),
            P(None, "mp"),
            P("mp", None, None),
            P(None, "mp", None, None),
            P(None, "mp"),
            P("mp", None),
            P("mp", None),
            P(),
            P("mp", None),
            P("groups", None),
            P("groups", None),
        ),
        out_specs=(
            P("groups"),
            P("groups", "mp"),
            P(("groups", "mp"), None),
            P(("groups", "mp"), None, None),
            P("groups", "mp", None, None),
        ),
        check_vma=False,
    )
```

profile of v0, /device:TPU:0, one launch (start us, length us, event | category | flops | bytes accessed | tf_op | source)
XLA Modules:
  0.0 426.8 jit_solution(9516157749034228818)
XLA Ops:
  7.2 0.7 multiply_exponential_fusion.1
  8.0 0.1 broadcast_in_dim.30
  8.2 4.6 %broadcast_in_dim.31 = f32[4096,8,128]{2,1,0:T(8,128)S(1)} broadcast(f32[4096,8]{1,0:T(8,128)S(1)} %bitcast.242), dimensions={0,1} | broadcast | bytes 16908288 | tf_op jit(solution)/shard_map/broadcast_in_dim | solution.py:19
  12.8 9.6 %multiply_convert_fusion.1 = (bf16[128,1024]{0,1:T(8,128)(2,1)S(1)}, f32[128,1024]{0,1:T(8,128)}) fusion(bf16[128,4096]{1,0:T(8,128)(2,1)S(1)} %copy-done.4, f32[512,8,8,128]{3,2,1,0:T(8,128)S(1)} %bitcast.235, bf16[4096,1024]{1,0:T(8,128)(2,1)} %param.13), kind=kOutput, calls=%fused_computation.81 | convolution fusion | flops 1086980096 | bytes 27000832 | tf_op jit(solution)/shard_map/dot_general | solution.py:91
  22.4 0.8 copy.111
  23.3 4.0 collective-permute-start.3
  27.3 1.6 collective-permute-start.2
  28.9 1.5 collective-permute-start.1
  30.4 3.8 copy.107
  34.2 2.1 multiply_convert_fusion
  36.3 1.0 convolution_bitcast_fusion.6
  37.4 1.0 convolution_bitcast_fusion.7
  38.4 0.2 convolution_bitcast_fusion.8
  38.6 1.5 fusion.15
  40.2 0.3 convolution_bitcast_fusion.2
  40.5 1.2 convolution_bitcast_fusion.3
  41.7 1.3 convolution_bitcast_fusion.4
  43.0 1.3 fusion.40
  44.3 16.1 %broadcast_in_dim.33 = f32[1024,32,128]{2,1,0:T(8,128)S(1)} broadcast(f32[1024,32]{1,0:T(8,128)S(1)} %bitcast.254), dimensions={0,1} | broadcast | bytes 16908288 | tf_op jit(solution)/shard_map/broadcast_in_dim | solution.py:19
  60.5 6.1 %copy-done.1 = f32[1024,32,128]{2,1,0:T(8,128)} copy-done((f32[1024,32,128]{2,1,0:T(8,128)}, f32[1024,32,128]{2,1,0:T(8,128)S(1)}, u32[]{:S(2)}) %copy-start.1) | copy-done | bytes 16777240
  66.7 14.9 %fusion.93 = f32[128,4096]{1,0:T(8,128)} fusion(bf16[128,1024]{0,1:T(8,128)(2,1)S(1)} %bitcast.243, f32[128,8,32,128]{3,2,1,0:T(8,128)S(1)} %bitcast.233, bf16[1024,4096]{1,0:T(8,128)(2,1)} %param.18), kind=kOutput, calls=%fused_computation.145 | convolution fusion | flops 1086324736 | bytes 27525120 | tf_op jit(solution)/shard_map/dot_general | solution.py:108
  81.6 62.2 %reduce-scatter.2.cloned.1.call-done = f32[8,4096]{1,0:T(8,128)} async-done(((f32[128,4096]{1,0:T(8,128)}), f32[8,4096]{1,0:T(8,128)}) %reduce-scatter.2.cloned.1.call-update) | async-done | bytes 131088 | tf_op jit(solution)/shard_map/reduce_scatter | solution.py:107
  143.8 1.5 add_convert_fusion
  145.4 0.1 copy.103
  145.5 0.5 exponential_reduce_fusion.1
  146.1 37.6 %all-gather.2.cloned.1.call-done = bf16[128,4096]{1,0:T(8,128)(2,1)} async-done(((bf16[8,4096]{1,0:T(8,128)(2,1)}), bf16[128,4096]{1,0:T(8,128)(2,1)}) %all-gather.2.cloned.1.call-update) | async-done | bytes 1048592 | tf_op jit(solution)/shard_map/all_gather | solution.py:115
  183.7 1.5 fusion.12
  185.2 0.6 copy-done.23
  185.8 11.8 %fusion.46 = f32[128,2048]{1,0:T(8,128)S(1)} fusion(bf16[2048,4096]{1,0:T(8,128)(2,1)} %param.21, bf16[128,4096]{1,0:T(8,128)(2,1)} %all-gather.2.cloned.1.call-done, f32[4096]{0:T(1024)S(1)} %copy-done.18, f32[128]{0:T(128)S(1)} %add_rsqrt_fusion), kind=kOutput, calls=%fused_computation.73 | convolution fusion | flops 2149580800 | bytes 18891264 | tf_op jit(solution)/shard_map/td,vd->tv/dot_general | solution.py:121
  197.6 1.1 select_reduce_fusion.1
  198.8 31.6 %psum.14 = f32[128,8]{0,1:T(8,128)S(1)} all-reduce(f32[128,8]{0,1:T(8,128)S(1)} %copy.115), channel_id=1, replica_groups=mesh['groups'=2,'mp'=16] {'mp'}, use_global_device_ids=true, to_apply=%region_4.5 | all-reduce | flops 1024 | bytes 8192 | tf_op jit(solution)/shard_map/psum | solution.py:123
  230.4 1.3 fusion.75
  231.8 3.2 select_reduce_fusion
  235.1 9.6 %fusion.96 = f32[128,4096]{1,0:T(8,128)} fusion(bf16[128,2048]{1,0:T(8,128)(2,1)S(1)} %select_reduce_fusion, bf16[2048,4096]{1,0:T(8,128)(2,1)} %param.21), kind=kOutput, calls=%fused_computation.147 | convolution fusion | flops 2147483648 | bytes 19398656 | tf_op jit(solution)/shard_map/dot_general | solution.py:132
  245.2 94.5 %all-reduce.2.cloned.1.call-done = f32[128,4096]{1,0:T(8,128)} async-done(((f32[128,4096]{1,0:T(8,128)}), f32[128,4096]{1,0:T(8,128)}) %all-reduce.2.cloned.1.call-update) | async-done | bytes 2097168 | tf_op jit(solution)/shard_map/psum | solution.py:133
  339.8 2.2 fusion.8
  342.0 0.5 fusion.11
  342.6 18.4 %fusion.45 = bf16[16,8,8,128]{3,2,1,0:T(8,128)(2,1)S(1)} fusion(bf16[128,4096]{1,0:T(8,128)(2,1)S(1)} %fusion.11, f32[128,8,32,128]{3,2,1,0:T(8,128)} %bitcast.234, bf16[1024,4096]{1,0:T(8,128)(2,1)} %param.18), kind=kOutput, calls=%fused_computation.72 | convolution fusion | flops 1086455808 | bytes 26476544 | tf_op jit(solution)/shard_map/td,hd->th/dot_general | solution.py:136
  361.0 1.0 fusion.44
  362.0 1.1 fusion.43
  363.1 1.0 fusion.42
  364.1 1.0 fusion.41
  365.1 1.1 fusion.66
  366.3 1.2 fusion.68
  367.4 1.1 fusion.70
  368.6 8.5 %fusion.95 = f32[1024,4096]{1,0:T(8,128)} fusion(bf16[128,1024]{0,1:T(8,128)(2,1)S(1)} %bitcast.244, bf16[128,4096]{1,0:T(8,128)(2,1)S(1)} %fusion.11), kind=kOutput, calls=%fused_computation.146 | convolution fusion | flops 1073741824 | bytes 18087936 | tf_op jit(solution)/shard_map/th,td->hd/dot_general | solution.py:135
  377.1 1.7 collective-permute-start.7
  378.8 1.3 collective-permute-start.6
  380.1 0.7 collective-permute-start.5
  380.8 0.2 fusion.36
  381.0 0.2 fusion.34
  381.3 0.2 fusion.32
  381.5 1.2 fusion.30
  382.7 1.2 fusion.28
  384.0 1.2 fusion.26
  385.2 1.2 fusion.60
  386.4 0.8 copy-done.19
  387.3 2.0 rev.27
  389.3 2.0 fusion.24
  391.3 0.1 collective-permute-done.6
  391.5 1.7 convert_add_fusion
  393.2 0.2 fusion.50
  393.4 8.1 %convolution_bitcast_fusion = f32[4096,1024]{0,1:T(8,128)} fusion(bf16[128,1024]{0,1:T(8,128)(2,1)S(1)} %fusion.50, bf16[128,4096]{1,0:T(8,128)(2,1)S(1)} %copy-done.5), kind=kOutput, calls=%fused_computation.4 | convolution fusion | flops 1073741824 | bytes 18087936 | tf_op jit(solution)/shard_map/td,th->dh/dot_general | solution.py:159
  401.5 17.4 %copy.144 = f32[4096,1024]{1,0:T(8,128)} copy(f32[4096,1024]{0,1:T(8,128)} %convolution_bitcast_fusion) | data formatting | bytes 33554432
  (83 shorter events, 0.8 us)
Async XLA Ops:
  7.2 31.5 %copy-start = (bf16[8,128,128]{2,1,0:T(8,128)(2,1)S(1)}, bf16[8,128,128]{2,1,0:T(8,128)(2,1)}, u32[]{:S(2)}) copy-start(bf16[8,128,128]{2,1,0:T(8,128)(2,1)} %param.15) | copy-start | bytes 786436
  7.2 136.6 %reduce-scatter.2.cloned.1.call-start = ((), (), s32[]{:S(2)}) async-start(), calls=%async_computation.1 | async-start | bytes 2228224 | tf_op jit(solution)/shard_map/reduce_scatter | solution.py:107
  8.2 4.6 %copy-start.4 = (bf16[128,4096]{1,0:T(8,128)(2,1)S(1)}, bf16[128,4096]{1,0:T(8,128)(2,1)}, u32[]{:S(2)}) copy-start(bf16[128,4096]{1,0:T(8,128)(2,1)} %param.12) | copy-start | bytes 3145732
  22.4 11.8 %copy-start.21 = (s32[7,8]{1,0:T(8,128)S(1)}, s32[7,8]{1,0:T(8,128)}, u32[]{:S(2)}) copy-start(s32[7,8]{1,0:T(8,128)} %param.17) | copy-start | bytes 676
  23.3 16.9 %collective-permute-start.3 = (bf16[128,8,128]{2,0,1:T(8,128)(2,1)}, bf16[128,8,128]{2,0,1:T(8,128)(2,1)S(1)}, u32[]{:S(2)}, u32[]{:S(2)}) collective-permute-start(bf16[128,8,128]{2,0,1:T(8,128)(2,1)} %copy.111), channel_id=1, source_target_pairs={{0,8},{8,0},{1,9},{9,1},{2,10},{10,2},{3,11},{11,3},{4,12},{12,4},... | collective-permute-start | bytes 786440 | tf_op jit(solution)/shard_map/ppermute | solution.py:14
  27.3 13.2 %collective-permute-start.2 = (bf16[128,8,128]{2,0,1:T(8,128)(2,1)}, bf16[128,8,128]{2,0,1:T(8,128)(2,1)}, u32[]{:S(2)}, u32[]{:S(2)}) collective-permute-start(bf16[128,8,128]{2,0,1:T(8,128)(2,1)} %copy.111), channel_id=1, source_target_pairs={{0,4},{4,0},{1,5},{5,1},{2,6},{6,2},{3,7},{7,3},{8,12},{12,8},{9,1... | collective-permute-start | bytes 786440 | tf_op jit(solution)/shard_map/ppermute | solution.py:14
  28.9 12.9 %collective-permute-start.1 = (bf16[128,8,128]{2,0,1:T(8,128)(2,1)}, bf16[128,8,128]{2,0,1:T(8,128)(2,1)}, u32[]{:S(2)}, u32[]{:S(2)}) collective-permute-start(bf16[128,8,128]{2,0,1:T(8,128)(2,1)} %copy.111), channel_id=1, source_target_pairs={{0,2},{2,0},{1,3},{3,1},{4,6},{6,4},{5,7},{7,5},{8,10},{10,8},{9,1... | collective-permute-start | bytes 786440 | tf_op jit(solution)/shard_map/ppermute | solution.py:14
  30.4 12.6 %collective-permute-start = (bf16[128,8,128]{2,0,1:T(8,128)(2,1)}, bf16[128,8,128]{2,0,1:T(8,128)(2,1)}, u32[]{:S(2)}, u32[]{:S(2)}) collective-permute-start(bf16[128,8,128]{2,0,1:T(8,128)(2,1)} %copy.111), channel_id=1, source_target_pairs={{0,1},{1,0},{2,3},{3,2},{4,5},{5,4},{6,7},{7,6},{8,9},{9,8},{10,11... | collective-permute-start | bytes 786440 | tf_op jit(solution)/shard_map/ppermute | solution.py:14
  34.2 4.4 %copy-start.8 = (bf16[128,1,2,4,128]{0,4,3,2,1:T(8,128)(2,1)}, bf16[128,1,2,4,128]{0,4,3,2,1:T(8,128)(2,1)S(1)}, u32[]{:S(2)}) copy-start(bf16[128,1,2,4,128]{0,4,3,2,1:T(8,128)(2,1)S(1)} %rev.26) | copy-start | bytes 786436
  34.2 4.4 %copy-start.10 = (bf16[128,2,2,2,128]{0,4,3,2,1:T(8,128)(2,1)}, bf16[128,2,2,2,128]{0,4,3,2,1:T(8,128)(2,1)S(1)}, u32[]{:S(2)}) copy-start(bf16[128,2,2,2,128]{0,4,3,2,1:T(8,128)(2,1)S(1)} %rev.25) | copy-start | bytes 786436
  36.3 3.8 copy-start.25
  38.4 5.9 %copy-start.12 = (bf16[128,4,2,1,128]{0,4,2,1,3:T(8,128)(2,1)}, bf16[128,4,2,1,128]{0,4,2,1,3:T(8,128)(2,1)S(1)}, u32[]{:S(2)}) copy-start(bf16[128,4,2,1,128]{0,4,2,1,3:T(8,128)(2,1)S(1)} %rev.24) | copy-start | bytes 786436
  40.2 20.3 %copy-start.17 = (bf16[128,8,128]{2,0,1:T(8,128)(2,1)}, bf16[128,8,128]{2,0,1:T(8,128)(2,1)S(1)}, u32[]{:S(2)}) copy-start(bf16[128,8,128]{2,0,1:T(8,128)(2,1)S(1)} %collective-permute-done.3) | copy-start | bytes 786436
  44.3 16.2 %copy-start.6 = (bf16[128,8,128]{0,2,1:T(8,128)(2,1)}, bf16[128,8,128]{0,2,1:T(8,128)(2,1)S(1)}, u32[]{:S(2)}) copy-start(bf16[128,8,128]{0,2,1:T(8,128)(2,1)S(1)} %fusion.40) | copy-start | bytes 786436
  60.5 6.2 %copy-start.1 = (f32[1024,32,128]{2,1,0:T(8,128)}, f32[1024,32,128]{2,1,0:T(8,128)S(1)}, u32[]{:S(2)}) copy-start(f32[1024,32,128]{2,1,0:T(8,128)S(1)} %broadcast_in_dim.33) | copy-start | bytes 50331652
  66.7 78.7 %copy-start.26 = (s32[128,8]{0,1:T(8,128)S(1)}, s32[128,8]{0,1:T(8,128)}, u32[]{:S(2)}) copy-start(s32[128,8]{0,1:T(8,128)} %param.22) | copy-start | bytes 12292
  66.7 78.9 %copy-start.20 = (f32[128,8]{0,1:T(8,128)S(1)}, f32[128,8]{0,1:T(8,128)}, u32[]{:S(2)}) copy-start(f32[128,8]{0,1:T(8,128)} %param.23) | copy-start | bytes 12292
  66.7 119.1 %copy-start.18 = (f32[4096]{0:T(1024)S(1)}, f32[4096]{0:T(1024)}, u32[]{:S(2)}) copy-start(f32[4096]{0:T(1024)} %param.20) | copy-start | bytes 49156
  81.6 102.1 %all-gather.2.cloned.1.call-start = ((), (), s32[]{:S(2)}) async-start(), calls=%async_computation.2 | async-start | bytes 1114112 | tf_op jit(solution)/shard_map/all_gather | solution.py:115
  145.4 194.4 %all-reduce.2.cloned.1.call-start = ((), (), s32[]{:S(2)}) async-start(), calls=%async_computation.3 | async-start | bytes 4194304 | tf_op jit(solution)/shard_map/psum | solution.py:133
  185.2 0.6 copy-start.23
  235.0 9.6 %copy-start.22 = (s32[7,8]{1,0:T(8,128)S(1)}, s32[7,8]{1,0:T(8,128)}, u32[]{:S(2)}) copy-start(s32[7,8]{1,0:T(8,128)} %param.17) | copy-start | bytes 676
  235.1 104.7 %copy-start.2 = (bf16[128,4096]{1,0:T(8,128)(2,1)S(1)}, bf16[128,4096]{1,0:T(8,128)(2,1)}, u32[]{:S(2)}) copy-start(bf16[128,4096]{1,0:T(8,128)(2,1)} %all-gather.2.cloned.1.call-done) | copy-start | bytes 3145732
  235.1 104.7 %copy-start.24 = (f32[128]{0:T(128)S(1)}, f32[128]{0:T(128)}, u32[]{:S(2)}) copy-start(f32[128]{0:T(128)} %copy-done.23) | copy-start | bytes 1540
  339.8 2.2 copy-start.3
  361.0 7.6 %copy-start.7 = (bf16[128,8,128]{0,2,1:T(8,128)(2,1)S(1)}, bf16[128,8,128]{0,2,1:T(8,128)(2,1)}, u32[]{:S(2)}) copy-start(bf16[128,8,128]{0,2,1:T(8,128)(2,1)} %copy-done.6) | copy-start | bytes 786436
  368.6 12.2 %copy-start.13 = (bf16[128,4,2,1,128]{0,4,2,1,3:T(8,128)(2,1)S(1)}, bf16[128,4,2,1,128]{0,4,2,1,3:T(8,128)(2,1)}, u32[]{:S(2)}) copy-start(bf16[128,4,2,1,128]{0,4,2,1,3:T(8,128)(2,1)} %copy-done.12) | copy-start | bytes 786436
  368.6 12.4 %copy-start.11 = (bf16[128,2,2,2,128]{0,4,3,2,1:T(8,128)(2,1)S(1)}, bf16[128,2,2,2,128]{0,4,3,2,1:T(8,128)(2,1)}, u32[]{:S(2)}) copy-start(bf16[128,2,2,2,128]{0,4,3,2,1:T(8,128)(2,1)} %copy-done.10) | copy-start | bytes 786436
  368.6 12.7 %copy-start.9 = (bf16[128,1,2,4,128]{0,4,3,2,1:T(8,128)(2,1)S(1)}, bf16[128,1,2,4,128]{0,4,3,2,1:T(8,128)(2,1)}, u32[]{:S(2)}) copy-start(bf16[128,1,2,4,128]{0,4,3,2,1:T(8,128)(2,1)} %copy-done.8) | copy-start | bytes 786436
  377.1 14.3 %collective-permute-start.7 = (bf16[128,8,128]{0,2,1:T(8,128)(2,1)}, bf16[128,8,128]{0,2,1:T(8,128)(2,1)}, u32[]{:S(2)}, u32[]{:S(2)}) collective-permute-start(bf16[128,8,128]{0,2,1:T(8,128)(2,1)} %fusion.44), channel_id=1, source_target_pairs={{0,8},{8,0},{1,9},{9,1},{2,10},{10,2},{3,11},{11,3},{4,12},{12,4},... | collective-permute-start | bytes 786440 | tf_op jit(solution)/shard_map/ppermute | solution.py:14
  378.8 12.7 %collective-permute-start.6 = (bf16[128,8,128]{0,2,1:T(8,128)(2,1)}, bf16[128,8,128]{0,2,1:T(8,128)(2,1)}, u32[]{:S(2)}, u32[]{:S(2)}) collective-permute-start(bf16[128,8,128]{0,2,1:T(8,128)(2,1)} %fusion.43), channel_id=1, source_target_pairs={{0,4},{4,0},{1,5},{5,1},{2,6},{6,2},{3,7},{7,3},{8,12},{12,8},{9,1... | collective-permute-start | bytes 786440 | tf_op jit(solution)/shard_map/ppermute | solution.py:14
  380.1 11.4 %collective-permute-start.5 = (bf16[128,8,128]{0,2,1:T(8,128)(2,1)}, bf16[128,8,128]{0,2,1:T(8,128)(2,1)}, u32[]{:S(2)}, u32[]{:S(2)}) collective-permute-start(bf16[128,8,128]{0,2,1:T(8,128)(2,1)} %fusion.42), channel_id=1, source_target_pairs={{0,2},{2,0},{1,3},{3,1},{4,6},{6,4},{5,7},{7,5},{8,10},{10,8},{9,1... | collective-permute-start | bytes 786440 | tf_op jit(solution)/shard_map/ppermute | solution.py:14
  380.8 10.7 %collective-permute-start.4 = (bf16[128,8,128]{0,2,1:T(8,128)(2,1)}, bf16[128,8,128]{0,2,1:T(8,128)(2,1)}, u32[]{:S(2)}, u32[]{:S(2)}) collective-permute-start(bf16[128,8,128]{0,2,1:T(8,128)(2,1)} %fusion.41), channel_id=1, source_target_pairs={{0,1},{1,0},{2,3},{3,2},{4,5},{5,4},{6,7},{7,6},{8,9},{9,8},{10,11... | collective-permute-start | bytes 786440 | tf_op jit(solution)/shard_map/ppermute | solution.py:14
  380.8 6.4 %copy-start.16 = (f32[8,128,128]{2,1,0:T(8,128)S(1)}, f32[8,128,128]{2,1,0:T(8,128)}, u32[]{:S(2)}) copy-start(f32[8,128,128]{2,1,0:T(8,128)} %fusion.66) | copy-start | bytes 1572868
  381.2 6.0 %copy-start.15 = (f32[8,128,128]{2,1,0:T(8,128)S(1)}, f32[8,128,128]{2,1,0:T(8,128)}, u32[]{:S(2)}) copy-start(f32[8,128,128]{2,1,0:T(8,128)} %fusion.68) | copy-start | bytes 1572868
  385.2 2.0 copy-start.19
  387.2 6.0 %copy-start.14 = (f32[128,1024]{0,1:T(8,128)S(1)}, f32[128,1024]{0,1:T(8,128)}, u32[]{:S(2)}) copy-start(f32[128,1024]{0,1:T(8,128)} %get-tuple-element.30) | copy-start | bytes 1572868
  387.3 6.1 %copy-start.5 = (bf16[128,4096]{1,0:T(8,128)(2,1)S(1)}, bf16[128,4096]{1,0:T(8,128)(2,1)}, u32[]{:S(2)}) copy-start(bf16[128,4096]{1,0:T(8,128)(2,1)} %param.12) | copy-start | bytes 3145732
Sparse Core Ops, SparseCore 0:
  81.7 62.0 reduce-scatter.1
  146.7 36.9 all-gather.1
  244.8 94.9 all-reduce.1
where the time goes:
time: 429 us; the launch traced here: 427 us
  waiting for transfers between devices  195 us (45%)
  matrix products  105 us (24%)
  local copies, waits for them, and re-layouts  53 us (12%)
  blocking collectives  31.6 us (7%)
  between operations  16.2 us (4%)
  other arithmetic  15.1 us (4%)
  starting transfers between devices  11 us (3%)
    psum x1, waiting for transfers between devices, on_device(): upstream = lax.psum(local_upstream, 'mp')  94.5 us
    reduce_scatter x1, waiting for transfers between devices, on_device(): lax.psum_scatter(jnp.dot(mixed, down_eff, preferred_element_type=jnp.floa...  62.2 us
    all_gather x1, waiting for transfers between devices, on_device(): stream = lax.all_gather(stream_rows, 'mp', axis=0, tiled=True)  37.6 us
    psum x1, blocking collectives, on_device(): scores = lax.psum(picked_scores, 'mp')  31.6 us
    unnamed x56, local copies, waits for them, and re-layouts  28.8 us
    broadcast_in_dim x2, local copies, waits for them, and re-layouts, scaled_weight(): jnp.repeat(jnp.repeat(factors, block_width, axis=0), block_width, axis=1)  20.7 us
    dot_general x1, matrix products, on_device(): jnp.einsum('td,hd->th', stream_grad, down_eff, preferred_element_type=jnp...  18.4 us
    dot_general x1, matrix products, on_device(): jnp.dot(mixed, down_eff, preferred_element_type=jnp.float32)  14.9 us
  transfers between devices with their start and end apart: 11, of which 4 were waited for; matrix products, arithmetic and copies ran while one was open for 5% of the time, Pallas kernels for 0%

commit v1 on v0

v1 whole, which is shorter than its diff:
```python
import functools

import jax
import jax.numpy as jnp
from jax import lax
from jax.experimental import pallas as pl
from jax.experimental.pallas import tpu as pltpu
from jax.sharding import PartitionSpec as P

F32, BF16 = jnp.float32, jnp.bfloat16
VMEM_LIMIT = 48 << 20
EPS = 1e-05


def bit_groups(bits):
    if bits == 4:
        return [[0], [1], [2, 3]]
    return [[b] for b in range(bits)]


def group_masks(group):
    return [sum(1 << b for i, b in enumerate(group) if j >> i & 1) for j in range(1 << len(group))]


def swap(block, mask):
    if mask == 0:
        return block
    count = lax.axis_size("mp")
    return lax.ppermute(block, "mp", [(i, i ^ mask) for i in range(count)])


def reduce_rows(keep, send, groups):
    received = swap(send, group_masks(groups[0])[1])
    total = (keep.astype(F32) + received.astype(F32)).astype(BF16)
    terms = None
    for n, group in enumerate(groups[1:]):
        masks = group_masks(group)
        rows = total.shape[0] // len(masks)
        terms = [total[:rows]] + [
            swap(total[j * rows : (j + 1) * rows], masks[j]) for j in range(1, len(masks))
        ]
        if n < len(groups) - 2:
            total = sum(t.astype(F32) for t in terms).astype(BF16)
    return terms


def gather_rows(rows, groups):
    for group in reversed(groups):
        masks = group_masks(group)
        rows = jnp.concatenate([rows] + [swap(rows, m) for m in masks[1:]], 0)
    return rows


def row_order(me, tokens, rows, groups, transposed):
    rel = lax.broadcasted_iota(jnp.int32, (tokens, tokens), 1 if transposed else 0)
    whole = lax.broadcasted_iota(jnp.int32, (tokens, tokens), 0 if transposed else 1)
    slot = rel // rows
    mask = jnp.zeros_like(slot)
    place = tokens // rows
    for group in groups:
        place >>= len(group)
        part = slot // place
        for i, b in enumerate(group):
            mask = mask | ((part >> i & 1) << b)
    source = ((me ^ mask) * rows) + rel % rows
    return (source == whole).astype(F32).astype(BF16)


def dot(a, b):
    return jnp.dot(a, b, preferred_element_type=F32)


def dot_nt(a, b):
    return lax.dot_general(a, b, (((1,), (1,)), ((), ())), preferred_element_type=F32)


def dot_tn(a, b):
    return lax.dot_general(a, b, (((0,), (0,)), ((), ())), preferred_element_type=F32)


def spread_factors(scale, width, first, count):
    blocks = scale.shape[1]
    column = lax.broadcasted_iota(jnp.int32, (blocks, count), 1) // width + first
    row = lax.broadcasted_iota(jnp.int32, (blocks, count), 0)
    pick = (column == row).astype(F32).astype(BF16)
    return dot(jnp.exp2(scale.astype(F32)).astype(BF16), pick).astype(BF16)


def params():
    return pltpu.CompilerParams(vmem_limit_bytes=VMEM_LIMIT)


def whole(shape):
    return pl.BlockSpec(shape, lambda i: (0,) * len(shape))


SMEM = pl.BlockSpec(memory_space=pltpu.SMEM)


def cost(flops, nbytes):
    return pl.CostEstimate(flops=int(flops), bytes_accessed=int(nbytes), transcendentals=0)


def up_phase(tokens, values, scale, width):
    token_count, depth = tokens.shape
    hidden = values.shape[1]
    chunk = min(512, depth)
    blocks = chunk // width

    def kernel(tok, val, sc, pre, act, acc):
        i = pl.program_id(0)
        factors = spread_factors(sc[pl.ds(i * blocks, blocks), :], width, 0, hidden)
        weight = jnp.concatenate(
            [val[b * width : (b + 1) * width, :] * factors[b : b + 1, :] for b in range(blocks)], 0
        )
        part = dot(tok[...], weight)

        @pl.when(i == 0)
        def _():
            acc[...] = part

        @pl.when(i > 0)
        def _():
            acc[...] += part

        @pl.when(i == pl.num_programs(0) - 1)
        def _():
            total = acc[...]
            pre[...] = total
            act[...] = (total * jax.nn.sigmoid(total)).astype(BF16)

    return pl.pallas_call(
        kernel,
        grid=(depth // chunk,),
        in_specs=[
            pl.BlockSpec((token_count, chunk), lambda i: (0, i)),
            pl.BlockSpec((chunk, hidden), lambda i: (i, 0)),
            whole(scale.shape),
        ],
        out_specs=[whole((token_count, hidden))] * 2,
        out_shape=[
            jax.ShapeDtypeStruct((token_count, hidden), F32),
            jax.ShapeDtypeStruct((token_count, hidden), BF16),
        ],
        scratch_shapes=[pltpu.VMEM((token_count, hidden), F32)],
        compiler_params=params(),
        cost_estimate=cost(2 * token_count * depth * hidden, depth * hidden * 2),
        name="up_phase",
    )(tokens, values, scale)


def mix_phase(me, pattern, act, received, diag, partner, down, scale, rows, groups):
    token_count, hidden = act.shape
    width = diag.shape[-1]
    levels, blocks = pattern.shape
    features = down.shape[1]
    chunk = min(512, features)
    crossing = len(received)
    local = levels - crossing
    half = token_count // 2

    def kernel(me_ref, pat, act_ref, *refs):
        recv = refs[:crossing]
        diag_ref, part_ref, down_ref, sc, mixed, keep, send = refs[crossing:]
        c = pl.program_id(0)

        @pl.when(c == 0)
        def _():
            order = row_order(me_ref[0], token_count, rows, groups, False)
            for h in range(blocks):
                here = slice(h * width, (h + 1) * width)
                total = dot(act_ref[:, here], diag_ref[h])
                for k in range(levels):
                    if k < local:
                        other = h ^ (1 << k)
                        source = act_ref[:, other * width : (other + 1) * width]
                    else:
                        source = recv[k - local][:, here]
                    keeps = pat[k, h].astype(F32).astype(BF16)
                    total = total + dot(source, part_ref[k, h] * keeps)
                mixed[:, here] = dot(order, total.astype(BF16)).astype(BF16)

        factors = spread_factors(sc[...], width, c * (chunk // width), chunk)
        weight = jnp.concatenate(
            [down_ref[h * width : (h + 1) * width, :] * factors[h : h + 1, :] for h in range(blocks)], 0
        )
        result = dot(mixed[...], weight).astype(BF16)
        keep[...] = result[:half]
        send[...] = result[half:]

    return pl.pallas_call(
        kernel,
        grid=(features // chunk,),
        in_specs=[SMEM, SMEM]
        + [whole((token_count, hidden))] * (1 + crossing)
        + [
            whole(diag.shape),
            whole(partner.shape),
            pl.BlockSpec((hidden, chunk), lambda i: (0, i)),
            whole(scale.shape),
        ],
        out_specs=[whole((token_count, hidden))] + [pl.BlockSpec((half, chunk), lambda i: (0, i))] * 2,
        out_shape=[jax.ShapeDtypeStruct((token_count, hidden), BF16)]
        + [jax.ShapeDtypeStruct((half, features), BF16)] * 2,
        compiler_params=params(),
        cost_estimate=cost(2 * token_count * features * hidden, features * hidden * 2),
        name="mix_phase",
    )(me, pattern, act, *received, diag, partner, down, scale)


def norm_phase(terms, own, gain):
    rows, features = own.shape

    def kernel(*refs):
        n = len(terms)
        own_ref, gain_ref, stream_ref, normed_ref = refs[n:]
        total = refs[0][...].astype(F32)
        for r in refs[1:n]:
            total = total + r[...].astype(F32)
        stream = (own_ref[...].astype(F32) + total).astype(BF16)
        values = stream.astype(F32)
        inverse = lax.rsqrt(jnp.mean(values * values, axis=1, keepdims=True) + EPS)
        stream_ref[...] = stream
        normed_ref[...] = (values * inverse * gain_ref[...]).astype(BF16)

    return pl.pallas_call(
        kernel,
        out_shape=[jax.ShapeDtypeStruct((rows, features), BF16)] * 2,
        compiler_params=params(),
        name="norm_phase",
    )(*terms, own, gain)


def score_phase(me, normed, vocab, ids, rows, groups):
    token_count, features = normed.shape
    entries = vocab.shape[0]
    picks = ids.shape[1]
    chunk = min(256, entries)

    def kernel(me_ref, normed_ref, vocab_ref, ids_ref, out, ordered):
        i = pl.program_id(0)

        @pl.when(i == 0)
        def _():
            order = row_order(me_ref[0], token_count, rows, groups, True)
            ordered[...] = dot(order, normed_ref[...]).astype(BF16)
            out[...] = jnp.zeros_like(out)

        scores = dot_nt(ordered[...], vocab_ref[...])
        offset = ids_ref[...] - (me_ref[0] * entries + i * chunk)
        number = lax.broadcasted_iota(jnp.int32, (token_count, chunk), 1)
        picked = [
            jnp.sum(jnp.where(offset[:, j : j + 1] == number, scores, 0.0), axis=1, keepdims=True)
            for j in range(picks)
        ]
        out[...] += jnp.concatenate(picked, 1)

    return pl.pallas_call(
        kernel,
        grid=(entries // chunk,),
        in_specs=[
            SMEM,
            whole((token_count, features)),
            pl.BlockSpec((chunk, features), lambda i: (i, 0)),
            whole(ids.shape),
        ],
        out_specs=whole((token_count, picks)),
        out_shape=jax.ShapeDtypeStruct((token_count, picks), F32),
        scratch_shapes=[pltpu.VMEM((token_count, features), BF16)],
        compiler_params=params(),
        cost_estimate=cost(2 * token_count * features * entries, features * entries * 2),
        name="score_phase",
    )(me, normed, vocab, ids)


def loss_phase(me, scores, logits, ids, vocab, rows, groups):
    token_count, picks = scores.shape
    entries, features = vocab.shape
    chunk = min(512, features)
    half = token_count // 2

    def kernel(me_ref, scores_ref, logits_ref, ids_ref, vocab_ref, loss, keep, send, spread):
        i = pl.program_id(0)

        @pl.when(i == 0)
        def _():
            values = scores_ref[...]
            log_student = values - jnp.log(jnp.sum(jnp.exp(values), axis=1, keepdims=True))
            weights = jnp.exp(logits_ref[...])
            teacher = weights / jnp.sum(weights, axis=1, keepdims=True)
            each = jnp.sum(teacher * log_student, axis=1, keepdims=True)
            loss[...] = -jnp.sum(each, axis=0, keepdims=True) / token_count
            grad = (jnp.exp(log_student) - teacher).astype(BF16).astype(F32)
            offset = ids_ref[...] - me_ref[0] * entries
            number = lax.broadcasted_iota(jnp.int32, (token_count, entries), 1)
            total = jnp.zeros((token_count, entries), F32)
            for j in range(picks):
                total = jnp.where(offset[:, j : j + 1] == number, grad[:, j : j + 1], total)
            order = row_order(me_ref[0], token_count, rows, groups, False)
            spread[...] = dot(order, total.astype(BF16)).astype(BF16)

        result = dot(spread[...], vocab_ref[...]).astype(BF16)
        keep[...] = result[:half]
        send[...] = result[half:]

    return pl.pallas_call(
        kernel,
        grid=(features // chunk,),
        in_specs=[
            SMEM,
            whole(scores.shape),
            whole(logits.shape),
            whole(ids.shape),
            pl.BlockSpec((entries, chunk), lambda i: (0, i)),
        ],
        out_specs=[whole((1, 1))] + [pl.BlockSpec((half, chunk), lambda i: (0, i))] * 2,
        out_shape=[jax.ShapeDtypeStruct((1, 1), F32)]
        + [jax.ShapeDtypeStruct((half, features), BF16)] * 2,
        scratch_shapes=[pltpu.VMEM((token_count, entries), BF16)],
        compiler_params=params(),
        cost_estimate=cost(2 * token_count * features * entries, features * entries * 2),
        name="loss_phase",
    )(me, scores, logits, ids, vocab)


def norm_back_phase(terms, stream, gain):
    rows, features = stream.shape

    def kernel(*refs):
        n = len(terms)
        stream_ref, gain_ref, out = refs[n:]
        upstream = refs[0][...].astype(F32)
        for r in refs[1:n]:
            upstream = upstream + r[...].astype(F32)
        values = stream_ref[...].astype(F32)
        inverse = lax.rsqrt(jnp.mean(values * values, axis=1, keepdims=True) + EPS)
        unit = values * inverse
        scaled = upstream * gain_ref[...]
        out[...] = (
            inverse * (scaled - unit * jnp.mean(scaled * unit, axis=1, keepdims=True))
        ).astype(BF16)

    return pl.pallas_call(
        kernel,
        out_shape=jax.ShapeDtypeStruct((rows, features), BF16),
        compiler_params=params(),
        name="norm_back_phase",
    )(*terms, stream, gain)


def mixed_grad_phase(me, pattern, grad, down, scale, partner, rows, groups, local):
    token_count, features = grad.shape
    hidden = down.shape[0]
    levels, blocks = pattern.shape
    width = partner.shape[-1]
    crossing = levels - local

    def kernel(me_ref, pat, grad_ref, down_ref, sc, part_ref, mixed_grad, *refs):
        outgoing, factors, order = refs[:crossing], refs[crossing], refs[crossing + 1]
        h = pl.program_id(0)

        @pl.when(h == 0)
        def _():
            factors[...] = spread_factors(sc[...], width, 0, features).astype(F32)
            order[...] = row_order(me_ref[0], token_count, rows, groups, True)

        weight = down_ref[...] * factors[pl.ds(h, 1), :].astype(BF16)
        result = dot_nt(grad_ref[...], weight).astype(BF16)
        result = dot(order[...], result).astype(BF16)
        mixed_grad[...] = result
        for n in range(crossing):
            keeps = pat[local + n, h].astype(F32).astype(BF16)
            outgoing[n][...] = dot_nt(result, part_ref[local + n, 0] * keeps).astype(BF16)

    block = pl.BlockSpec((token_count, width), lambda i: (0, i))
    return pl.pallas_call(
        kernel,
        grid=(blocks,),
        in_specs=[
            SMEM,
            SMEM,
            whole((token_count, features)),
            pl.BlockSpec((width, features), lambda i: (i, 0)),
            whole(scale.shape),
            pl.BlockSpec((levels, 1, width, width), lambda i: (0, i, 0, 0)),
        ],
        out_specs=[block] * (1 + crossing),
        out_shape=[jax.ShapeDtypeStruct((token_count, hidden), BF16)] * (1 + crossing),
        scratch_shapes=[
            pltpu.VMEM((blocks, features), F32),
            pltpu.VMEM((token_count, token_count), BF16),
        ],
        compiler_params=params(),
        cost_estimate=cost(2 * token_count * features * hidden, features * hidden * 2),
        name="mixed_grad_phase",
    )(me, pattern, grad, down, scale, partner)


def block_grad_phase(pattern, act, received, mixed_grad, diag, partner):
    token_count, hidden = act.shape
    levels, blocks = pattern.shape
    width = diag.shape[-1]
    crossing = len(received)
    local = levels - crossing

    def kernel(pat, act_ref, mg, *refs):
        recv = refs[:crossing]
        diag_ref, part_ref, grad_diag, grad_part, act_grad = refs[crossing:]
        h = pl.program_id(0)

        def columns(index):
            return pl.ds(pl.multiple_of(index * width, width), width)

        grad = mg[:, columns(h)]
        grad_diag[0] = dot_tn(act_ref[:, columns(h)], grad)
        total = dot_nt(grad, diag_ref[h])
        for k in range(levels):
            keeps = pat[k, h].astype(F32)
            if k < local:
                other = h ^ (1 << k)
                source = act_ref[:, columns(other)]
                kept = pat[k, other].astype(F32).astype(BF16)
                total = total + dot_nt(mg[:, columns(other)], part_ref[k, other] * kept)
            else:
                source = recv[k - local][:, columns(h)]
            grad_part[k, 0] = dot_tn(source, grad) * keeps
        act_grad[...] = total

    return pl.pallas_call(
        kernel,
        grid=(blocks,),
        in_specs=[SMEM]
        + [whole((token_count, hidden))] * (2 + crossing)
        + [whole(diag.shape), whole(partner.shape)],
        out_specs=[
            pl.BlockSpec((1, width, width), lambda i: (i, 0, 0)),
            pl.BlockSpec((levels, 1, width, width), lambda i: (0, i, 0, 0)),
            pl.BlockSpec((token_count, width), lambda i: (0, i)),
        ],
        out_shape=[
            jax.ShapeDtypeStruct(diag.shape, F32),
            jax.ShapeDtypeStruct(partner.shape, F32),
            jax.ShapeDtypeStruct((token_count, hidden), F32),
        ],
        compiler_params=params(),
        cost_estimate=cost(2 * token_count * hidden * width * 12, 12 << 20),
        name="block_grad_phase",
    )(pattern, act, mixed_grad, *received, diag, partner)


def down_grad_phase(mixed, grad):
    token_count, hidden = mixed.shape
    features = grad.shape[1]
    chunk = min(512, features)

    def kernel(mixed_ref, grad_ref, out, turned):
        @pl.when(pl.program_id(0) == 0)
        def _():
            turned[...] = mixed_ref[...].T

        out[...] = dot(turned[...], grad_ref[...])

    return pl.pallas_call(
        kernel,
        grid=(features // chunk,),
        in_specs=[
            whole((token_count, hidden)),
            pl.BlockSpec((token_count, chunk), lambda i: (0, i)),
        ],
        out_specs=pl.BlockSpec((hidden, chunk), lambda i: (0, i)),
        out_shape=jax.ShapeDtypeStruct((hidden, features), F32),
        scratch_shapes=[pltpu.VMEM((hidden, token_count), BF16)],
        compiler_params=params(),
        cost_estimate=cost(2 * token_count * features * hidden, features * hidden * 4),
        name="down_grad_phase",
    )(mixed, grad)


def up_grad_phase(tokens, pre, act_grad, received):
    token_count, depth = tokens.shape
    hidden = pre.shape[1]
    chunk = min(512, depth)

    def kernel(tok, pre_ref, grad_ref, *refs):
        recv, (out, pre_grad) = refs[: len(received)], refs[len(received) :]

        @pl.when(pl.program_id(0) == 0)
        def _():
            total = grad_ref[...]
            for r in recv:
                total = total + r[...].astype(F32)
            value = pre_ref[...]
            gate = jax.nn.sigmoid(value)
            pre_grad[...] = (total * (gate * (1.0 + value * (1.0 - gate)))).astype(BF16)

        out[...] = dot_tn(tok[...], pre_grad[...])

    return pl.pallas_call(
        kernel,
        grid=(depth // chunk,),
        in_specs=[pl.BlockSpec((token_count, chunk), lambda i: (0, i))]
        + [whole((token_count, hidden))] * (2 + len(received)),
        out_specs=pl.BlockSpec((chunk, hidden), lambda i: (i, 0)),
        out_shape=jax.ShapeDtypeStruct((depth, hidden), F32),
        scratch_shapes=[pltpu.VMEM((token_count, hidden), BF16)],
        compiler_params=params(),
        cost_estimate=cost(2 * token_count * depth * hidden, depth * hidden * 4),
        name="up_grad_phase",
    )(tokens, pre, act_grad, *received)


def on_device(
    tokens,
    up_values,
    up_scale,
    diag_blocks,
    partner_blocks,
    pattern,
    down_values,
    down_scale,
    norm_gain,
    vocab_table,
    teacher_ids,
    teacher_logits,
):
    width = diag_blocks.shape[-1]
    token_count = tokens.shape[0]
    blocks = diag_blocks.shape[0]
    levels = partner_blocks.shape[0]
    local = blocks.bit_length() - 1
    count = lax.axis_size("mp")
    bits = count.bit_length() - 1
    groups = bit_groups(bits)
    rows = token_count // count
    me = lax.axis_index("mp").astype(jnp.int32).reshape(1)
    gain = norm_gain.reshape(1, -1)
    own = lax.dynamic_slice_in_dim(tokens, me[0] * rows, rows, 0)

    pre, act = up_phase(tokens, up_values, up_scale, width)
    received = [swap(act, 1 << k - local) for k in range(local, levels)]
    mixed, keep, send = mix_phase(
        me, pattern, act, received, diag_blocks, partner_blocks, down_values, down_scale, rows, groups
    )
    stream, normed = norm_phase(reduce_rows(keep, send, groups), own, gain)
    normed = gather_rows(normed, groups)
    scores = score_phase(me, normed, vocab_table, teacher_ids, rows, groups)
    for b in range(bits):
        scores = scores + swap(scores, 1 << b)
    loss, keep, send = loss_phase(me, scores, teacher_logits, teacher_ids, vocab_table, rows, groups)
    grad = norm_back_phase(reduce_rows(keep, send, groups), stream, gain)
    grad = gather_rows(grad, groups)
    mixed_grad, *outgoing = mixed_grad_phase(
        me, pattern, grad, down_values, down_scale, partner_blocks, rows, groups, local
    )
    incoming = [swap(block, 1 << n) for n, block in enumerate(outgoing)]
    grad_diag, grad_partner, act_grad = block_grad_phase(
        pattern, act, received, mixed_grad, diag_blocks, partner_blocks
    )
    grad_down = down_grad_phase(mixed, grad)
    grad_up = up_grad_phase(tokens, pre, act_grad, incoming)
    return (loss.reshape(1), grad_up, grad_down, grad_diag, grad_partner)


def solution(mesh):
    return jax.shard_map(
        on_device,
        mesh=mesh,
        in_specs=(
            P("groups", None),
            P(None, "mp"),
            P(None, "mp"),
            P("mp", None, None),
            P(None, "mp", None, None),
            P(None, "mp"),
            P("mp", None),
            P("mp", None),
            P(),
            P("mp", None),
            P("groups", None),
            P("groups", None),
        ),
        out_specs=(
            P("groups"),
            P("groups", "mp"),
            P(("groups", "mp"), None),
            P(("groups", "mp"), None, None),
            P("groups", "mp", None, None),
        ),
        check_vma=False,
    )
```

time: 429 us -> 196 us (0.46)
  waiting for transfers between devices: 195 us -> 70.5 us
  matrix products: 105 us -> 0 us
  Pallas kernels: 0 us -> 74.3 us
  local copies, waits for them, and re-layouts: 53 us -> 10.2 us
  blocking collectives: 31.6 us -> 0 us
  starting transfers between devices: 11 us -> 35.8 us
  between operations: 16.2 us -> 0.98 us
  other arithmetic: 15.1 us -> 2.98 us
    dot_general x31 -> x0, matrix products: 105 us -> none  [the longest x1 18.4 us: on_device(): jnp.einsum('td,hd->th', stream_grad, down_eff, preferred_element_type=jnp...]
    psum x1 -> x0, waiting for transfers between devices: 94.5 us -> none  [on_device(): upstream = lax.psum(local_upstream, 'mp')]
    pallas_call x0 -> x10, Pallas kernels: none -> 74.3 us  [the longest x1 12.7 us: score_phase(): pl.pallas_call(kernel, grid=(entries // chunk,), in_specs=[SMEM, whole((t...]
    ppermute x8 -> x32, waiting for transfers between devices: 0.13 us -> 70.5 us  [swap(): return lax.ppermute(block, 'mp', [(i, i ^ mask) for i in range(count)])]
    reduce_scatter x1 -> x0, waiting for transfers between devices: 62.2 us -> none  [on_device(): lax.psum_scatter(jnp.dot(mixed, down_eff, preferred_element_type=jnp.floa...]
    all_gather x1 -> x0, waiting for transfers between devices: 37.6 us -> none  [on_device(): stream = lax.all_gather(stream_rows, 'mp', axis=0, tiled=True)]
    psum x1 -> x0, blocking collectives: 31.6 us -> none  [on_device(): scores = lax.psum(picked_scores, 'mp')]
    ppermute x8 -> x32, starting transfers between devices: 10.9 us -> 35.8 us  [swap(): return lax.ppermute(block, 'mp', [(i, i ^ mask) for i in range(count)])]
  transfers between devices with their start and end apart: 11 -> 32, of which waited for: 4 -> 23; matrix products, arithmetic and copies ran while one was open for 5% -> 2% of each run, Pallas kernels for 0% -> 7%
where the time goes in v1:
time: 196 us; the launch traced here: 195 us
  Pallas kernels  74.3 us (38%)
  waiting for transfers between devices  70.5 us (36%)
  starting transfers between devices  35.8 us (18%)
  local copies, waits for them, and re-layouts  10.2 us (5%)
  other arithmetic  2.98 us (2%)
    ppermute x32, waiting for transfers between devices, swap(): return lax.ppermute(block, 'mp', [(i, i ^ mask) for i in range(count)])  70.5 us
    ppermute x32, starting transfers between devices, swap(): return lax.ppermute(block, 'mp', [(i, i ^ mask) for i in range(count)])  35.8 us
    pallas_call x1, Pallas kernels, score_phase(): pl.pallas_call(kernel, grid=(entries // chunk,), in_specs=[SMEM, whole((t...  12.7 us
    pallas_call x1, Pallas kernels, loss_phase(): pl.pallas_call(kernel, grid=(features // chunk,), in_specs=[SMEM, whole(s...  11.1 us
    pallas_call x1, Pallas kernels, mix_phase(): pl.pallas_call(kernel, grid=(features // chunk,), in_specs=[SMEM, SMEM] +...  10.2 us
    pallas_call x1, Pallas kernels, mixed_grad_phase(): pl.pallas_call(kernel, grid=(blocks,), in_specs=[SMEM, SMEM, whole((token...  10.1 us
    pallas_call x1, Pallas kernels, up_grad_phase(): pl.pallas_call(kernel, grid=(depth // chunk,), in_specs=[pl.BlockSpec((to...  8.13 us
    pallas_call x1, Pallas kernels, down_grad_phase(): pl.pallas_call(kernel, grid=(features // chunk,), in_specs=[whole((token_...  7.81 us
  transfers between devices with their start and end apart: 32, of which 23 were waited for; matrix products, arithmetic and copies ran while one was open for 2% of the time, Pallas kernels for 7%

profile of v1, /device:TPU:0, one launch (start us, length us, event | category | flops | bytes accessed | tf_op | source)
XLA Modules:
  0.0 194.7 jit_solution(8912093987216574169)
XLA Ops:
  0.6 0.9 copy.17.sc
  1.5 1.2 copy-done.1
  2.8 7.8 %up_phase.1 = (f32[128,1024]{1,0:T(8,128)S(1)}, bf16[128,1024]{1,0:T(8,128)(2,1)S(1)}) custom-call(bf16[128,4096]{1,0:T(8,128)(2,1)S(1)} %copy-done.1, bf16[4096,1024]{1,0:T(8,128)(2,1)} %val.1, s32[32,8]{1,0:T(8,128)S(1)} %copy.17.sc), custom_call_target="tpu_custom_call" | custom-call | flops 1073741824 | bytes 8388608 | tf_op jit(solution)/shard_map/up_phase/pallas_call | solution.py:132
  10.6 0.8 copy-done.4
  11.4 4.0 %collective-permute-start.3 = (bf16[128,1024]{1,0:T(8,128)(2,1)S(1)}, bf16[128,1024]{1,0:T(8,128)(2,1)}, u32[]{:S(2)}, u32[]{:S(2)}) collective-permute-start(bf16[128,1024]{1,0:T(8,128)(2,1)S(1)} %get-tuple-element.23.act_ref), channel_id=1, source_target_pairs={{0,8},{1,9},{2,10},{3,11},{4,12},{5,13},{6,14},{7,15},{8,0},{9,1},... | collective-permute-start | bytes 786440 | tf_op jit(solution)/shard_map/ppermute | solution.py:29
  15.4 1.6 collective-permute-start.2
  17.0 1.5 collective-permute-start.1
  18.5 9.0 %collective-permute-done.3.refs_3_ = bf16[128,1024]{1,0:T(8,128)(2,1)} collective-permute-done((bf16[128,1024]{1,0:T(8,128)(2,1)S(1)}, bf16[128,1024]{1,0:T(8,128)(2,1)}, u32[]{:S(2)}, u32[]{:S(2)}) %collective-permute-start.3) | collective-permute-done | bytes 262176 | tf_op jit(solution)/shard_map/ppermute | solution.py:29
  27.8 10.2 %mix_phase.1 = (bf16[128,1024]{1,0:T(8,128)(2,1)S(1)}, bf16[64,4096]{1,0:T(8,128)(2,1)S(1)}, bf16[64,4096]{1,0:T(8,128)(2,1)S(1)}) custom-call(s32[1]{0:T(128)} %bitcast.me_ref, s32[7,8]{1,0:T(8,128)S(1)} %copy-done.11, bf16[128,1024]{1,0:T(8,128)(2,1)S(1)} %get-tuple-element.23.act_ref, bf16[128,1024]{1,0:T(8,128)(2,1)} %collective-permute-done.refs_0_, ...), custom_call_target="tpu_custom_call" | custom-call | flops 1073741824 | bytes 8388608 | tf_op jit(solution)/shard_map/mix_phase/pallas_call | solution.py:191
  38.1 1.9 collective-permute-done.4
  40.1 0.8 slice.49
  41.0 1.6 collective-permute-start.5
  42.6 7.1 %collective-permute-done.5 = bf16[32,4096]{1,0:T(8,128)(2,1)} collective-permute-done((bf16[32,4096]{1,0:T(8,128)(2,1)}, bf16[32,4096]{1,0:T(8,128)(2,1)}, u32[]{:S(2)}, u32[]{:S(2)}) %collective-permute-start.5) | collective-permute-done | bytes 262176 | tf_op jit(solution)/shard_map/ppermute | solution.py:29
  49.7 1.1 add_convert_fusion.3
  50.8 3.3 %collective-permute-start.8 = (bf16[8,4096]{1,0:T(8,128)(2,1)S(1)}, bf16[8,4096]{1,0:T(8,128)(2,1)S(1)}, u32[]{:S(2)}, u32[]{:S(2)}) collective-permute-start(bf16[8,4096]{1,0:T(8,128)(2,1)S(1)} %get-tuple-element.49), channel_id=1, source_target_pairs={{0,12},{1,13},{2,14},{3,15},{4,8},{5,9},{6,10},{7,11},{8,4},{9,5},... | collective-permute-start | bytes 196616 | tf_op jit(solution)/shard_map/ppermute | solution.py:29
  54.1 1.1 collective-permute-start.6
  55.2 1.8 collective-permute-done.8.refs_3_
  57.0 2.5 %collective-permute-done.7.refs_2_ = bf16[8,4096]{1,0:T(8,128)(2,1)S(1)} collective-permute-done((bf16[8,4096]{1,0:T(8,128)(2,1)S(1)}, bf16[8,4096]{1,0:T(8,128)(2,1)S(1)}, u32[]{:S(2)}, u32[]{:S(2)}) %collective-permute-start.7) | collective-permute-done | bytes 65568 | tf_op jit(solution)/shard_map/ppermute | solution.py:29
  59.9 1.9 collective-permute-start.11
  62.0 2.4 %collective-permute-start.9 = (bf16[8,4096]{1,0:T(8,128)(2,1)S(1)}, bf16[8,4096]{1,0:T(8,128)(2,1)S(1)}, u32[]{:S(2)}, u32[]{:S(2)}) collective-permute-start(bf16[8,4096]{1,0:T(8,128)(2,1)S(1)} %get-tuple-element.26), channel_id=1, source_target_pairs={{0,4},{1,5},{2,6},{3,7},{4,0},{5,1},{6,2},{7,3},{8,12},{9,13},{10,... | collective-permute-start | bytes 196616 | tf_op jit(solution)/shard_map/ppermute | solution.py:29
  64.4 0.7 constant_dynamic-update-slice_fusion.4
  65.1 1.5 collective-permute-done.11
  66.6 1.6 collective-permute-done.10
  68.2 1.6 collective-permute-start.12
  69.8 0.7 constant_dynamic-update-slice_fusion.3
  70.5 0.7 constant_dynamic-update-slice_fusion.2
  71.1 0.7 constant_dynamic-update-slice_fusion.1
  71.8 3.6 %collective-permute-done.12 = bf16[32,4096]{1,0:T(8,128)(2,1)S(1)} collective-permute-done((bf16[32,4096]{1,0:T(8,128)(2,1)S(1)}, bf16[32,4096]{1,0:T(8,128)(2,1)S(1)}, u32[]{:S(2)}, u32[]{:S(2)}) %collective-permute-start.12) | collective-permute-done | bytes 262176 | tf_op jit(solution)/shard_map/ppermute | solution.py:29
  75.4 0.8 constant_dynamic-update-slice_fusion
  76.3 2.1 %collective-permute-done.13 = bf16[64,4096]{1,0:T(8,128)(2,1)} collective-permute-done((bf16[64,4096]{1,0:T(8,128)(2,1)}, bf16[64,4096]{1,0:T(8,128)(2,1)}, u32[]{:S(2)}, u32[]{:S(2)}) %collective-permute-start.13) | collective-permute-done | bytes 524320 | tf_op jit(solution)/shard_map/ppermute | solution.py:29
  78.5 1.9 constant_dynamic-update-slice_fusion.5.normed_ref
  80.3 12.7 %score_phase.1 = f32[128,8]{1,0:T(8,128)S(1)} custom-call(s32[1]{0:T(128)} %bitcast.me_ref, bf16[128,4096]{1,0:T(8,128)(2,1)} %constant_dynamic-update-slice_fusion.5.normed_ref, bf16[2048,4096]{1,0:T(8,128)(2,1)} %vocab_ref.3, s32[128,8]{1,0:T(8,128)S(1)} %copy.18.ids_ref), custom_call_target="tpu_custom_call" | custom-call | flops 2147483648 | bytes 16777216 | tf_op jit(solution)/shard_map/score_phase/pallas_call | solution.py:258
  93.0 0.2 collective-permute-start.14
  93.2 1.1 collective-permute-done.14
  94.3 0.9 collective-permute-start.15
  95.2 3.5 %collective-permute-done.15 = f32[128,8]{1,0:T(8,128)S(1)} collective-permute-done((f32[128,8]{1,0:T(8,128)S(1)}, f32[128,8]{1,0:T(8,128)S(1)}, u32[]{:S(2)}, u32[]{:S(2)}) %collective-permute-start.15) | collective-permute-done | bytes 4128 | tf_op jit(solution)/shard_map/ppermute | solution.py:29
  98.9 4.1 %collective-permute-done.16 = f32[128,8]{1,0:T(8,128)S(1)} collective-permute-done((f32[128,8]{1,0:T(8,128)S(1)}, f32[128,8]{1,0:T(8,128)S(1)}, u32[]{:S(2)}, u32[]{:S(2)}) %collective-permute-start.16) | collective-permute-done | bytes 4128 | tf_op jit(solution)/shard_map/ppermute | solution.py:29
  103.0 0.6 add.32
  103.8 0.8 copy.19.logits_ref
  104.6 4.8 %collective-permute-done.17 = f32[128,8]{1,0:T(8,128)} collective-permute-done((f32[128,8]{1,0:T(8,128)}, f32[128,8]{1,0:T(8,128)}, u32[]{:S(2)}, u32[]{:S(2)}) %collective-permute-start.17) | collective-permute-done | bytes 4128 | tf_op jit(solution)/shard_map/ppermute | solution.py:29
  109.4 0.9 add.33.scores_ref
  110.3 11.1 %loss_phase.1 = (f32[1,1]{1,0:T(1,128)}, bf16[64,4096]{1,0:T(8,128)(2,1)S(1)}, bf16[64,4096]{1,0:T(8,128)(2,1)S(1)}) custom-call(s32[1]{0:T(128)} %bitcast.me_ref, f32[128,8]{1,0:T(8,128)S(1)} %add.33.scores_ref, f32[128,8]{1,0:T(8,128)S(1)} %copy.19.logits_ref, s32[128,8]{1,0:T(8,128)S(1)} %copy.18.ids_ref, bf16[2048,4096]{1,0:T(8,128)(2,1)} %vocab_ref.3), custom_call_target="tpu_custom_call" | custom-call | flops 2147483648 | bytes 16777216 | tf_op jit(solution)/shard_map/loss_phase/pallas_call | solution.py:306
  121.5 1.9 collective-permute-done.18
  123.5 1.3 collective-permute-start.19
  124.8 7.1 %collective-permute-done.19 = bf16[32,4096]{1,0:T(8,128)(2,1)S(1)} collective-permute-done((bf16[32,4096]{1,0:T(8,128)(2,1)S(1)}, bf16[32,4096]{1,0:T(8,128)(2,1)S(1)}, u32[]{:S(2)}, u32[]{:S(2)}) %collective-permute-start.19) | collective-permute-done | bytes 262176 | tf_op jit(solution)/shard_map/ppermute | solution.py:29
  132.0 1.4 collective-permute-start.22
  133.5 3.0 %collective-permute-start.20 = (bf16[8,4096]{1,0:T(8,128)(2,1)S(1)}, bf16[8,4096]{1,0:T(8,128)(2,1)S(1)}, u32[]{:S(2)}, u32[]{:S(2)}) collective-permute-start(bf16[8,4096]{1,0:T(8,128)(2,1)S(1)} %get-tuple-element.45), channel_id=1, source_target_pairs={{0,4},{1,5},{2,6},{3,7},{4,0},{5,1},{6,2},{7,3},{8,12},{9,13},{10,... | collective-permute-start | bytes 196616 | tf_op jit(solution)/shard_map/ppermute | solution.py:29
  136.5 2.2 %collective-permute-done.22.refs_3_ = bf16[8,4096]{1,0:T(8,128)(2,1)S(1)} collective-permute-done((bf16[8,4096]{1,0:T(8,128)(2,1)S(1)}, bf16[8,4096]{1,0:T(8,128)(2,1)S(1)}, u32[]{:S(2)}, u32[]{:S(2)}) %collective-permute-start.22) | collective-permute-done | bytes 65568 | tf_op jit(solution)/shard_map/ppermute | solution.py:29
  138.7 1.3 collective-permute-done.21.refs_2_
  140.0 0.3 norm_back_phase.1
  140.3 1.5 collective-permute-start.25
  141.8 0.8 collective-permute-start.24
  142.6 2.2 %collective-permute-start.23 = (bf16[8,4096]{1,0:T(8,128)(2,1)S(1)}, bf16[8,4096]{1,0:T(8,128)(2,1)S(1)}, u32[]{:S(2)}, u32[]{:S(2)}) collective-permute-start(bf16[8,4096]{1,0:T(8,128)(2,1)S(1)} %norm_back_phase.1), channel_id=1, source_target_pairs={{0,4},{1,5},{2,6},{3,7},{4,0},{5,1},{6,2},{7,3},{8,12},{9,13},{10,... | collective-permute-start | bytes 196616 | tf_op jit(solution)/shard_map/ppermute | solution.py:29
  144.8 2.4 %collective-permute-done.25 = bf16[8,4096]{1,0:T(8,128)(2,1)S(1)} collective-permute-done((bf16[8,4096]{1,0:T(8,128)(2,1)S(1)}, bf16[8,4096]{1,0:T(8,128)(2,1)S(1)}, u32[]{:S(2)}, u32[]{:S(2)}) %collective-permute-start.25) | collective-permute-done | bytes 65568 | tf_op jit(solution)/shard_map/ppermute | solution.py:29
  147.1 1.9 collective-permute-done.24
  149.0 1.3 collective-permute-start.26
  150.4 6.6 %collective-permute-done.26 = bf16[32,4096]{1,0:T(8,128)(2,1)S(1)} collective-permute-done((bf16[32,4096]{1,0:T(8,128)(2,1)S(1)}, bf16[32,4096]{1,0:T(8,128)(2,1)S(1)}, u32[]{:S(2)}, u32[]{:S(2)}) %collective-permute-start.26) | collective-permute-done | bytes 262176 | tf_op jit(solution)/shard_map/ppermute | solution.py:29
  157.1 1.9 collective-permute-done.27
  159.1 10.1 %mixed_grad_phase.1 = (bf16[128,1024]{1,0:T(8,128)(2,1)S(1)}, bf16[128,1024]{1,0:T(8,128)(2,1)S(1)}, bf16[128,1024]{1,0:T(8,128)(2,1)S(1)}, bf16[128,1024]{1,0:T(8,128)(2,1)S(1)}, bf16[128,1024]{1,0:T(8,128)(2,1)S(1)}) custom-call(s32[1]{0:T(128)} %bitcast.me_ref, s32[7,8]{1,0:T(8,128)S(1)} %copy-done.12, ...), custom_call_target="tpu_custom_call" | custom-call | flops 1073741824 | bytes 8388608 | tf_op jit(solution)/shard_map/mixed_grad_phase/pallas_call | solution.py:376
  169.4 1.3 collective-permute-start.29
  170.7 2.1 %collective-permute-start.31 = (bf16[128,1024]{1,0:T(8,128)(2,1)S(1)}, bf16[128,1024]{1,0:T(8,128)(2,1)S(1)}, u32[]{:S(2)}, u32[]{:S(2)}) collective-permute-start(bf16[128,1024]{1,0:T(8,128)(2,1)S(1)} %get-tuple-element.37), channel_id=1, source_target_pairs={{0,8},{1,9},{2,10},{3,11},{4,12},{5,13},{6,14},{7,15},{8,0},{9,1},... | collective-permute-start | bytes 786440 | tf_op jit(solution)/shard_map/ppermute | solution.py:29
  172.7 6.0 %block_grad_phase.1 = (f32[8,128,128]{2,1,0:T(8,128)}, f32[7,8,128,128]{3,2,1,0:T(8,128)}, f32[128,1024]{1,0:T(8,128)S(1)}) custom-call(s32[7,8]{1,0:T(8,128)S(1)} %copy-done.12, bf16[128,1024]{1,0:T(8,128)(2,1)S(1)} %get-tuple-element.23.act_ref, bf16[128,1024]{1,0:T(8,128)(2,1)S(1)} %get-tuple-element.32.mg, ...), custom_call_target="tpu_custom_call" | custom-call | flops 402653184 | bytes 12582912 | tf_op jit(solution)/shard_map/block_grad_phase/pallas_call | solution.py:429
  178.8 7.8 %down_grad_phase.1 = f32[1024,4096]{1,0:T(8,128)} custom-call(bf16[128,1024]{1,0:T(8,128)(2,1)S(1)} %copy-done.7, bf16[128,4096]{1,0:T(8,128)(2,1)S(1)} %constant_dynamic-update-slice_fusion.16.grad_ref), custom_call_target="tpu_custom_call" | custom-call | flops 1073741824 | bytes 16777216 | tf_op jit(solution)/shard_map/down_grad_phase/pallas_call | solution.py:463
  186.6 8.1 %up_grad_phase.1 = f32[4096,1024]{1,0:T(8,128)} custom-call(bf16[128,4096]{1,0:T(8,128)(2,1)S(1)} %copy-done.2, f32[128,1024]{1,0:T(8,128)S(1)} %copy-done.5, f32[128,1024]{1,0:T(8,128)S(1)} %get-tuple-element.33.grad_ref, bf16[128,1024]{1,0:T(8,128)(2,1)S(1)} %collective-permute-done.28.refs_0_, bf16[128,1024]{1,0:T(8,128)(2,1)S(1)} %collective-permute-done.29.refs_1_, ...), custom_call_target="tpu_custom_call" | custom-call | flops 1073741824 | bytes 16777216 | tf_op jit(solution)/shard_map/up_grad_phase/pallas_call | solution.py:498
  (74 shorter events, 2.2 us)
Async XLA Ops:
  0.6 27.1 %copy-start = (bf16[7,8,128,128]{3,2,1,0:T(8,128)(2,1)S(1)}, bf16[7,8,128,128]{3,2,1,0:T(8,128)(2,1)}, u32[]{:S(2)}) copy-start(bf16[7,8,128,128]{3,2,1,0:T(8,128)(2,1)} %refs_5_.3) | copy-start | bytes 5505028
  1.5 1.2 copy-start.1
  2.8 25.0 %copy-start.3 = (bf16[8,128,128]{2,1,0:T(8,128)(2,1)S(1)}, bf16[8,128,128]{2,1,0:T(8,128)(2,1)}, u32[]{:S(2)}) copy-start(bf16[8,128,128]{2,1,0:T(8,128)(2,1)} %refs_4_.3) | copy-start | bytes 786436
  2.8 25.0 %copy-start.11 = (s32[7,8]{1,0:T(8,128)S(1)}, s32[7,8]{1,0:T(8,128)}, u32[]{:S(2)}) copy-start(s32[7,8]{1,0:T(8,128)} %pat.5) | copy-start | bytes 676
  2.8 25.0 %copy-start.13 = (s32[8,32]{1,0:T(8,128)S(1)}, s32[8,32]{1,0:T(8,128)}, u32[]{:S(2)}) copy-start(s32[8,32]{1,0:T(8,128)} %sc.2) | copy-start | bytes 3076
  10.6 0.8 copy-start.4
  11.4 43.9 %copy-start.2 = (bf16[128,4096]{1,0:T(8,128)(2,1)S(1)}, bf16[128,4096]{1,0:T(8,128)(2,1)}, u32[]{:S(2)}) copy-start(bf16[128,4096]{1,0:T(8,128)(2,1)} %tok.3) | copy-start | bytes 3145732
  11.4 48.4 %copy-start.10 = (f32[4096]{0:T(1024)S(1)}, f32[4096]{0:T(1024)}, u32[]{:S(2)}) copy-start(f32[4096]{0:T(1024)} %param.20) | copy-start | bytes 49156
  11.4 16.2 %collective-permute-start.3 = (bf16[128,1024]{1,0:T(8,128)(2,1)S(1)}, bf16[128,1024]{1,0:T(8,128)(2,1)}, u32[]{:S(2)}, u32[]{:S(2)}) collective-permute-start(bf16[128,1024]{1,0:T(8,128)(2,1)S(1)} %get-tuple-element.23.act_ref), channel_id=1, source_target_pairs={{0,8},{1,9},{2,10},{3,11},{4,12},{5,13},{6,14},{7,15},{8,0},{9,1},... | collective-permute-start | bytes 786440 | tf_op jit(solution)/shard_map/ppermute | solution.py:29
  15.4 12.3 %collective-permute-start.2 = (bf16[128,1024]{1,0:T(8,128)(2,1)S(1)}, bf16[128,1024]{1,0:T(8,128)(2,1)}, u32[]{:S(2)}, u32[]{:S(2)}) collective-permute-start(bf16[128,1024]{1,0:T(8,128)(2,1)S(1)} %get-tuple-element.23.act_ref), channel_id=1, source_target_pairs={{0,4},{1,5},{2,6},{3,7},{4,0},{5,1},{6,2},{7,3},{8,12},{9,13},{10,... | collective-permute-start | bytes 786440 | tf_op jit(solution)/shard_map/ppermute | solution.py:29
  17.0 10.8 %collective-permute-start.1 = (bf16[128,1024]{1,0:T(8,128)(2,1)S(1)}, bf16[128,1024]{1,0:T(8,128)(2,1)}, u32[]{:S(2)}, u32[]{:S(2)}) collective-permute-start(bf16[128,1024]{1,0:T(8,128)(2,1)S(1)} %get-tuple-element.23.act_ref), channel_id=1, source_target_pairs={{0,2},{1,3},{2,0},{3,1},{4,6},{5,7},{6,4},{7,5},{8,10},{9,11},{10,... | collective-permute-start | bytes 786440 | tf_op jit(solution)/shard_map/ppermute | solution.py:29
  18.5 9.2 %collective-permute-start = (bf16[128,1024]{1,0:T(8,128)(2,1)S(1)}, bf16[128,1024]{1,0:T(8,128)(2,1)}, u32[]{:S(2)}, u32[]{:S(2)}) collective-permute-start(bf16[128,1024]{1,0:T(8,128)(2,1)S(1)} %get-tuple-element.23.act_ref), channel_id=1, source_target_pairs={{0,1},{1,0},{2,3},{3,2},{4,5},{5,4},{6,7},{7,6},{8,9},{9,8},{10,11... | collective-permute-start | bytes 786440 | tf_op jit(solution)/shard_map/ppermute | solution.py:29
  27.8 48.4 %copy-start.16 = (s32[128,8]{0,1:T(8,128)S(1)}, s32[128,8]{0,1:T(8,128)}, u32[]{:S(2)}) copy-start(s32[128,8]{0,1:T(8,128)} %param.22) | copy-start | bytes 12292
  38.0 2.1 %copy-start.6 = (bf16[128,1024]{1,0:T(8,128)(2,1)}, bf16[128,1024]{1,0:T(8,128)(2,1)S(1)}, u32[]{:S(2)}) copy-start(bf16[128,1024]{1,0:T(8,128)(2,1)S(1)} %get-tuple-element.38.mixed_ref) | copy-start | bytes 786436
  38.0 2.0 %collective-permute-start.4 = (bf16[64,4096]{1,0:T(8,128)(2,1)S(1)}, bf16[64,4096]{1,0:T(8,128)(2,1)S(1)}, u32[]{:S(2)}, u32[]{:S(2)}) collective-permute-start(bf16[64,4096]{1,0:T(8,128)(2,1)S(1)} %get-tuple-element.25), channel_id=1, source_target_pairs={{0,1},{1,0},{2,3},{3,2},{4,5},{5,4},{6,7},{7,6},{8,9},{9,8},{10,11... | collective-permute-start | bytes 1572872 | tf_op jit(solution)/shard_map/ppermute | solution.py:29
  40.1 0.9 copy-start.15
  41.0 8.7 %collective-permute-start.5 = (bf16[32,4096]{1,0:T(8,128)(2,1)}, bf16[32,4096]{1,0:T(8,128)(2,1)}, u32[]{:S(2)}, u32[]{:S(2)}) collective-permute-start(bf16[32,4096]{1,0:T(8,128)(2,1)} %slice.49), channel_id=1, source_target_pairs={{0,2},{1,3},{2,0},{3,1},{4,6},{5,7},{6,4},{7,5},{8,10},{9,11},{10,... | collective-permute-start | bytes 786440 | tf_op jit(solution)/shard_map/ppermute | solution.py:29
  50.8 6.2 %collective-permute-start.8 = (bf16[8,4096]{1,0:T(8,128)(2,1)S(1)}, bf16[8,4096]{1,0:T(8,128)(2,1)S(1)}, u32[]{:S(2)}, u32[]{:S(2)}) collective-permute-start(bf16[8,4096]{1,0:T(8,128)(2,1)S(1)} %get-tuple-element.49), channel_id=1, source_target_pairs={{0,12},{1,13},{2,14},{3,15},{4,8},{5,9},{6,10},{7,11},{8,4},{9,5},... | collective-permute-start | bytes 196616 | tf_op jit(solution)/shard_map/ppermute | solution.py:29
  54.1 5.5 %collective-permute-start.7 = (bf16[8,4096]{1,0:T(8,128)(2,1)S(1)}, bf16[8,4096]{1,0:T(8,128)(2,1)S(1)}, u32[]{:S(2)}, u32[]{:S(2)}) collective-permute-start(bf16[8,4096]{1,0:T(8,128)(2,1)S(1)} %get-tuple-element.50), channel_id=1, source_target_pairs={{0,8},{1,9},{2,10},{3,11},{4,12},{5,13},{6,14},{7,15},{8,0},{9,1},... | collective-permute-start | bytes 196616 | tf_op jit(solution)/shard_map/ppermute | solution.py:29
  54.1 5.7 %collective-permute-start.6 = (bf16[8,4096]{1,0:T(8,128)(2,1)S(1)}, bf16[8,4096]{1,0:T(8,128)(2,1)S(1)}, u32[]{:S(2)}, u32[]{:S(2)}) collective-permute-start(bf16[8,4096]{1,0:T(8,128)(2,1)S(1)} %get-tuple-element.51), channel_id=1, source_target_pairs={{0,4},{1,5},{2,6},{3,7},{4,0},{5,1},{6,2},{7,3},{8,12},{9,13},{10,... | collective-permute-start | bytes 196616 | tf_op jit(solution)/shard_map/ppermute | solution.py:29
  59.9 16.3 %copy-start.8 = (bf16[8,4096]{1,0:T(8,128)(2,1)}, bf16[8,4096]{1,0:T(8,128)(2,1)S(1)}, u32[]{:S(2)}) copy-start(bf16[8,4096]{1,0:T(8,128)(2,1)S(1)} %get-tuple-element.31.refs_4_) | copy-start | bytes 196612
  59.9 6.6 %collective-permute-start.11 = (bf16[8,4096]{1,0:T(8,128)(2,1)S(1)}, bf16[8,4096]{1,0:T(8,128)(2,1)S(1)}, u32[]{:S(2)}, u32[]{:S(2)}) collective-permute-start(bf16[8,4096]{1,0:T(8,128)(2,1)S(1)} %get-tuple-element.26), channel_id=1, source_target_pairs={{0,12},{1,13},{2,14},{3,15},{4,8},{5,9},{6,10},{7,11},{8,4},{9,5},... | collective-permute-start | bytes 196616 | tf_op jit(solution)/shard_map/ppermute | solution.py:29
  61.8 6.3 %collective-permute-start.10 = (bf16[8,4096]{1,0:T(8,128)(2,1)S(1)}, bf16[8,4096]{1,0:T(8,128)(2,1)S(1)}, u32[]{:S(2)}, u32[]{:S(2)}) collective-permute-start(bf16[8,4096]{1,0:T(8,128)(2,1)S(1)} %get-tuple-element.26), channel_id=1, source_target_pairs={{0,8},{1,9},{2,10},{3,11},{4,12},{5,13},{6,14},{7,15},{8,0},{9,1},... | collective-permute-start | bytes 196616 | tf_op jit(solution)/shard_map/ppermute | solution.py:29
  62.0 6.2 %collective-permute-start.9 = (bf16[8,4096]{1,0:T(8,128)(2,1)S(1)}, bf16[8,4096]{1,0:T(8,128)(2,1)S(1)}, u32[]{:S(2)}, u32[]{:S(2)}) collective-permute-start(bf16[8,4096]{1,0:T(8,128)(2,1)S(1)} %get-tuple-element.26), channel_id=1, source_target_pairs={{0,4},{1,5},{2,6},{3,7},{4,0},{5,1},{6,2},{7,3},{8,12},{9,13},{10,... | collective-permute-start | bytes 196616 | tf_op jit(solution)/shard_map/ppermute | solution.py:29
  68.2 7.2 %collective-permute-start.12 = (bf16[32,4096]{1,0:T(8,128)(2,1)S(1)}, bf16[32,4096]{1,0:T(8,128)(2,1)S(1)}, u32[]{:S(2)}, u32[]{:S(2)}) collective-permute-start(bf16[32,4096]{1,0:T(8,128)(2,1)S(1)} %pad_maximum_fusion), channel_id=1, source_target_pairs={{0,2},{1,3},{2,0},{3,1},{4,6},{5,7},{6,4},{7,5},{8,10},{9,11},{10,... | collective-permute-start | bytes 786440 | tf_op jit(solution)/shard_map/ppermute | solution.py:29
  76.2 2.3 %collective-permute-start.13 = (bf16[64,4096]{1,0:T(8,128)(2,1)}, bf16[64,4096]{1,0:T(8,128)(2,1)}, u32[]{:S(2)}, u32[]{:S(2)}) collective-permute-start(bf16[64,4096]{1,0:T(8,128)(2,1)} %get-tuple-element.47), channel_id=1, source_target_pairs={{0,1},{1,0},{2,3},{3,2},{4,5},{5,4},{6,7},{7,6},{8,9},{9,8},{10,11... | collective-permute-start | bytes 1572872 | tf_op jit(solution)/shard_map/ppermute | solution.py:29
  93.0 1.3 collective-permute-start.14
  94.3 4.3 %collective-permute-start.15 = (f32[128,8]{1,0:T(8,128)S(1)}, f32[128,8]{1,0:T(8,128)S(1)}, u32[]{:S(2)}, u32[]{:S(2)}) collective-permute-start(f32[128,8]{1,0:T(8,128)S(1)} %add.30), channel_id=1, source_target_pairs={{0,2},{1,3},{2,0},{3,1},{4,6},{5,7},{6,4},{7,5},{8,10},{9,11},{10,... | collective-permute-start | bytes 12296 | tf_op jit(solution)/shard_map/ppermute | solution.py:29
  98.7 4.3 %collective-permute-start.16 = (f32[128,8]{1,0:T(8,128)S(1)}, f32[128,8]{1,0:T(8,128)S(1)}, u32[]{:S(2)}, u32[]{:S(2)}) collective-permute-start(f32[128,8]{1,0:T(8,128)S(1)} %add.31), channel_id=1, source_target_pairs={{0,4},{1,5},{2,6},{3,7},{4,0},{5,1},{6,2},{7,3},{8,12},{9,13},{10,... | collective-permute-start | bytes 12296 | tf_op jit(solution)/shard_map/ppermute | solution.py:29
  103.7 5.7 %collective-permute-start.17 = (f32[128,8]{1,0:T(8,128)}, f32[128,8]{1,0:T(8,128)}, u32[]{:S(2)}, u32[]{:S(2)}) collective-permute-start(f32[128,8]{1,0:T(8,128)} %add.32), channel_id=1, source_target_pairs={{0,8},{1,9},{2,10},{3,11},{4,12},{5,13},{6,14},{7,15},{8,0},{9,1},... | collective-permute-start | bytes 12296 | tf_op jit(solution)/shard_map/ppermute | solution.py:29
  110.3 29.7 %copy-start.9 = (bf16[8,4096]{1,0:T(8,128)(2,1)S(1)}, bf16[8,4096]{1,0:T(8,128)(2,1)}, u32[]{:S(2)}) copy-start(bf16[8,4096]{1,0:T(8,128)(2,1)} %copy-done.8) | copy-start | bytes 196612
  110.3 48.8 %copy-start.12 = (s32[7,8]{1,0:T(8,128)S(1)}, s32[7,8]{1,0:T(8,128)}, u32[]{:S(2)}) copy-start(s32[7,8]{1,0:T(8,128)} %pat.5) | copy-start | bytes 676
  110.3 48.8 %copy-start.14 = (s32[8,32]{1,0:T(8,128)S(1)}, s32[8,32]{1,0:T(8,128)}, u32[]{:S(2)}) copy-start(s32[8,32]{1,0:T(8,128)} %sc.2) | copy-start | bytes 3076
  121.5 1.9 collective-permute-start.18
  123.5 8.4 %collective-permute-start.19 = (bf16[32,4096]{1,0:T(8,128)(2,1)S(1)}, bf16[32,4096]{1,0:T(8,128)(2,1)S(1)}, u32[]{:S(2)}, u32[]{:S(2)}) collective-permute-start(bf16[32,4096]{1,0:T(8,128)(2,1)S(1)} %slice.55), channel_id=1, source_target_pairs={{0,2},{1,3},{2,0},{3,1},{4,6},{5,7},{6,4},{7,5},{8,10},{9,11},{10,... | collective-permute-start | bytes 786440 | tf_op jit(solution)/shard_map/ppermute | solution.py:29
  132.0 6.6 %collective-permute-start.22 = (bf16[8,4096]{1,0:T(8,128)(2,1)S(1)}, bf16[8,4096]{1,0:T(8,128)(2,1)S(1)}, u32[]{:S(2)}, u32[]{:S(2)}) collective-permute-start(bf16[8,4096]{1,0:T(8,128)(2,1)S(1)} %get-tuple-element.43), channel_id=1, source_target_pairs={{0,12},{1,13},{2,14},{3,15},{4,8},{5,9},{6,10},{7,11},{8,4},{9,5},... | collective-permute-start | bytes 196616 | tf_op jit(solution)/shard_map/ppermute | solution.py:29
  133.4 6.6 %collective-permute-start.21 = (bf16[8,4096]{1,0:T(8,128)(2,1)S(1)}, bf16[8,4096]{1,0:T(8,128)(2,1)S(1)}, u32[]{:S(2)}, u32[]{:S(2)}) collective-permute-start(bf16[8,4096]{1,0:T(8,128)(2,1)S(1)} %get-tuple-element.44), channel_id=1, source_target_pairs={{0,8},{1,9},{2,10},{3,11},{4,12},{5,13},{6,14},{7,15},{8,0},{9,1},... | collective-permute-start | bytes 196616 | tf_op jit(solution)/shard_map/ppermute | solution.py:29
  133.5 6.6 %collective-permute-start.20 = (bf16[8,4096]{1,0:T(8,128)(2,1)S(1)}, bf16[8,4096]{1,0:T(8,128)(2,1)S(1)}, u32[]{:S(2)}, u32[]{:S(2)}) collective-permute-start(bf16[8,4096]{1,0:T(8,128)(2,1)S(1)} %get-tuple-element.45), channel_id=1, source_target_pairs={{0,4},{1,5},{2,6},{3,7},{4,0},{5,1},{6,2},{7,3},{8,12},{9,13},{10,... | collective-permute-start | bytes 196616 | tf_op jit(solution)/shard_map/ppermute | solution.py:29
  140.3 6.9 %collective-permute-start.25 = (bf16[8,4096]{1,0:T(8,128)(2,1)S(1)}, bf16[8,4096]{1,0:T(8,128)(2,1)S(1)}, u32[]{:S(2)}, u32[]{:S(2)}) collective-permute-start(bf16[8,4096]{1,0:T(8,128)(2,1)S(1)} %norm_back_phase.1), channel_id=1, source_target_pairs={{0,12},{1,13},{2,14},{3,15},{4,8},{5,9},{6,10},{7,11},{8,4},{9,5},... | collective-permute-start | bytes 196616 | tf_op jit(solution)/shard_map/ppermute | solution.py:29
  141.8 7.2 %collective-permute-start.24 = (bf16[8,4096]{1,0:T(8,128)(2,1)S(1)}, bf16[8,4096]{1,0:T(8,128)(2,1)S(1)}, u32[]{:S(2)}, u32[]{:S(2)}) collective-permute-start(bf16[8,4096]{1,0:T(8,128)(2,1)S(1)} %norm_back_phase.1), channel_id=1, source_target_pairs={{0,8},{1,9},{2,10},{3,11},{4,12},{5,13},{6,14},{7,15},{8,0},{9,1},... | collective-permute-start | bytes 196616 | tf_op jit(solution)/shard_map/ppermute | solution.py:29
  142.6 6.5 %collective-permute-start.23 = (bf16[8,4096]{1,0:T(8,128)(2,1)S(1)}, bf16[8,4096]{1,0:T(8,128)(2,1)S(1)}, u32[]{:S(2)}, u32[]{:S(2)}) collective-permute-start(bf16[8,4096]{1,0:T(8,128)(2,1)S(1)} %norm_back_phase.1), channel_id=1, source_target_pairs={{0,4},{1,5},{2,6},{3,7},{4,0},{5,1},{6,2},{7,3},{8,12},{9,13},{10,... | collective-permute-start | bytes 196616 | tf_op jit(solution)/shard_map/ppermute | solution.py:29
  149.0 8.0 %collective-permute-start.26 = (bf16[32,4096]{1,0:T(8,128)(2,1)S(1)}, bf16[32,4096]{1,0:T(8,128)(2,1)S(1)}, u32[]{:S(2)}, u32[]{:S(2)}) collective-permute-start(bf16[32,4096]{1,0:T(8,128)(2,1)S(1)} %pad_maximum_fusion.1), channel_id=1, source_target_pairs={{0,2},{1,3},{2,0},{3,1},{4,6},{5,7},{6,4},{7,5},{8,10},{9,11},{10,... | collective-permute-start | bytes 786440 | tf_op jit(solution)/shard_map/ppermute | solution.py:29
  157.0 21.8 %copy-start.7 = (bf16[128,1024]{1,0:T(8,128)(2,1)S(1)}, bf16[128,1024]{1,0:T(8,128)(2,1)}, u32[]{:S(2)}) copy-start(bf16[128,1024]{1,0:T(8,128)(2,1)} %copy-done.6) | copy-start | bytes 786436
  157.1 2.0 %collective-permute-start.27 = (bf16[64,4096]{1,0:T(8,128)(2,1)S(1)}, bf16[64,4096]{1,0:T(8,128)(2,1)S(1)}, u32[]{:S(2)}, u32[]{:S(2)}) collective-permute-start(bf16[64,4096]{1,0:T(8,128)(2,1)S(1)} %get-tuple-element.41), channel_id=1, source_target_pairs={{0,1},{1,0},{2,3},{3,2},{4,5},{5,4},{6,7},{7,6},{8,9},{9,8},{10,11... | collective-permute-start | bytes 1572872 | tf_op jit(solution)/shard_map/ppermute | solution.py:29
  169.2 17.4 %collective-permute-start.28 = (bf16[128,1024]{1,0:T(8,128)(2,1)S(1)}, bf16[128,1024]{1,0:T(8,128)(2,1)S(1)}, u32[]{:S(2)}, u32[]{:S(2)}) collective-permute-start(bf16[128,1024]{1,0:T(8,128)(2,1)S(1)} %get-tuple-element.34), channel_id=1, source_target_pairs={{0,1},{1,0},{2,3},{3,2},{4,5},{5,4},{6,7},{7,6},{8,9},{9,8},{10,11... | collective-permute-start | bytes 786440 | tf_op jit(solution)/shard_map/ppermute | solution.py:29
  169.4 17.2 %collective-permute-start.29 = (bf16[128,1024]{1,0:T(8,128)(2,1)S(1)}, bf16[128,1024]{1,0:T(8,128)(2,1)S(1)}, u32[]{:S(2)}, u32[]{:S(2)}) collective-permute-start(bf16[128,1024]{1,0:T(8,128)(2,1)S(1)} %get-tuple-element.35), channel_id=1, source_target_pairs={{0,2},{1,3},{2,0},{3,1},{4,6},{5,7},{6,4},{7,5},{8,10},{9,11},{10,... | collective-permute-start | bytes 786440 | tf_op jit(solution)/shard_map/ppermute | solution.py:29
  170.7 15.9 %collective-permute-start.30 = (bf16[128,1024]{1,0:T(8,128)(2,1)S(1)}, bf16[128,1024]{1,0:T(8,128)(2,1)S(1)}, u32[]{:S(2)}, u32[]{:S(2)}) collective-permute-start(bf16[128,1024]{1,0:T(8,128)(2,1)S(1)} %get-tuple-element.36), channel_id=1, source_target_pairs={{0,4},{1,5},{2,6},{3,7},{4,0},{5,1},{6,2},{7,3},{8,12},{9,13},{10,... | collective-permute-start | bytes 786440 | tf_op jit(solution)/shard_map/ppermute | solution.py:29
  170.7 15.9 %collective-permute-start.31 = (bf16[128,1024]{1,0:T(8,128)(2,1)S(1)}, bf16[128,1024]{1,0:T(8,128)(2,1)S(1)}, u32[]{:S(2)}, u32[]{:S(2)}) collective-permute-start(bf16[128,1024]{1,0:T(8,128)(2,1)S(1)} %get-tuple-element.37), channel_id=1, source_target_pairs={{0,8},{1,9},{2,10},{3,11},{4,12},{5,13},{6,14},{7,15},{8,0},{9,1},... | collective-permute-start | bytes 786440 | tf_op jit(solution)/shard_map/ppermute | solution.py:29
  178.8 7.8 %copy-start.5 = (f32[128,1024]{1,0:T(8,128)S(1)}, f32[128,1024]{1,0:T(8,128)}, u32[]{:S(2)}) copy-start(f32[128,1024]{1,0:T(8,128)} %copy-done.4) | copy-start | bytes 1572868

commit v2 on v1

v2 whole, which is shorter than its diff:
```python
import functools

import jax
import jax.numpy as jnp
from jax import lax
from jax.experimental import pallas as pl
from jax.experimental.pallas import tpu as pltpu
from jax.sharding import PartitionSpec as P

F32, BF16 = jnp.float32, jnp.bfloat16
EPS = 1e-05
LANES = 128
SHARED = 2
SLOTS = 32
HELD = 128


def bit_groups(bits):
    if bits == 4:
        return [[0], [1], [2, 3]]
    return [[b] for b in range(bits)]


def group_masks(group):
    return [sum(1 << b for i, b in enumerate(group) if j >> i & 1) for j in range(1 << len(group))]


def swap(block, mask):
    if mask == 0:
        return block
    count = lax.axis_size("mp")
    return lax.ppermute(block, "mp", [(i, i ^ mask) for i in range(count)])


def reduce_rows(keep, send, groups, after=None):
    for n, group in enumerate(groups):
        masks = group_masks(group)
        if n == len(groups) - 1:
            return [keep] + [swap(s, m) for s, m in zip(send, masks[1:])]
        total = swap(send if n == 0 else send[0], masks[1])
        parts = 1 << len(groups[n + 1])
        keep, *send = add_phase(keep, total, parts, after[n] if after else [])


def gather_rows(rows, groups):
    for group in reversed(groups):
        masks = group_masks(group)
        rows = jnp.concatenate([rows] + [swap(rows, m) for m in masks[1:]], 0)
    return rows


def row_order(me, tokens, rows, groups, transposed):
    rel = lax.broadcasted_iota(jnp.int32, (tokens, tokens), 1 if transposed else 0)
    whole = lax.broadcasted_iota(jnp.int32, (tokens, tokens), 0 if transposed else 1)
    slot = rel // rows
    mask = jnp.zeros_like(slot)
    place = tokens // rows
    for group in groups:
        place >>= len(group)
        part = slot // place
        for i, b in enumerate(group):
            mask = mask | ((part >> i & 1) << b)
    source = ((me ^ mask) * rows) + rel % rows
    return (source == whole).astype(F32).astype(BF16)


def dot(a, b):
    return jnp.dot(a, b, preferred_element_type=F32)


def dot_nt(a, b):
    return lax.dot_general(a, b, (((1,), (1,)), ((), ())), preferred_element_type=F32)


def dot_tn(a, b):
    return lax.dot_general(a, b, (((0,), (0,)), ((), ())), preferred_element_type=F32)


def spread_factors(scale, width, first, count):
    blocks = scale.shape[1]
    column = lax.broadcasted_iota(jnp.int32, (blocks, count), 1) // width + first
    row = lax.broadcasted_iota(jnp.int32, (blocks, count), 0)
    pick = (column == row).astype(F32).astype(BF16)
    return dot(jnp.exp2(scale.astype(F32)).astype(BF16), pick).astype(BF16)


def params(mebibytes=16):
    return pltpu.CompilerParams(vmem_limit_bytes=mebibytes << 20)


def whole(shape):
    return pl.BlockSpec(shape, lambda i: (0,) * len(shape))


SMEM = pl.BlockSpec(memory_space=pltpu.SMEM)
UNREAD = pl.BlockSpec(memory_space=pl.ANY)
VMEM = pl.BlockSpec(memory_space=pltpu.VMEM)
HBM = pl.BlockSpec(memory_space=pltpu.HBM)


def columns(index, width):
    return pl.ds(pl.multiple_of(index * width, width), width)


def cost(flops, nbytes):
    return pl.CostEstimate(flops=int(flops), bytes_accessed=int(nbytes), transcendentals=0)


def up_phase(tokens, values, scale, width, after):
    token_count, depth = tokens.shape
    hidden = values.shape[1]
    chunk = min(512, depth)
    blocks = chunk // width
    steps = depth // chunk

    def kernel(tok, val, sc, *refs):
        pre, act, factors, table, arrived = refs[len(after) :]

        def fetch(i):
            return pltpu.make_async_copy(val.at[columns(i, chunk), :], table.at[i], arrived.at[i])

        for i in range(steps):
            fetch(i).start()
        factors[...] = spread_factors(sc[...], width, 0, hidden).astype(F32)

        def step(i, carry):
            fetch(i).wait()
            weight = jnp.concatenate(
                [
                    table[i, b * width : (b + 1) * width, :]
                    * factors[pl.ds(i * blocks + b, 1), :].astype(BF16)
                    for b in range(blocks)
                ],
                0,
            )
            part = dot(tok[:, columns(i, chunk)], weight)
            pre[...] = jnp.where(i == 0, part, pre[...] + part)
            return carry

        lax.fori_loop(0, steps, step, 0)
        total = pre[...]
        act[...] = (total * jax.nn.sigmoid(total)).astype(BF16)

    return pl.pallas_call(
        kernel,
        in_specs=[VMEM, HBM, VMEM] + [UNREAD] * len(after),
        out_specs=[VMEM] * 2,
        out_shape=[
            jax.ShapeDtypeStruct((token_count, hidden), F32),
            jax.ShapeDtypeStruct((token_count, hidden), BF16),
        ],
        scratch_shapes=[
            pltpu.VMEM((depth // width, hidden), F32),
            pltpu.VMEM((steps, chunk, hidden), BF16),
            pltpu.SemaphoreType.DMA((steps,)),
        ],
        compiler_params=params(52),
        cost_estimate=cost(2 * token_count * depth * hidden, depth * hidden * 2),
        name="up_phase",
    )(tokens, values, scale, *after)


def own_mix_phase(pattern, act, diag, partner, local, after):
    token_count, hidden = act.shape
    width = diag.shape[-1]
    levels, blocks = pattern.shape

    def kernel(pat, act_ref, diag_ref, part_ref, *refs):
        out = refs[-1]

        def mix(h):
            source = [act_ref[:, columns(h, width)]]
            weight = [diag_ref[h]]
            for k in range(local):
                source.append(act_ref[:, columns(h ^ (1 << k), width)])
                weight.append(part_ref[k, h] * pat[k, h].astype(F32).astype(BF16))
            out[:, columns(h, width)] = dot(
                jnp.concatenate(source, 1), jnp.concatenate(weight, 0)
            )

        for h in range(blocks):
            mix(h)

    return pl.pallas_call(
        kernel,
        in_specs=[SMEM] + [VMEM] * 3 + [UNREAD] * len(after),
        out_specs=VMEM,
        out_shape=jax.ShapeDtypeStruct((token_count, hidden), F32),
        compiler_params=params(),
        cost_estimate=cost(2 * token_count * hidden * width * 4, 4 << 20),
        name="own_mix_phase",
    )(pattern, act, diag, partner, *after)


def mix_phase(me, pattern, own, received, partner, down, scale, rows, groups, after):
    token_count, hidden = own.shape
    width = partner.shape[-1]
    levels, blocks = pattern.shape
    features = down.shape[1]
    chunk = min(512, features)
    steps = features // chunk
    crossing = len(received)
    local = levels - crossing
    half = token_count // 2

    def kernel(me_ref, pat, own_ref, *refs):
        recv = refs[:crossing]
        part_ref, down_ref, sc = refs[crossing : crossing + 3]
        mixed, keep, send, factors, table, arrived = refs[-6:]

        def fetch(c):
            return pltpu.make_async_copy(
                down_ref.at[:, columns(c, chunk)], table.at[c], arrived.at[c]
            )

        for c in range(steps):
            fetch(c).start()
        factors[...] = spread_factors(sc[...], width, 0, features).astype(F32)
        order = row_order(me_ref[0], token_count, rows, groups, False)

        def mix(h):
            here = columns(h, width)
            source = jnp.concatenate([r[:, here] for r in recv], 1)
            weight = jnp.concatenate(
                [
                    part_ref[k, h] * pat[k, h].astype(F32).astype(BF16)
                    for k in range(local, levels)
                ],
                0,
            )
            total = own_ref[:, here] + dot(source, weight)
            mixed[:, here] = dot(order, total.astype(BF16)).astype(BF16)

        for h in range(blocks):
            mix(h)

        def project(c, carry):
            fetch(c).wait()
            weight = jnp.concatenate(
                [
                    table[c, h * width : (h + 1) * width, :]
                    * factors[h : h + 1, columns(c, chunk)].astype(BF16)
                    for h in range(blocks)
                ],
                0,
            )
            result = dot(mixed[...], weight).astype(BF16)
            keep[:, columns(c, chunk)] = result[:half]
            send[:, columns(c, chunk)] = result[half:]
            return carry

        lax.fori_loop(0, steps, project, 0, unroll=2)

    return pl.pallas_call(
        kernel,
        in_specs=[SMEM, SMEM] + [VMEM] * (2 + crossing) + [HBM, VMEM] + [UNREAD] * len(after),
        out_specs=[VMEM] * 3,
        out_shape=[jax.ShapeDtypeStruct((token_count, hidden), BF16)]
        + [jax.ShapeDtypeStruct((half, features), BF16)] * 2,
        scratch_shapes=[
            pltpu.VMEM((blocks, features), F32),
            pltpu.VMEM((steps, hidden, chunk), BF16),
            pltpu.SemaphoreType.DMA((steps,)),
        ],
        compiler_params=params(52),
        cost_estimate=cost(2 * token_count * features * hidden, features * hidden * 2),
        name="mix_phase",
    )(me, pattern, own, *received, partner, down, scale, *after)


def add_phase(keep, received, parts, after):
    rows, features = keep.shape
    rows //= parts

    def kernel(a, b, *refs):
        outs = refs[len(after) :]
        for n, out in enumerate(outs):
            here = slice(n * rows, (n + 1) * rows)
            out[...] = (a[here, :].astype(F32) + b[here, :].astype(F32)).astype(BF16)

    return pl.pallas_call(
        kernel,
        in_specs=[VMEM] * 2 + [UNREAD] * len(after),
        out_specs=[VMEM] * parts,
        out_shape=[jax.ShapeDtypeStruct((rows, features), BF16)] * parts,
        compiler_params=params(),
        name="add_phase",
    )(keep, received, *after)


def norm_phase(terms, own, gain):
    rows, features = own.shape

    def kernel(*refs):
        n = len(terms)
        own_ref, gain_ref, stream_ref, normed_ref = refs[n:]
        total = refs[0][...].astype(F32)
        for r in refs[1:n]:
            total = total + r[...].astype(F32)
        stream = (own_ref[...].astype(F32) + total).astype(BF16)
        values = stream.astype(F32)
        inverse = lax.rsqrt(jnp.mean(values * values, axis=1, keepdims=True) + EPS)
        stream_ref[...] = stream
        normed_ref[...] = (values * inverse * gain_ref[...]).astype(BF16)

    return pl.pallas_call(
        kernel,
        out_shape=[jax.ShapeDtypeStruct((rows, features), BF16)] * 2,
        compiler_params=params(),
        name="norm_phase",
    )(*terms, own, gain)


def score_phase(me, normed, vocab, ids, rows, groups):
    token_count, features = normed.shape
    entries = vocab.shape[0]
    picks = ids.shape[1]
    chunk = min(256, entries)

    def kernel(me_ref, normed_ref, vocab_ref, ids_ref, out, ordered):
        i = pl.program_id(0)

        @pl.when(i == 0)
        def _():
            order = row_order(me_ref[0], token_count, rows, groups, True)
            ordered[...] = dot(order, normed_ref[...]).astype(BF16)
            out[...] = jnp.zeros_like(out)

        scores = dot_nt(ordered[...], vocab_ref[...])
        offset = ids_ref[...] - (me_ref[0] * entries + i * chunk)
        number = lax.broadcasted_iota(jnp.int32, (token_count, chunk), 1)
        picked = [
            jnp.sum(jnp.where(offset[:, j : j + 1] == number, scores, 0.0), axis=1, keepdims=True)
            for j in range(picks)
        ]
        out[...] += jnp.concatenate(picked, 1)

    return pl.pallas_call(
        kernel,
        grid=(entries // chunk,),
        in_specs=[
            SMEM,
            whole((token_count, features)),
            pl.BlockSpec((chunk, features), lambda i: (i, 0)),
            whole(ids.shape),
        ],
        out_specs=whole((token_count, picks)),
        out_shape=jax.ShapeDtypeStruct((token_count, picks), F32),
        scratch_shapes=[pltpu.VMEM((token_count, features), BF16)],
        compiler_params=params(24),
        cost_estimate=cost(2 * token_count * features * entries, features * entries * 2),
        name="score_phase",
    )(me, normed, vocab, ids)


def loss_phase(me, scores, logits, ids, vocab, rows, groups):
    token_count, picks = scores.shape
    entries, features = vocab.shape
    chunk = min(512, features)
    half = token_count // 2

    def kernel(me_ref, scores_ref, logits_ref, ids_ref, vocab_ref, loss, keep, send, spread):
        i = pl.program_id(0)

        @pl.when(i == 0)
        def _():
            values = scores_ref[...]
            log_student = values - jnp.log(jnp.sum(jnp.exp(values), axis=1, keepdims=True))
            weights = jnp.exp(logits_ref[...])
            teacher = weights / jnp.sum(weights, axis=1, keepdims=True)
            each = jnp.sum(teacher * log_student, axis=1, keepdims=True)
            loss[...] = -jnp.sum(each, axis=0, keepdims=True) / token_count
            grad = (jnp.exp(log_student) - teacher).astype(BF16).astype(F32)
            offset = ids_ref[...] - me_ref[0] * entries
            number = lax.broadcasted_iota(jnp.int32, (token_count, entries), 1)
            total = jnp.zeros((token_count, entries), F32)
            for j in range(picks):
                total = jnp.where(offset[:, j : j + 1] == number, grad[:, j : j + 1], total)
            order = row_order(me_ref[0], token_count, rows, groups, False)
            spread[...] = dot(order, total.astype(BF16)).astype(BF16)

        result = dot(spread[...], vocab_ref[...]).astype(BF16)
        keep[...] = result[:half]
        send[...] = result[half:]

    return pl.pallas_call(
        kernel,
        grid=(features // chunk,),
        in_specs=[
            SMEM,
            whole(scores.shape),
            whole(logits.shape),
            whole(ids.shape),
            pl.BlockSpec((entries, chunk), lambda i: (0, i)),
        ],
        out_specs=[whole((1, 1))] + [pl.BlockSpec((half, chunk), lambda i: (0, i))] * 2,
        out_shape=[jax.ShapeDtypeStruct((1, 1), F32)]
        + [jax.ShapeDtypeStruct((half, features), BF16)] * 2,
        scratch_shapes=[pltpu.VMEM((token_count, entries), BF16)],
        compiler_params=params(24),
        cost_estimate=cost(2 * token_count * features * entries, features * entries * 2),
        name="loss_phase",
    )(me, scores, logits, ids, vocab)


def split_loss(loss):
    lane = lax.broadcasted_iota(jnp.int32, (loss.shape[0], LANES), 1)
    high = loss.astype(BF16).astype(F32)
    middle = (loss - high).astype(BF16).astype(F32)
    low = loss - high - middle
    return jnp.where(lane == 0, high, jnp.where(lane == 1, middle, jnp.where(lane == 2, low, 0.0)))


def norm_back_phase(terms, stream, gain, loss):
    rows, features = stream.shape

    def kernel(*refs):
        n = len(terms)
        stream_ref, gain_ref, loss_ref, out = refs[n:]
        upstream = refs[0][...].astype(F32)
        for r in refs[1:n]:
            upstream = upstream + r[...].astype(F32)
        values = stream_ref[...].astype(F32)
        inverse = lax.rsqrt(jnp.mean(values * values, axis=1, keepdims=True) + EPS)
        unit = values * inverse
        scaled = upstream * gain_ref[...]
        out[:, :features] = (
            inverse * (scaled - unit * jnp.mean(scaled * unit, axis=1, keepdims=True))
        ).astype(BF16)
        out[:, features:] = split_loss(jnp.broadcast_to(loss_ref[...], (rows, 1))).astype(BF16)

    return pl.pallas_call(
        kernel,
        out_shape=jax.ShapeDtypeStruct((rows, features + LANES), BF16),
        compiler_params=params(),
        name="norm_back_phase",
    )(*terms, stream, gain, loss)


def slot_of(index, count, groups):
    slot = jnp.zeros_like(index)
    place = count
    for group in groups:
        place >>= len(group)
        for i, b in enumerate(group):
            slot = slot | ((index >> b & 1) << i) * place
    return slot


def pick_phase(me, ids, vocab, rows, groups):
    token_count, picks = ids.shape
    entries, features = vocab.shape
    count = token_count // rows
    sharers = count >> SHARED
    chunk = min(512, features)
    half = count * SLOTS // 2
    wide = picks * sharers

    def ones(mask):
        return mask.astype(F32).astype(BF16)

    def iota(shape, axis):
        return lax.broadcasted_iota(jnp.int32, shape, axis)

    def kernel(me_ref, ids_ref, vocab_ref, rank_ref, flag_ref, keep, send, chosen, layout, table, arrived):
        def fetch(c):
            return pltpu.make_async_copy(
                vocab_ref.at[:, columns(c, chunk)], table.at[c], arrived.at[c]
            )

        for c in range(features // chunk):
            fetch(c).start()

        mine = me_ref[0]
        wanted = ids_ref[...]
        shard = wanted // entries
        lane = iota((token_count, wide), 1)
        sharer = jnp.full((token_count, wide), -1, jnp.int32)
        for j in range(picks):
            sharer = jnp.where(lane // sharers == j, shard[:, j : j + 1] >> SHARED, sharer)
        asks = (sharer == lane % sharers).astype(F32)
        row, column = iota((token_count, token_count), 0), iota((token_count, token_count), 1)
        together = row // rows == column // rows
        earlier = dot(ones(together & (column < row)), asks.astype(BF16))
        total = dot(ones(together), asks.astype(BF16)).astype(BF16)
        a, b = iota((wide, wide), 0), iota((wide, wide), 1)
        before = dot(total, ones((a % sharers == b % sharers) & (a // sharers < b // sharers)))
        gathered = (asks * (earlier + before)).astype(BF16)
        rank = dot(gathered, ones(iota((wide, picks), 0) // sharers == iota((wide, picks), 1)))
        rank_ref[...] = rank.astype(jnp.int32)

        held = jnp.zeros((token_count, count), F32)
        for j in range(picks):
            held = held + (shard[:, j : j + 1] == iota((token_count, count), 1)).astype(F32)
        held = jnp.sum(held, axis=0, keepdims=True)
        over = (jnp.max(rank, keepdims=True) >= SLOTS) | (jnp.max(held, keepdims=True) > HELD)
        flag_ref[...] = jnp.broadcast_to(over.astype(F32), flag_ref.shape)

        here = (shard == mine).astype(F32)
        local = here.astype(BF16)
        place = dot(ones(column < row), local) + dot(
            dot(jnp.ones((token_count, token_count), BF16), local).astype(BF16),
            ones(iota((picks, picks), 0) < iota((picks, picks), 1)),
        )
        place = jnp.where(here > 0, place, -1.0).astype(jnp.int32)
        index = wanted - mine * entries + 1
        owner = iota((token_count, picks), 0) // rows
        target = slot_of(owner ^ mine, count, groups) * SLOTS + rank.astype(jnp.int32) + 1
        source_high = jnp.zeros((HELD, 1), F32)
        source_low = jnp.zeros((HELD, 1), F32)
        target_high = jnp.zeros((1, HELD), F32)
        target_low = jnp.zeros((1, HELD), F32)
        for j in range(picks):
            at = ones(place[:, j : j + 1] == iota((token_count, HELD), 1))
            one = slice(j, j + 1)

            def part(value):
                return value[:, one].astype(F32).astype(BF16)

            source_high += dot_tn(at, part(index >> 7))
            source_low += dot_tn(at, part(index & 127))
            target_high += dot_tn(part(target >> 7), at)
            target_low += dot_tn(part(target & 127), at)
        source = (source_high * 128 + source_low).astype(jnp.int32) - 1
        aim = (target_high * 128 + target_low).astype(jnp.int32) - 1
        chosen[...] = ones(source == iota((HELD, entries), 1))
        layout[...] = ones(iota((2 * half, HELD), 0) == aim)

        def lay(c, carry):
            fetch(c).wait()
            found = dot(chosen[...], table[c]).astype(BF16)
            laid = dot(layout[...], found).astype(BF16)
            keep[:, columns(c, chunk)] = laid[:half]
            send[:, columns(c, chunk)] = laid[half:]
            return carry

        lax.fori_loop(0, features // chunk, lay, 0)

    return pl.pallas_call(
        kernel,
        in_specs=[SMEM, VMEM, pl.BlockSpec(memory_space=pltpu.HBM)],
        out_specs=[VMEM] * 4,
        out_shape=[
            jax.ShapeDtypeStruct(ids.shape, jnp.int32),
            jax.ShapeDtypeStruct((8, LANES), F32),
        ]
        + [jax.ShapeDtypeStruct((half, features), BF16)] * 2,
        scratch_shapes=[
            pltpu.VMEM((HELD, entries), BF16),
            pltpu.VMEM((2 * half, HELD), BF16),
            pltpu.VMEM((features // chunk, entries, chunk), BF16),
            pltpu.SemaphoreType.DMA((features // chunk,)),
        ],
        compiler_params=params(32),
        cost_estimate=cost(4 * token_count * features * entries, features * entries * 2),
        name="pick_phase",
    )(me, ids, vocab)


def token_phase(me, terms, own, gain, picked, ids, rank, logits, entries):
    rows, features = own.shape
    picks = ids.shape[1]
    span = len(picked) * SLOTS

    def kernel(me_ref, *refs):
        n, p = len(terms), len(picked)
        sources = refs[n : n + p]
        own_ref, gain_ref, ids_ref, rank_ref, logits_ref, out, table, arrived = refs[n + p :]
        mine = pl.ds(pl.multiple_of(me_ref[0] * rows, rows), rows)
        copies = [
            pltpu.make_async_copy(source, table.at[m], arrived.at[m])
            for m, source in enumerate(sources)
        ]
        for copy in copies:
            copy.start()
        total = refs[0][...].astype(F32)
        for r in refs[1:n]:
            total = total + r[...].astype(F32)
        values = (own_ref[...].astype(F32) + total).astype(BF16).astype(F32)
        inverse = lax.rsqrt(jnp.mean(values * values, axis=1, keepdims=True) + EPS)
        unit = values * inverse
        normed = (unit * gain_ref[...]).astype(BF16)
        for copy in copies:
            copy.wait()
        dense = jnp.concatenate([dot_nt(normed, table[m]) for m in range(p)], 1)
        piece = (ids_ref[mine, :] // entries >> SHARED) ^ (me_ref[0] >> SHARED)
        place = piece * SLOTS + rank_ref[mine, :]
        number = lax.broadcasted_iota(jnp.int32, (rows, span), 1)
        hits = [place[:, j : j + 1] == number for j in range(picks)]
        scores = jnp.concatenate(
            [jnp.sum(jnp.where(hit, dense, 0.0), axis=1, keepdims=True) for hit in hits], 1
        )
        log_student = scores - jnp.log(jnp.sum(jnp.exp(scores), axis=1, keepdims=True))
        weights = jnp.exp(logits_ref[mine, :])
        teacher = weights / jnp.sum(weights, axis=1, keepdims=True)
        loss = -jnp.sum(teacher * log_student, axis=1, keepdims=True)
        grad = (jnp.exp(log_student) - teacher).astype(BF16).astype(F32)
        spread = jnp.zeros((rows, span), F32)
        for j in range(picks):
            spread = jnp.where(hits[j], grad[:, j : j + 1], spread)
        spread = spread.astype(BF16)
        upstream = dot(spread[:, :SLOTS], table[0])
        for m in range(1, p):
            upstream = upstream + dot(spread[:, m * SLOTS : (m + 1) * SLOTS], table[m])
        scaled = upstream * gain_ref[...]
        out[:, :features] = (
            inverse * (scaled - unit * jnp.mean(scaled * unit, axis=1, keepdims=True))
        ).astype(BF16)
        out[:, features:] = split_loss(loss).astype(BF16)

    return pl.pallas_call(
        kernel,
        in_specs=[SMEM] + [VMEM] * len(terms) + [UNREAD] * len(picked) + [VMEM] * 5,
        scratch_shapes=[
            pltpu.VMEM((len(picked), SLOTS, features), BF16),
            pltpu.SemaphoreType.DMA((len(picked),)),
        ],
        out_shape=jax.ShapeDtypeStruct((rows, features + LANES), BF16),
        compiler_params=params(),
        name="token_phase",
    )(me, *terms, *picked, own, gain, ids, rank, logits)


def mixed_grad_phase(me, pattern, grad, down, scale, partner, rows, groups, local):
    token_count = grad.shape[0]
    hidden, features = down.shape
    levels, blocks = pattern.shape
    width = partner.shape[-1]
    crossing = levels - local
    pair = 2 if blocks % 2 == 0 else 1

    def kernel(me_ref, pat, grad_ref, down_ref, sc, part_ref, loss, mixed_grad, *refs):
        outgoing, (factors, result, table, arrived) = refs[:crossing], refs[crossing:]

        def fetch(i):
            return pltpu.make_async_copy(
                down_ref.at[columns(i, pair * width), :], table.at[i], arrived.at[i]
            )

        for i in range(blocks // pair):
            fetch(i).start()
        factors[...] = spread_factors(sc[...], width, 0, features).astype(F32)
        order = row_order(me_ref[0], token_count, rows, groups, True)
        each = jnp.sum(grad_ref[:, features:].astype(F32), axis=1, keepdims=True)
        loss[...] = jnp.sum(each, axis=0, keepdims=True) / token_count

        def step(i, carry):
            fetch(i).wait()
            weight = jnp.concatenate(
                [
                    table[i, b * width : (b + 1) * width, :]
                    * factors[pl.ds(i * pair + b, 1), :].astype(BF16)
                    for b in range(pair)
                ],
                0,
            )
            result[:, columns(i, pair * width)] = dot_nt(grad_ref[:, :features], weight).astype(BF16)
            return carry

        lax.fori_loop(0, blocks // pair, step, 0, unroll=2)
        mixed_grad[...] = dot(order, result[...]).astype(BF16)
        for h in range(blocks):
            here = slice(h * width, (h + 1) * width)
            weights = jnp.concatenate(
                [part_ref[k, h] * pat[k, h].astype(F32).astype(BF16) for k in range(local, levels)], 0
            )
            terms = dot_nt(mixed_grad[:, here], weights).astype(BF16)
            for n in range(crossing):
                outgoing[n][:, here] = terms[:, n * width : (n + 1) * width]

    return pl.pallas_call(
        kernel,
        in_specs=[SMEM, SMEM, VMEM, HBM, VMEM, VMEM],
        out_specs=[VMEM] * (2 + crossing),
        out_shape=[jax.ShapeDtypeStruct((1, 1), F32)]
        + [jax.ShapeDtypeStruct((token_count, hidden), BF16)] * (1 + crossing),
        scratch_shapes=[
            pltpu.VMEM((blocks, features), F32),
            pltpu.VMEM((token_count, hidden), BF16),
            pltpu.VMEM((blocks // pair, pair * width, features), BF16),
            pltpu.SemaphoreType.DMA((blocks // pair,)),
        ],
        compiler_params=params(52),
        cost_estimate=cost(2 * token_count * features * hidden, features * hidden * 2),
        name="mixed_grad_phase",
    )(me, pattern, grad, down, scale, partner)


def block_grad_phase(pattern, act, received, mixed_grad, diag, partner):
    token_count, hidden = act.shape
    levels, blocks = pattern.shape
    width = diag.shape[-1]
    crossing = len(received)
    local = levels - crossing

    def kernel(pat, act_ref, mg, *refs):
        recv = refs[:crossing]
        diag_ref, part_ref, grad_diag, grad_part, act_grad = refs[crossing:]
        h = pl.program_id(0)

        grad = mg[:, columns(h, width)]
        grad_diag[0] = dot_tn(act_ref[:, columns(h, width)], grad)
        total = dot_nt(grad, diag_ref[h])
        for k in range(levels):
            keeps = pat[k, h].astype(F32)
            if k < local:
                other = h ^ (1 << k)
                source = act_ref[:, columns(other, width)]
                kept = pat[k, other].astype(F32).astype(BF16)
                total = total + dot_nt(mg[:, columns(other, width)], part_ref[k, other] * kept)
            else:
                source = recv[k - local][:, columns(h, width)]
            grad_part[k, 0] = dot_tn(source, grad) * keeps
        act_grad[...] = total

    return pl.pallas_call(
        kernel,
        grid=(blocks,),
        in_specs=[SMEM]
        + [whole((token_count, hidden))] * (2 + crossing)
        + [whole(diag.shape), whole(partner.shape)],
        out_specs=[
            pl.BlockSpec((1, width, width), lambda i: (i, 0, 0)),
            pl.BlockSpec((levels, 1, width, width), lambda i: (0, i, 0, 0)),
            pl.BlockSpec((token_count, width), lambda i: (0, i)),
        ],
        out_shape=[
            jax.ShapeDtypeStruct(diag.shape, F32),
            jax.ShapeDtypeStruct(partner.shape, F32),
            jax.ShapeDtypeStruct((token_count, hidden), F32),
        ],
        compiler_params=params(),
        cost_estimate=cost(2 * token_count * hidden * width * 12, 12 << 20),
        name="block_grad_phase",
    )(pattern, act, mixed_grad, *received, diag, partner)


def down_grad_phase(mixed, grad, features):
    token_count, hidden = mixed.shape
    chunk = min(512, features)
    steps = features // chunk

    def kernel(mixed_ref, grad_ref, out, turned, table, left):
        def store(c):
            return pltpu.make_async_copy(table.at[c], out.at[:, columns(c, chunk)], left.at[c])

        turned[...] = mixed_ref[...].T

        def step(c, carry):
            table[c] = dot(turned[...], grad_ref[:, columns(c, chunk)])
            store(c).start()
            return carry

        lax.fori_loop(0, steps, step, 0)
        for c in range(steps):
            store(c).wait()

    return pl.pallas_call(
        kernel,
        in_specs=[VMEM] * 2,
        out_specs=HBM,
        out_shape=jax.ShapeDtypeStruct((hidden, features), F32),
        scratch_shapes=[
            pltpu.VMEM((hidden, token_count), BF16),
            pltpu.VMEM((steps, hidden, chunk), F32),
            pltpu.SemaphoreType.DMA((steps,)),
        ],
        compiler_params=params(28),
        cost_estimate=cost(2 * token_count * features * hidden, features * hidden * 4),
        name="down_grad_phase",
    )(mixed, grad)


def up_grad_phase(tokens, pre, act_grad, received):
    token_count, depth = tokens.shape
    hidden = pre.shape[1]
    chunk = min(512, depth)
    steps = depth // chunk

    def kernel(tok, pre_ref, grad_ref, *refs):
        recv, (out, pre_grad, table, left) = refs[: len(received)], refs[len(received) :]

        def store(i):
            return pltpu.make_async_copy(table.at[i], out.at[columns(i, chunk), :], left.at[i])

        total = grad_ref[...]
        for r in recv:
            total = total + r[...].astype(F32)
        value = pre_ref[...]
        gate = jax.nn.sigmoid(value)
        pre_grad[...] = (total * (gate * (1.0 + value * (1.0 - gate)))).astype(BF16)

        def step(i, carry):
            table[i] = dot_tn(tok[:, columns(i, chunk)], pre_grad[...])
            store(i).start()
            return carry

        lax.fori_loop(0, steps, step, 0)
        for i in range(steps):
            store(i).wait()

    return pl.pallas_call(
        kernel,
        in_specs=[VMEM] * (3 + len(received)),
        out_specs=HBM,
        out_shape=jax.ShapeDtypeStruct((depth, hidden), F32),
        scratch_shapes=[
            pltpu.VMEM((token_count, hidden), BF16),
            pltpu.VMEM((steps, chunk, hidden), F32),
            pltpu.SemaphoreType.DMA((steps,)),
        ],
        compiler_params=params(28),
        cost_estimate=cost(2 * token_count * depth * hidden, depth * hidden * 4),
        name="up_grad_phase",
    )(tokens, pre, act_grad, *received)


def on_device(
    tokens,
    up_values,
    up_scale,
    diag_blocks,
    partner_blocks,
    pattern,
    down_values,
    down_scale,
    norm_gain,
    vocab_table,
    teacher_ids,
    teacher_logits,
):
    width = diag_blocks.shape[-1]
    token_count = tokens.shape[0]
    blocks = diag_blocks.shape[0]
    levels = partner_blocks.shape[0]
    local = blocks.bit_length() - 1
    count = lax.axis_size("mp")
    bits = count.bit_length() - 1
    groups = bit_groups(bits)
    rows = token_count // count
    me = lax.axis_index("mp").astype(jnp.int32).reshape(1)
    gain = norm_gain.reshape(1, -1)
    own = lax.dynamic_slice_in_dim(tokens, me[0] * rows, rows, 0)

    sparse = groups[:SHARED] == [[b] for b in range(SHARED)] and len(groups) == SHARED + 1
    if sparse:
        rank, flag, kept, sent = pick_phase(me, teacher_ids, vocab_table, rows, groups)
        pre, act = up_phase(tokens, up_values, up_scale, width, [flag])
        received = [swap(act, 1 << k - local) for k in range(local, levels)]
        own_mix = own_mix_phase(pattern, act, diag_blocks, partner_blocks, local, ())
        kept, sent = add_phase(kept, swap(sent, group_masks(groups[0])[1]), 2, [own_mix, *received[1:2]])
        parts = lax.axis_size("groups")
        turned = flag
        for _ in range(parts - 1):
            turned = lax.ppermute(turned, "groups", [(i, (i + 1) % parts) for i in range(parts)])
            flag = flag + turned
        crowded = flag[0, 0] > 0
        laid = swap(sent, group_masks(groups[1])[1])
    else:
        pre, act = up_phase(tokens, up_values, up_scale, width, [])
        received = [swap(act, 1 << k - local) for k in range(local, levels)]
        own_mix = own_mix_phase(pattern, act, diag_blocks, partner_blocks, local, ())
    mixed, keep, send = mix_phase(
        me, pattern, own_mix, received, partner_blocks, down_values, down_scale, rows, groups, []
    )
    if sparse:
        masks = group_masks(groups[SHARED])
        pieces = add_phase(kept, laid, len(masks), [])
        picked = [swap(piece, m) for piece, m in zip(pieces, masks)]
        terms = reduce_rows(keep, send, groups, [pieces[1:], picked[1:]])
    else:
        terms = reduce_rows(keep, send, groups)

    def dense_tokens(*terms):
        stream, normed = norm_phase(terms, own, gain)
        normed = gather_rows(normed, groups)
        scores = score_phase(me, normed, vocab_table, teacher_ids, rows, groups)
        for b in range(bits):
            scores = scores + swap(scores, 1 << b)
        loss, keep, send = loss_phase(
            me, scores, teacher_logits, teacher_ids, vocab_table, rows, groups
        )
        return norm_back_phase(reduce_rows(keep, send, groups), stream, gain, loss)

    if sparse:
        grad = token_phase(
            me, terms, own, gain, picked, teacher_ids, rank, teacher_logits, vocab_table.shape[0]
        )
        grad = lax.cond(crowded, lambda grad, *terms: dense_tokens(*terms), lambda grad, *terms: grad, grad, *terms)
    else:
        grad = dense_tokens(*terms)
    grad = gather_rows(grad, groups)
    loss, mixed_grad, *outgoing = mixed_grad_phase(
        me, pattern, grad, down_values, down_scale, partner_blocks, rows, groups, local
    )
    incoming = [swap(block, 1 << n) for n, block in enumerate(outgoing)]
    grad_diag, grad_partner, act_grad = block_grad_phase(
        pattern, act, received, mixed_grad, diag_blocks, partner_blocks
    )
    grad_down = down_grad_phase(mixed, grad, down_values.shape[1])
    grad_up = up_grad_phase(tokens, pre, act_grad, incoming)
    return (loss.reshape(1), grad_up, grad_down, grad_diag, grad_partner)


def solution(mesh):
    return jax.shard_map(
        on_device,
        mesh=mesh,
        in_specs=(
            P("groups", None),
            P(None, "mp"),
            P(None, "mp"),
            P("mp", None, None),
            P(None, "mp", None, None),
            P(None, "mp"),
            P("mp", None),
            P("mp", None),
            P(),
            P("mp", None),
            P("groups", None),
            P("groups", None),
        ),
        out_specs=(
            P("groups"),
            P("groups", "mp"),
            P(("groups", "mp"), None),
            P(("groups", "mp"), None, None),
            P("groups", "mp", None, None),
        ),
        check_vma=False,
    )
```

time: 196 us -> 149 us (0.76)
  waiting for transfers between devices: 70.5 us -> 48.4 us
  Pallas kernels: 74.3 us -> 58 us
  starting transfers between devices: 35.8 us -> 30.7 us
  other arithmetic: 2.98 us -> 0.7 us
    ppermute x32 -> x23, waiting for transfers between devices: 70.5 us -> 48.4 us  [swap(): return lax.ppermute(block, 'mp', [(i, i ^ mask) for i in range(count)])]
    pallas_call x9 -> x12, Pallas kernels: 68.3 us -> 52.5 us  [the longest x1 9.63 us: mixed_grad_phase(): pl.pallas_call(kernel, in_specs=[SMEM, SMEM, VMEM, HBM, VMEM, VMEM], out_...]
    ppermute x32 -> x23, starting transfers between devices: 35.8 us -> 29.2 us  [swap(): return lax.ppermute(block, 'mp', [(i, i ^ mask) for i in range(count)])]
    concatenate x4 -> x2, local copies, waits for them, and re-layouts: 2.76 us -> 0.09 us  [gather_rows(): rows = jnp.concatenate([rows] + [swap(rows, m) for m in masks[1:]], 0)]
    unnamed x45 -> x59, local copies, waits for them, and re-layouts: 6.64 us -> 7.4 us
  transfers between devices with their start and end apart: 32 -> 24, of which waited for: 23 -> 14; matrix products, arithmetic and copies ran while one was open for 2% -> 2% of each run, Pallas kernels for 7% -> 18%
where the time goes in v2:
time: 149 us; the launch traced here: 148 us
  Pallas kernels  58 us (39%)
  waiting for transfers between devices  48.4 us (32%)
  starting transfers between devices  30.7 us (21%)
  local copies, waits for them, and re-layouts  8.64 us (6%)
  between operations  1.76 us (1%)
    ppermute x23, waiting for transfers between devices, swap(): return lax.ppermute(block, 'mp', [(i, i ^ mask) for i in range(count)])  48.4 us
    ppermute x23, starting transfers between devices, swap(): return lax.ppermute(block, 'mp', [(i, i ^ mask) for i in range(count)])  29.2 us
    pallas_call x1, Pallas kernels, mixed_grad_phase(): pl.pallas_call(kernel, in_specs=[SMEM, SMEM, VMEM, HBM, VMEM, VMEM], out_...  9.63 us
    pallas_call x1, Pallas kernels, pick_phase(): pl.pallas_call(kernel, in_specs=[SMEM, VMEM, pl.BlockSpec(memory_space=pl...  9.13 us
    pallas_call x1, Pallas kernels, mix_phase(): pl.pallas_call(kernel, in_specs=[SMEM, SMEM] + [VMEM] * (2 + crossing) +...  7.6 us
    unnamed x59, local copies, waits for them, and re-layouts  7.4 us
    pallas_call x1, Pallas kernels, up_grad_phase(): pl.pallas_call(kernel, in_specs=[VMEM] * (3 + len(received)), out_specs=H...  6.65 us
    pallas_call x1, Pallas kernels, down_grad_phase(): pl.pallas_call(kernel, in_specs=[VMEM] * 2, out_specs=HBM, out_shape=jax....  6.46 us
  transfers between devices with their start and end apart: 24, of which 14 were waited for; matrix products, arithmetic and copies ran while one was open for 2% of the time, Pallas kernels for 18%

profile of v2, /device:TPU:0, one launch (start us, length us, event | category | flops | bytes accessed | tf_op | source)
XLA Modules:
  0.0 148.3 jit_solution(2733858140384137489)
XLA Ops:
  0.6 0.8 copy.17.ids_ref.refs_10_
  1.4 0.0 copy-start.5
  1.4 9.1 %pick_phase.1 = (s32[128,8]{1,0:T(8,128)S(1)}, f32[8,128]{1,0:T(8,128)S(1)}, bf16[256,4096]{1,0:T(8,128)(2,1)S(1)}, bf16[256,4096]{1,0:T(8,128)(2,1)}) custom-call(s32[1]{0:T(128)} %bitcast.me_ref, s32[128,8]{1,0:T(8,128)S(1)} %copy.17.ids_ref.refs_10_, bf16[2048,4096]{1,0:T(8,128)(2,1)} %vocab_ref.1), custom_call_target="tpu_custom_call" | custom-call | flops 4294967296 | bytes 16777216 | tf_op jit(solution)/shard_map/pick_phase/pallas_call | solution.py:539
  10.6 1.3 copy-done.6
  11.9 0.5 collective-permute-start.20
  12.4 0.1 copy.18.sc
  12.5 4.1 %up_phase.1 = (f32[128,1024]{1,0:T(8,128)S(1)}, bf16[128,1024]{1,0:T(8,128)(2,1)S(1)}) custom-call(bf16[128,4096]{1,0:T(8,128)(2,1)S(1)} %copy-done.5, bf16[4096,1024]{1,0:T(8,128)(2,1)} %val.1, s32[32,8]{1,0:T(8,128)S(1)} %copy.18.sc, f32[8,128]{1,0:T(8,128)S(1)} %get-tuple-element.80.refs_0_), custom_call_target="tpu_custom_call" | custom-call | flops 1073741824 | bytes 8388608 | tf_op jit(solution)/shard_map/up_phase/pallas_call | solution.py:144
  16.6 2.6 %collective-permute-start.16 = (bf16[128,1024]{1,0:T(8,128)(2,1)S(1)}, bf16[128,1024]{1,0:T(8,128)(2,1)S(1)}, u32[]{:S(2)}, u32[]{:S(2)}) collective-permute-start(bf16[128,1024]{1,0:T(8,128)(2,1)S(1)} %get-tuple-element.81.act_ref), channel_id=1, source_target_pairs={{0,2},{1,3},{2,0},{3,1},{4,6},{5,7},{6,4},{7,5},{8,10},{9,11},{10,... | collective-permute-start | bytes 786440 | tf_op jit(solution)/shard_map/ppermute | solution.py:32
  19.2 1.1 own_mix_phase.1.own_ref.refs_0_
  20.3 5.9 %collective-permute-done.16.refs_1_ = bf16[128,1024]{1,0:T(8,128)(2,1)S(1)} collective-permute-done((bf16[128,1024]{1,0:T(8,128)(2,1)S(1)}, bf16[128,1024]{1,0:T(8,128)(2,1)S(1)}, u32[]{:S(2)}, u32[]{:S(2)}) %collective-permute-start.16) | collective-permute-done | bytes 262176 | tf_op jit(solution)/shard_map/ppermute | solution.py:32
  26.2 2.1 %add_phase.8 = (bf16[128,4096]{1,0:T(8,128)(2,1)S(1)}, bf16[128,4096]{1,0:T(8,128)(2,1)S(1)}) custom-call(bf16[256,4096]{1,0:T(8,128)(2,1)S(1)} %copy-done.7, bf16[256,4096]{1,0:T(8,128)(2,1)} %collective-permute-done.20.b, f32[128,1024]{1,0:T(8,128)S(1)} %own_mix_phase.1.own_ref.refs_0_, bf16[128,1024]{1,0:T(8,128)(2,1)S(1)} %collective-permute-done.16.refs_1_), custom_call_target="tpu_custom_call" | custom-call | tf_op jit(solution)/shard_map/add_phase/pallas_call | solution.py:281
  28.3 1.8 %collective-permute-start.21 = (bf16[128,4096]{1,0:T(8,128)(2,1)S(1)}, bf16[128,4096]{1,0:T(8,128)(2,1)S(1)}, u32[]{:S(2)}, u32[]{:S(2)}) collective-permute-start(bf16[128,4096]{1,0:T(8,128)(2,1)S(1)} %get-tuple-element.87), channel_id=1, source_target_pairs={{0,2},{1,3},{2,0},{3,1},{4,6},{5,7},{6,4},{7,5},{8,10},{9,11},{10,... | collective-permute-start | bytes 3145736 | tf_op jit(solution)/shard_map/ppermute | solution.py:32
  30.1 2.6 %collective-permute-start.18 = (bf16[128,1024]{1,0:T(8,128)(2,1)S(1)}, bf16[128,1024]{1,0:T(8,128)(2,1)S(1)}, u32[]{:S(2)}, u32[]{:S(2)}) collective-permute-start(bf16[128,1024]{1,0:T(8,128)(2,1)S(1)} %get-tuple-element.81.act_ref), channel_id=1, source_target_pairs={{0,8},{1,9},{2,10},{3,11},{4,12},{5,13},{6,14},{7,15},{8,0},{9,1},... | collective-permute-start | bytes 786440 | tf_op jit(solution)/shard_map/ppermute | solution.py:32
  32.7 1.5 %collective-permute-start.17 = (bf16[128,1024]{1,0:T(8,128)(2,1)S(1)}, bf16[128,1024]{1,0:T(8,128)(2,1)S(1)}, u32[]{:S(2)}, u32[]{:S(2)}) collective-permute-start(bf16[128,1024]{1,0:T(8,128)(2,1)S(1)} %get-tuple-element.81.act_ref), channel_id=1, source_target_pairs={{0,4},{1,5},{2,6},{3,7},{4,0},{5,1},{6,2},{7,3},{8,12},{9,13},{10,... | collective-permute-start | bytes 786440 | tf_op jit(solution)/shard_map/ppermute | solution.py:32
  34.2 10.2 %collective-permute-done.18.refs_3_ = bf16[128,1024]{1,0:T(8,128)(2,1)S(1)} collective-permute-done((bf16[128,1024]{1,0:T(8,128)(2,1)S(1)}, bf16[128,1024]{1,0:T(8,128)(2,1)S(1)}, u32[]{:S(2)}, u32[]{:S(2)}) %collective-permute-start.18) | collective-permute-done | bytes 262176 | tf_op jit(solution)/shard_map/ppermute | solution.py:32
  44.3 0.2 collective-permute-done.17.refs_2_
  44.5 7.6 %mix_phase.1 = (bf16[128,1024]{1,0:T(8,128)(2,1)S(1)}, bf16[64,4096]{1,0:T(8,128)(2,1)S(1)}, bf16[64,4096]{1,0:T(8,128)(2,1)}) custom-call(s32[1]{0:T(128)} %bitcast.me_ref, s32[7,8]{1,0:T(8,128)S(1)} %copy-done.19, f32[128,1024]{1,0:T(8,128)} %copy-done.2, bf16[128,1024]{1,0:T(8,128)(2,1)S(1)} %collective-permute-done.15.refs_0_, ...), custom_call_target="tpu_custom_call" | custom-call | flops 1073741824 | bytes 8388608 | tf_op jit(solution)/shard_map/mix_phase/pallas_call | solution.py:254
  52.2 0.1 collective-permute-start.19
  52.2 1.1 collective-permute-done.21.b
  53.3 1.0 add_phase.9
  54.3 0.7 copy-done.17
  55.0 0.8 add_phase.10
  55.8 0.7 copy-done.15
  56.5 1.5 %collective-permute-start.22 = (bf16[32,4096]{1,0:T(8,128)(2,1)}, bf16[32,4096]{1,0:T(8,128)(2,1)}, u32[]{:S(2)}, u32[]{:S(2)}) collective-permute-start(bf16[32,4096]{1,0:T(8,128)(2,1)} %get-tuple-element.92), channel_id=1, source_target_pairs={{0,2},{1,3},{2,0},{3,1},{4,6},{5,7},{6,4},{7,5},{8,10},{9,11},{10,... | collective-permute-start | bytes 786440 | tf_op jit(solution)/shard_map/ppermute | solution.py:32
  58.0 1.6 %collective-permute-start.23 = (bf16[32,4096]{1,0:T(8,128)(2,1)}, bf16[32,4096]{1,0:T(8,128)(2,1)S(1)}, u32[]{:S(2)}, u32[]{:S(2)}) collective-permute-start(bf16[32,4096]{1,0:T(8,128)(2,1)} %get-tuple-element.88.refs_0_), channel_id=1, source_target_pairs={{0,4},{1,5},{2,6},{3,7},{4,0},{5,1},{6,2},{7,3},{8,12},{9,13},{10,... | collective-permute-start | bytes 786440 | tf_op jit(solution)/shard_map/ppermute | solution.py:32
  59.6 2.5 %collective-permute-start.24 = (bf16[32,4096]{1,0:T(8,128)(2,1)}, bf16[32,4096]{1,0:T(8,128)(2,1)S(1)}, u32[]{:S(2)}, u32[]{:S(2)}) collective-permute-start(bf16[32,4096]{1,0:T(8,128)(2,1)} %get-tuple-element.89.refs_1_), channel_id=1, source_target_pairs={{0,8},{1,9},{2,10},{3,11},{4,12},{5,13},{6,14},{7,15},{8,0},{9,1},... | collective-permute-start | bytes 786440 | tf_op jit(solution)/shard_map/ppermute | solution.py:32
  62.1 0.3 collective-permute-start.25
  62.4 1.5 %collective-permute-start.14 = (f32[8,128]{1,0:T(8,128)S(1)}, f32[8,128]{1,0:T(8,128)}, u32[]{:S(2)}, u32[]{:S(2)}) collective-permute-start(f32[8,128]{1,0:T(8,128)S(1)} %get-tuple-element.80.refs_0_), channel_id=1, source_target_pairs={{0,16},{16,0},{1,17},{17,1},{2,18},{18,2},{3,19},{19,3},{4,20},{20... | collective-permute-start | bytes 12296 | tf_op jit(solution)/shard_map/ppermute | solution.py:855
  63.9 0.6 collective-permute-done.22.b
  64.5 4.5 %collective-permute-done.23.refs_0_.refs_5_ = bf16[32,4096]{1,0:T(8,128)(2,1)S(1)} collective-permute-done((bf16[32,4096]{1,0:T(8,128)(2,1)}, bf16[32,4096]{1,0:T(8,128)(2,1)S(1)}, u32[]{:S(2)}, u32[]{:S(2)}) %collective-permute-start.23) | collective-permute-done | bytes 262176 | tf_op jit(solution)/shard_map/ppermute | solution.py:32
  69.0 12.2 %collective-permute-done.24.refs_1_.refs_6_ = bf16[32,4096]{1,0:T(8,128)(2,1)S(1)} collective-permute-done((bf16[32,4096]{1,0:T(8,128)(2,1)}, bf16[32,4096]{1,0:T(8,128)(2,1)S(1)}, u32[]{:S(2)}, u32[]{:S(2)}) %collective-permute-start.24) | collective-permute-done | bytes 262176 | tf_op jit(solution)/shard_map/ppermute | solution.py:32
  81.2 0.9 copy-done.16
  82.1 1.6 %add_phase.11 = (bf16[8,4096]{1,0:T(8,128)(2,1)}, bf16[8,4096]{1,0:T(8,128)(2,1)S(1)}, bf16[8,4096]{1,0:T(8,128)(2,1)S(1)}, bf16[8,4096]{1,0:T(8,128)(2,1)S(1)}) custom-call(bf16[32,4096]{1,0:T(8,128)(2,1)S(1)} %copy-done.16, bf16[32,4096]{1,0:T(8,128)(2,1)} %collective-permute-done.22.b, bf16[32,4096]{1,0:T(8,128)(2,1)S(1)} %collective-permute-done.23.refs_0_.refs_5_, ...), custom_call_target="tpu_custom_call" | custom-call | tf_op jit(solution)/shard_map/add_phase/pallas_call | solution.py:281
  83.7 3.5 %collective-permute-start.26 = (bf16[8,4096]{1,0:T(8,128)(2,1)S(1)}, bf16[8,4096]{1,0:T(8,128)(2,1)}, u32[]{:S(2)}, u32[]{:S(2)}) collective-permute-start(bf16[8,4096]{1,0:T(8,128)(2,1)S(1)} %get-tuple-element.94), channel_id=1, source_target_pairs={{0,4},{1,5},{2,6},{3,7},{4,0},{5,1},{6,2},{7,3},{8,12},{9,13},{10,... | collective-permute-start | bytes 196616 | tf_op jit(solution)/shard_map/ppermute | solution.py:32
  87.2 1.0 collective-permute-start.27
  88.2 1.5 collective-permute-start.28
  89.7 0.6 constant_dynamic-slice_fusion.refs_8_
  90.3 0.8 copy.20.refs_12_
  91.1 0.7 add.18
  91.8 0.5 slice.3
  93.0 0.2 collective-permute-done.27.refs_2_
  93.2 1.3 collective-permute-done.28.refs_3_
  94.5 0.9 copy-done.18
  95.5 2.4 %token_phase.1 = bf16[8,4224]{1,0:T(8,128)(2,1)S(1)} custom-call(s32[1]{0:T(128)} %bitcast.me_ref, bf16[8,4096]{1,0:T(8,128)(2,1)} %get-tuple-element.93.refs_0_, bf16[8,4096]{1,0:T(8,128)(2,1)} %collective-permute-done.26.refs_1_, bf16[8,4096]{1,0:T(8,128)(2,1)} %collective-permute-done.27.refs_2_, bf16[8,4096]{1,0:T(8,128)(2,1)} %collective-permute-done.28.refs_3_, ...), custom_call_target="tpu_custom_call" | custom-call | tf_op jit(solution)/shard_map/token_phase/pallas_call | solution.py:611
  98.0 0.2 conditional.1
  98.1 1.5 %collective-permute-start.31 = (bf16[8,4224]{1,0:T(8,128)(2,1)S(1)}, bf16[8,4224]{1,0:T(8,128)(2,1)S(1)}, u32[]{:S(2)}, u32[]{:S(2)}) collective-permute-start(bf16[8,4224]{1,0:T(8,128)(2,1)S(1)} %get-tuple-element.140), channel_id=1, source_target_pairs={{0,12},{1,13},{2,14},{3,15},{4,8},{5,9},{6,10},{7,11},{8,4},{9,5},... | collective-permute-start | bytes 202760 | tf_op jit(solution)/shard_map/ppermute | solution.py:32
  99.7 0.8 collective-permute-start.30
  100.5 2.1 %collective-permute-start.29 = (bf16[8,4224]{1,0:T(8,128)(2,1)S(1)}, bf16[8,4224]{1,0:T(8,128)(2,1)S(1)}, u32[]{:S(2)}, u32[]{:S(2)}) collective-permute-start(bf16[8,4224]{1,0:T(8,128)(2,1)S(1)} %get-tuple-element.140), channel_id=1, source_target_pairs={{0,4},{1,5},{2,6},{3,7},{4,0},{5,1},{6,2},{7,3},{8,12},{9,13},{10,... | collective-permute-start | bytes 202760 | tf_op jit(solution)/shard_map/ppermute | solution.py:32
  102.6 1.7 %collective-permute-done.31 = bf16[8,4224]{1,0:T(8,128)(2,1)S(1)} collective-permute-done((bf16[8,4224]{1,0:T(8,128)(2,1)S(1)}, bf16[8,4224]{1,0:T(8,128)(2,1)S(1)}, u32[]{:S(2)}, u32[]{:S(2)}) %collective-permute-start.31) | collective-permute-done | bytes 67616 | tf_op jit(solution)/shard_map/ppermute | solution.py:32
  104.3 1.4 collective-permute-done.30
  105.8 0.6 collective-permute-start.32
  106.5 5.8 %collective-permute-done.32 = bf16[32,4224]{1,0:T(8,128)(2,1)S(1)} collective-permute-done((bf16[32,4224]{1,0:T(8,128)(2,1)S(1)}, bf16[32,4224]{1,0:T(8,128)(2,1)S(1)}, u32[]{:S(2)}, u32[]{:S(2)}) %collective-permute-start.32) | collective-permute-done | bytes 270368 | tf_op jit(solution)/shard_map/ppermute | solution.py:32
  112.3 0.1 collective-permute-start.33
  112.4 1.9 %collective-permute-done.33 = bf16[64,4224]{1,0:T(8,128)(2,1)S(1)} collective-permute-done((bf16[64,4224]{1,0:T(8,128)(2,1)S(1)}, bf16[64,4224]{1,0:T(8,128)(2,1)S(1)}, u32[]{:S(2)}, u32[]{:S(2)}) %collective-permute-start.33) | collective-permute-done | bytes 540704 | tf_op jit(solution)/shard_map/ppermute | solution.py:32
  114.4 1.0 copy-done.3
  115.4 9.6 %mixed_grad_phase.1 = (f32[1,1]{1,0:T(1,128)}, bf16[128,1024]{1,0:T(8,128)(2,1)S(1)}, bf16[128,1024]{1,0:T(8,128)(2,1)S(1)}, bf16[128,1024]{1,0:T(8,128)(2,1)S(1...) custom-call(s32[1]{0:T(128)} %bitcast.me_ref, s32[7,8]{1,0:T(8,128)S(1)} %copy-done.19, ...), custom_call_target="tpu_custom_call" | custom-call | flops 1073741824 | bytes 8388608 | tf_op jit(solution)/shard_map/mixed_grad_phase/pallas_call | solution.py:671
  125.0 0.2 collective-permute-start.34
  125.2 0.6 collective-permute-start.35
  125.8 1.1 collective-permute-start.36
  127.0 1.2 collective-permute-start.37
  128.2 5.4 %block_grad_phase.1 = (f32[8,128,128]{2,1,0:T(8,128)}, f32[7,8,128,128]{3,2,1,0:T(8,128)}, f32[128,1024]{1,0:T(8,128)S(1)}) custom-call(s32[7,8]{1,0:T(8,128)S(1)} %copy-done.19, bf16[128,1024]{1,0:T(8,128)(2,1)S(1)} %copy-done.10, bf16[128,1024]{1,0:T(8,128)(2,1)S(1)} %get-tuple-element.101.mg, bf16[128,1024]{1,0:T(8,128)(2,1)S(1)} %collective-permute-done.15.refs_0_, ...), custom_call_target="tpu_custom_call" | custom-call | flops 402653184 | bytes 12582912 | tf_op jit(solution)/shard_map/block_grad_phase/pallas_call | solution.py:716
  133.6 6.5 %down_grad_phase.1 = f32[1024,4096]{1,0:T(8,128)} custom-call(bf16[128,1024]{1,0:T(8,128)(2,1)S(1)} %copy-done.14, bf16[128,4224]{1,0:T(8,128)(2,1)S(1)} %copy-done.4), custom_call_target="tpu_custom_call" | custom-call | flops 1073741824 | bytes 16777216 | tf_op jit(solution)/shard_map/down_grad_phase/pallas_call | solution.py:758
  140.1 1.4 collective-permute-done.37.refs_3_
  141.5 6.7 %up_grad_phase.1 = f32[4096,1024]{1,0:T(8,128)} custom-call(bf16[128,4096]{1,0:T(8,128)(2,1)S(1)} %copy-done.5, f32[128,1024]{1,0:T(8,128)S(1)} %copy-done.12, f32[128,1024]{1,0:T(8,128)S(1)} %get-tuple-element.102.grad_ref, bf16[128,1024]{1,0:T(8,128)(2,1)S(1)} %collective-permute-done.34.refs_0_, bf16[128,1024]{1,0:T(8,128)(2,1)S(1)} %collective-permute-done.35.refs_1_, ...), custom_call_target="tpu_custom_call" | custom-call | flops 1073741824 | bytes 16777216 | tf_op jit(solution)/shard_map/up_grad_phase/pallas_call | solution.py:802
  (63 shorter events, 0.3 us)
Async XLA Ops:
  1.4 10.9 %copy-start.27 = (s32[32,8]{0,1:T(8,128)S(1)}, s32[32,8]{0,1:T(8,128)}, u32[]{:S(2)}) copy-start(s32[32,8]{0,1:T(8,128)} %param.16) | copy-start | bytes 3076
  1.4 11.0 %copy-start.5 = (bf16[128,4096]{1,0:T(8,128)(2,1)S(1)}, bf16[128,4096]{1,0:T(8,128)(2,1)}, u32[]{:S(2)}) copy-start(bf16[128,4096]{1,0:T(8,128)(2,1)} %tok.3) | copy-start | bytes 3145732
  10.6 1.3 copy-start.6
  11.9 14.3 %collective-permute-start.20 = (bf16[256,4096]{1,0:T(8,128)(2,1)}, bf16[256,4096]{1,0:T(8,128)(2,1)}, u32[]{:S(2)}, u32[]{:S(2)}) collective-permute-start(bf16[256,4096]{1,0:T(8,128)(2,1)} %get-tuple-element.85), channel_id=1, source_target_pairs={{0,1},{1,0},{2,3},{3,2},{4,5},{5,4},{6,7},{7,6},{8,9},{9,8},{10,11... | collective-permute-start | bytes 6291464 | tf_op jit(solution)/shard_map/ppermute | solution.py:32
  12.4 6.8 %copy-start = (bf16[7,8,128,128]{3,2,1,0:T(8,128)(2,1)S(1)}, bf16[7,8,128,128]{3,2,1,0:T(8,128)(2,1)}, u32[]{:S(2)}) copy-start(bf16[7,8,128,128]{3,2,1,0:T(8,128)(2,1)} %refs_5_.3) | copy-start | bytes 5505028
  12.4 6.8 %copy-start.8 = (bf16[8,128,128]{2,1,0:T(8,128)(2,1)S(1)}, bf16[8,128,128]{2,1,0:T(8,128)(2,1)}, u32[]{:S(2)}) copy-start(bf16[8,128,128]{2,1,0:T(8,128)(2,1)} %refs_4_.3) | copy-start | bytes 786436
  12.4 6.8 %copy-start.19 = (s32[7,8]{1,0:T(8,128)S(1)}, s32[7,8]{1,0:T(8,128)}, u32[]{:S(2)}) copy-start(s32[7,8]{1,0:T(8,128)} %pat.7) | copy-start | bytes 676
  16.6 3.7 %copy-start.11 = (f32[128,1024]{1,0:T(8,128)}, f32[128,1024]{1,0:T(8,128)S(1)}, u32[]{:S(2)}) copy-start(f32[128,1024]{1,0:T(8,128)S(1)} %get-tuple-element.100.pre_ref) | copy-start | bytes 1572868
  16.6 17.6 %copy-start.9 = (bf16[128,1024]{1,0:T(8,128)(2,1)}, bf16[128,1024]{1,0:T(8,128)(2,1)S(1)}, u32[]{:S(2)}) copy-start(bf16[128,1024]{1,0:T(8,128)(2,1)S(1)} %get-tuple-element.81.act_ref) | copy-start | bytes 786436
  16.6 9.6 %copy-start.7 = (bf16[256,4096]{1,0:T(8,128)(2,1)S(1)}, bf16[256,4096]{1,0:T(8,128)(2,1)}, u32[]{:S(2)}) copy-start(bf16[256,4096]{1,0:T(8,128)(2,1)} %copy-done.6) | copy-start | bytes 6291460
  16.6 9.6 %collective-permute-start.16 = (bf16[128,1024]{1,0:T(8,128)(2,1)S(1)}, bf16[128,1024]{1,0:T(8,128)(2,1)S(1)}, u32[]{:S(2)}, u32[]{:S(2)}) collective-permute-start(bf16[128,1024]{1,0:T(8,128)(2,1)S(1)} %get-tuple-element.81.act_ref), channel_id=1, source_target_pairs={{0,2},{1,3},{2,0},{3,1},{4,6},{5,7},{6,4},{7,5},{8,10},{9,11},{10,... | collective-permute-start | bytes 786440 | tf_op jit(solution)/shard_map/ppermute | solution.py:32
  20.3 8.0 %copy-start.2 = (f32[128,1024]{1,0:T(8,128)}, f32[128,1024]{1,0:T(8,128)S(1)}, u32[]{:S(2)}) copy-start(f32[128,1024]{1,0:T(8,128)S(1)} %own_mix_phase.1.own_ref.refs_0_) | copy-start | bytes 1572868
  26.2 18.4 %copy-start.20 = (s32[8,32]{1,0:T(8,128)S(1)}, s32[8,32]{1,0:T(8,128)}, u32[]{:S(2)}) copy-start(s32[8,32]{1,0:T(8,128)} %sc.2) | copy-start | bytes 3076
  28.3 25.1 %collective-permute-start.21 = (bf16[128,4096]{1,0:T(8,128)(2,1)S(1)}, bf16[128,4096]{1,0:T(8,128)(2,1)S(1)}, u32[]{:S(2)}, u32[]{:S(2)}) collective-permute-start(bf16[128,4096]{1,0:T(8,128)(2,1)S(1)} %get-tuple-element.87), channel_id=1, source_target_pairs={{0,2},{1,3},{2,0},{3,1},{4,6},{5,7},{6,4},{7,5},{8,10},{9,11},{10,... | collective-permute-start | bytes 3145736 | tf_op jit(solution)/shard_map/ppermute | solution.py:32
  30.1 14.3 %collective-permute-start.18 = (bf16[128,1024]{1,0:T(8,128)(2,1)S(1)}, bf16[128,1024]{1,0:T(8,128)(2,1)S(1)}, u32[]{:S(2)}, u32[]{:S(2)}) collective-permute-start(bf16[128,1024]{1,0:T(8,128)(2,1)S(1)} %get-tuple-element.81.act_ref), channel_id=1, source_target_pairs={{0,8},{1,9},{2,10},{3,11},{4,12},{5,13},{6,14},{7,15},{8,0},{9,1},... | collective-permute-start | bytes 786440 | tf_op jit(solution)/shard_map/ppermute | solution.py:32
  32.7 11.9 %collective-permute-start.17 = (bf16[128,1024]{1,0:T(8,128)(2,1)S(1)}, bf16[128,1024]{1,0:T(8,128)(2,1)S(1)}, u32[]{:S(2)}, u32[]{:S(2)}) collective-permute-start(bf16[128,1024]{1,0:T(8,128)(2,1)S(1)} %get-tuple-element.81.act_ref), channel_id=1, source_target_pairs={{0,4},{1,5},{2,6},{3,7},{4,0},{5,1},{6,2},{7,3},{8,12},{9,13},{10,... | collective-permute-start | bytes 786440 | tf_op jit(solution)/shard_map/ppermute | solution.py:32
  34.2 10.4 %collective-permute-start.15 = (bf16[128,1024]{1,0:T(8,128)(2,1)S(1)}, bf16[128,1024]{1,0:T(8,128)(2,1)S(1)}, u32[]{:S(2)}, u32[]{:S(2)}) collective-permute-start(bf16[128,1024]{1,0:T(8,128)(2,1)S(1)} %get-tuple-element.81.act_ref), channel_id=1, source_target_pairs={{0,1},{1,0},{2,3},{3,2},{4,5},{5,4},{6,7},{7,6},{8,9},{9,8},{10,11... | collective-permute-start | bytes 786440 | tf_op jit(solution)/shard_map/ppermute | solution.py:32
  52.2 3.6 %copy-start.13 = (bf16[128,1024]{1,0:T(8,128)(2,1)}, bf16[128,1024]{1,0:T(8,128)(2,1)S(1)}, u32[]{:S(2)}) copy-start(bf16[128,1024]{1,0:T(8,128)(2,1)S(1)} %get-tuple-element.107.mixed_ref) | copy-start | bytes 786436
  52.2 2.8 %collective-permute-start.19 = (bf16[64,4096]{1,0:T(8,128)(2,1)}, bf16[64,4096]{1,0:T(8,128)(2,1)S(1)}, u32[]{:S(2)}, u32[]{:S(2)}) collective-permute-start(bf16[64,4096]{1,0:T(8,128)(2,1)} %get-tuple-element.83), channel_id=1, source_target_pairs={{0,1},{1,0},{2,3},{3,2},{4,5},{5,4},{6,7},{7,6},{8,9},{9,8},{10,11... | collective-permute-start | bytes 1572872 | tf_op jit(solution)/shard_map/ppermute | solution.py:32
  54.3 0.7 copy-start.17
  55.8 0.7 copy-start.15
  56.5 8.0 %collective-permute-start.22 = (bf16[32,4096]{1,0:T(8,128)(2,1)}, bf16[32,4096]{1,0:T(8,128)(2,1)}, u32[]{:S(2)}, u32[]{:S(2)}) collective-permute-start(bf16[32,4096]{1,0:T(8,128)(2,1)} %get-tuple-element.92), channel_id=1, source_target_pairs={{0,2},{1,3},{2,0},{3,1},{4,6},{5,7},{6,4},{7,5},{8,10},{9,11},{10,... | collective-permute-start | bytes 786440 | tf_op jit(solution)/shard_map/ppermute | solution.py:32
  58.0 11.0 %collective-permute-start.23 = (bf16[32,4096]{1,0:T(8,128)(2,1)}, bf16[32,4096]{1,0:T(8,128)(2,1)S(1)}, u32[]{:S(2)}, u32[]{:S(2)}) collective-permute-start(bf16[32,4096]{1,0:T(8,128)(2,1)} %get-tuple-element.88.refs_0_), channel_id=1, source_target_pairs={{0,4},{1,5},{2,6},{3,7},{4,0},{5,1},{6,2},{7,3},{8,12},{9,13},{10,... | collective-permute-start | bytes 786440 | tf_op jit(solution)/shard_map/ppermute | solution.py:32
  59.6 21.6 %collective-permute-start.24 = (bf16[32,4096]{1,0:T(8,128)(2,1)}, bf16[32,4096]{1,0:T(8,128)(2,1)S(1)}, u32[]{:S(2)}, u32[]{:S(2)}) collective-permute-start(bf16[32,4096]{1,0:T(8,128)(2,1)} %get-tuple-element.89.refs_1_), channel_id=1, source_target_pairs={{0,8},{1,9},{2,10},{3,11},{4,12},{5,13},{6,14},{7,15},{8,0},{9,1},... | collective-permute-start | bytes 786440 | tf_op jit(solution)/shard_map/ppermute | solution.py:32
  62.1 19.0 %collective-permute-start.25 = (bf16[32,4096]{1,0:T(8,128)(2,1)S(1)}, bf16[32,4096]{1,0:T(8,128)(2,1)S(1)}, u32[]{:S(2)}, u32[]{:S(2)}) collective-permute-start(bf16[32,4096]{1,0:T(8,128)(2,1)S(1)} %get-tuple-element.90.refs_2_), channel_id=1, source_target_pairs={{0,12},{1,13},{2,14},{3,15},{4,8},{5,9},{6,10},{7,11},{8,4},{9,5},... | collective-permute-start | bytes 786440 | tf_op jit(solution)/shard_map/ppermute | solution.py:32
  62.4 28.7 %collective-permute-start.14 = (f32[8,128]{1,0:T(8,128)S(1)}, f32[8,128]{1,0:T(8,128)}, u32[]{:S(2)}, u32[]{:S(2)}) collective-permute-start(f32[8,128]{1,0:T(8,128)S(1)} %get-tuple-element.80.refs_0_), channel_id=1, source_target_pairs={{0,16},{16,0},{1,17},{17,1},{2,18},{18,2},{3,19},{19,3},{4,20},{20... | collective-permute-start | bytes 12296 | tf_op jit(solution)/shard_map/ppermute | solution.py:855
  81.2 1.0 copy-start.16
  83.7 14.2 %copy-start.25 = (s32[128,8]{0,1:T(8,128)S(1)}, s32[128,8]{0,1:T(8,128)}, u32[]{:S(2)}) copy-start(s32[128,8]{0,1:T(8,128)} %param.24) | copy-start | bytes 12292
  83.7 9.2 %collective-permute-start.26 = (bf16[8,4096]{1,0:T(8,128)(2,1)S(1)}, bf16[8,4096]{1,0:T(8,128)(2,1)}, u32[]{:S(2)}, u32[]{:S(2)}) collective-permute-start(bf16[8,4096]{1,0:T(8,128)(2,1)S(1)} %get-tuple-element.94), channel_id=1, source_target_pairs={{0,4},{1,5},{2,6},{3,7},{4,0},{5,1},{6,2},{7,3},{8,12},{9,13},{10,... | collective-permute-start | bytes 196616 | tf_op jit(solution)/shard_map/ppermute | solution.py:32
  87.2 6.0 %collective-permute-start.27 = (bf16[8,4096]{1,0:T(8,128)(2,1)S(1)}, bf16[8,4096]{1,0:T(8,128)(2,1)}, u32[]{:S(2)}, u32[]{:S(2)}) collective-permute-start(bf16[8,4096]{1,0:T(8,128)(2,1)S(1)} %get-tuple-element.95), channel_id=1, source_target_pairs={{0,8},{1,9},{2,10},{3,11},{4,12},{5,13},{6,14},{7,15},{8,0},{9,1},... | collective-permute-start | bytes 196616 | tf_op jit(solution)/shard_map/ppermute | solution.py:32
  88.2 6.3 %collective-permute-start.28 = (bf16[8,4096]{1,0:T(8,128)(2,1)S(1)}, bf16[8,4096]{1,0:T(8,128)(2,1)}, u32[]{:S(2)}, u32[]{:S(2)}) collective-permute-start(bf16[8,4096]{1,0:T(8,128)(2,1)S(1)} %get-tuple-element.96), channel_id=1, source_target_pairs={{0,12},{1,13},{2,14},{3,15},{4,8},{5,9},{6,10},{7,11},{8,4},{9,5},... | collective-permute-start | bytes 196616 | tf_op jit(solution)/shard_map/ppermute | solution.py:32
  91.8 6.1 %copy-start.26 = (f32[128,8]{0,1:T(8,128)S(1)}, f32[128,8]{0,1:T(8,128)}, u32[]{:S(2)}) copy-start(f32[128,8]{0,1:T(8,128)} %param.25) | copy-start | bytes 12292
  94.5 1.0 copy-start.18
  95.5 2.5 %copy-start.21 = (bf16[8,4096]{1,0:T(8,128)(2,1)S(1)}, bf16[8,4096]{1,0:T(8,128)(2,1)}, u32[]{:S(2)}) copy-start(bf16[8,4096]{1,0:T(8,128)(2,1)} %constant_dynamic-slice_fusion.refs_8_) | copy-start | bytes 196612
  95.5 2.5 %copy-start.22 = (f32[4096]{0:T(1024)S(1)}, f32[4096]{0:T(1024)}, u32[]{:S(2)}) copy-start(f32[4096]{0:T(1024)} %param.22) | copy-start | bytes 49156
  98.1 6.2 %collective-permute-start.31 = (bf16[8,4224]{1,0:T(8,128)(2,1)S(1)}, bf16[8,4224]{1,0:T(8,128)(2,1)S(1)}, u32[]{:S(2)}, u32[]{:S(2)}) collective-permute-start(bf16[8,4224]{1,0:T(8,128)(2,1)S(1)} %get-tuple-element.140), channel_id=1, source_target_pairs={{0,12},{1,13},{2,14},{3,15},{4,8},{5,9},{6,10},{7,11},{8,4},{9,5},... | collective-permute-start | bytes 202760 | tf_op jit(solution)/shard_map/ppermute | solution.py:32
  99.7 6.1 %collective-permute-start.30 = (bf16[8,4224]{1,0:T(8,128)(2,1)S(1)}, bf16[8,4224]{1,0:T(8,128)(2,1)S(1)}, u32[]{:S(2)}, u32[]{:S(2)}) collective-permute-start(bf16[8,4224]{1,0:T(8,128)(2,1)S(1)} %get-tuple-element.140), channel_id=1, source_target_pairs={{0,8},{1,9},{2,10},{3,11},{4,12},{5,13},{6,14},{7,15},{8,0},{9,1},... | collective-permute-start | bytes 202760 | tf_op jit(solution)/shard_map/ppermute | solution.py:32
  100.5 5.2 %collective-permute-start.29 = (bf16[8,4224]{1,0:T(8,128)(2,1)S(1)}, bf16[8,4224]{1,0:T(8,128)(2,1)S(1)}, u32[]{:S(2)}, u32[]{:S(2)}) collective-permute-start(bf16[8,4224]{1,0:T(8,128)(2,1)S(1)} %get-tuple-element.140), channel_id=1, source_target_pairs={{0,4},{1,5},{2,6},{3,7},{4,0},{5,1},{6,2},{7,3},{8,12},{9,13},{10,... | collective-permute-start | bytes 202760 | tf_op jit(solution)/shard_map/ppermute | solution.py:32
  105.8 6.5 %collective-permute-start.32 = (bf16[32,4224]{1,0:T(8,128)(2,1)S(1)}, bf16[32,4224]{1,0:T(8,128)(2,1)S(1)}, u32[]{:S(2)}, u32[]{:S(2)}) collective-permute-start(bf16[32,4224]{1,0:T(8,128)(2,1)S(1)} %pad_maximum_fusion.1), channel_id=1, source_target_pairs={{0,2},{1,3},{2,0},{3,1},{4,6},{5,7},{6,4},{7,5},{8,10},{9,11},{10,... | collective-permute-start | bytes 811016 | tf_op jit(solution)/shard_map/ppermute | solution.py:32
  112.3 2.0 %collective-permute-start.33 = (bf16[64,4224]{1,0:T(8,128)(2,1)S(1)}, bf16[64,4224]{1,0:T(8,128)(2,1)S(1)}, u32[]{:S(2)}, u32[]{:S(2)}) collective-permute-start(bf16[64,4224]{1,0:T(8,128)(2,1)S(1)} %get-tuple-element.130), channel_id=1, source_target_pairs={{0,1},{1,0},{2,3},{3,2},{4,5},{5,4},{6,7},{7,6},{8,9},{9,8},{10,11... | collective-permute-start | bytes 1622024 | tf_op jit(solution)/shard_map/ppermute | solution.py:32
  114.4 1.0 copy-start.3
  115.4 12.8 %copy-start.1 = (bf16[7,8,128,128]{3,2,1,0:T(8,128)(2,1)S(1)}, bf16[7,8,128,128]{3,2,1,0:T(8,128)(2,1)}, u32[]{:S(2)}) copy-start(bf16[7,8,128,128]{3,2,1,0:T(8,128)(2,1)} %refs_5_.3) | copy-start | bytes 5505028
  115.4 12.8 %copy-start.10 = (bf16[128,1024]{1,0:T(8,128)(2,1)S(1)}, bf16[128,1024]{1,0:T(8,128)(2,1)}, u32[]{:S(2)}) copy-start(bf16[128,1024]{1,0:T(8,128)(2,1)} %copy-done.9) | copy-start | bytes 786436
  125.0 15.1 %collective-permute-start.34 = (bf16[128,1024]{1,0:T(8,128)(2,1)S(1)}, bf16[128,1024]{1,0:T(8,128)(2,1)S(1)}, u32[]{:S(2)}, u32[]{:S(2)}) collective-permute-start(bf16[128,1024]{1,0:T(8,128)(2,1)S(1)} %get-tuple-element.103), channel_id=1, source_target_pairs={{0,1},{1,0},{2,3},{3,2},{4,5},{5,4},{6,7},{7,6},{8,9},{9,8},{10,11... | collective-permute-start | bytes 786440 | tf_op jit(solution)/shard_map/ppermute | solution.py:32
  125.2 14.9 %collective-permute-start.35 = (bf16[128,1024]{1,0:T(8,128)(2,1)S(1)}, bf16[128,1024]{1,0:T(8,128)(2,1)S(1)}, u32[]{:S(2)}, u32[]{:S(2)}) collective-permute-start(bf16[128,1024]{1,0:T(8,128)(2,1)S(1)} %get-tuple-element.104), channel_id=1, source_target_pairs={{0,2},{1,3},{2,0},{3,1},{4,6},{5,7},{6,4},{7,5},{8,10},{9,11},{10,... | collective-permute-start | bytes 786440 | tf_op jit(solution)/shard_map/ppermute | solution.py:32
  125.8 14.3 %collective-permute-start.36 = (bf16[128,1024]{1,0:T(8,128)(2,1)S(1)}, bf16[128,1024]{1,0:T(8,128)(2,1)S(1)}, u32[]{:S(2)}, u32[]{:S(2)}) collective-permute-start(bf16[128,1024]{1,0:T(8,128)(2,1)S(1)} %get-tuple-element.105), channel_id=1, source_target_pairs={{0,4},{1,5},{2,6},{3,7},{4,0},{5,1},{6,2},{7,3},{8,12},{9,13},{10,... | collective-permute-start | bytes 786440 | tf_op jit(solution)/shard_map/ppermute | solution.py:32
  127.0 14.6 %collective-permute-start.37 = (bf16[128,1024]{1,0:T(8,128)(2,1)S(1)}, bf16[128,1024]{1,0:T(8,128)(2,1)S(1)}, u32[]{:S(2)}, u32[]{:S(2)}) collective-permute-start(bf16[128,1024]{1,0:T(8,128)(2,1)S(1)} %get-tuple-element.106), channel_id=1, source_target_pairs={{0,8},{1,9},{2,10},{3,11},{4,12},{5,13},{6,14},{7,15},{8,0},{9,1},... | collective-permute-start | bytes 786440 | tf_op jit(solution)/shard_map/ppermute | solution.py:32
  128.2 5.5 %copy-start.4 = (bf16[128,4224]{1,0:T(8,128)(2,1)S(1)}, bf16[128,4224]{1,0:T(8,128)(2,1)}, u32[]{:S(2)}) copy-start(bf16[128,4224]{1,0:T(8,128)(2,1)} %copy-done.3) | copy-start | bytes 3244036
  128.2 5.5 %copy-start.14 = (bf16[128,1024]{1,0:T(8,128)(2,1)S(1)}, bf16[128,1024]{1,0:T(8,128)(2,1)}, u32[]{:S(2)}) copy-start(bf16[128,1024]{1,0:T(8,128)(2,1)} %copy-done.13) | copy-start | bytes 786436
  133.6 7.9 %copy-start.12 = (f32[128,1024]{1,0:T(8,128)S(1)}, f32[128,1024]{1,0:T(8,128)}, u32[]{:S(2)}) copy-start(f32[128,1024]{1,0:T(8,128)} %copy-done.11) | copy-start | bytes 1572868

commit v3 on v2

--- a/solution.py
+++ b/solution.py
@@ -249,7 +249,7 @@
             send[:, columns(c, chunk)] = result[half:]
             return carry
 
-        lax.fori_loop(0, steps, project, 0, unroll=2)
+        lax.fori_loop(0, steps, project, 0)
 
     return pl.pallas_call(
         kernel,
@@ -657,7 +657,7 @@
             result[:, columns(i, pair * width)] = dot_nt(grad_ref[:, :features], weight).astype(BF16)
             return carry
 
-        lax.fori_loop(0, blocks // pair, step, 0, unroll=2)
+        lax.fori_loop(0, blocks // pair, step, 0)
         mixed_grad[...] = dot(order, result[...]).astype(BF16)
         for h in range(blocks):
             here = slice(h * width, (h + 1) * width)
@@ -848,14 +848,17 @@
         pre, act = up_phase(tokens, up_values, up_scale, width, [flag])
         received = [swap(act, 1 << k - local) for k in range(local, levels)]
         own_mix = own_mix_phase(pattern, act, diag_blocks, partner_blocks, local, ())
-        kept, sent = add_phase(kept, swap(sent, group_masks(groups[0])[1]), 2, [own_mix, *received[1:2]])
+        near, far, near_sent, far_sent = add_phase(
+            kept, swap(sent, group_masks(groups[0])[1]), 4, [own_mix, *received[1:2]]
+        )
         parts = lax.axis_size("groups")
         turned = flag
         for _ in range(parts - 1):
             turned = lax.ppermute(turned, "groups", [(i, (i + 1) % parts) for i in range(parts)])
             flag = flag + turned
         crowded = flag[0, 0] > 0
-        laid = swap(sent, group_masks(groups[1])[1])
+        far_laid = swap(far_sent, group_masks(groups[1])[1])
+        near_laid = swap(near_sent, group_masks(groups[1])[1])
     else:
         pre, act = up_phase(tokens, up_values, up_scale, width, [])
         received = [swap(act, 1 << k - local) for k in range(local, levels)]
@@ -865,9 +868,10 @@
     )
     if sparse:
         masks = group_masks(groups[SHARED])
-        pieces = add_phase(kept, laid, len(masks), [])
-        picked = [swap(piece, m) for piece, m in zip(pieces, masks)]
-        terms = reduce_rows(keep, send, groups, [pieces[1:], picked[1:]])
+        far = add_phase(far, far_laid, len(masks) // 2, [])
+        near = add_phase(near, near_laid, len(masks) // 2, far[:1])
+        picked = [swap(piece, m) for piece, m in zip([*near, *far], masks)]
+        terms = reduce_rows(keep, send, groups, [far, picked[1:]])
     else:
         terms = reduce_rows(keep, send, groups)
 

time: 149 us -> 135 us (0.906)
  waiting for transfers between devices: 48.4 us -> 39.7 us
  local copies, waits for them, and re-layouts: 8.64 us -> 6.44 us
  Pallas kernels: 58 us -> 56.1 us
    ppermute x23 -> x24, waiting for transfers between devices: 48.4 us -> 39.7 us  [swap(): return lax.ppermute(block, 'mp', [(i, i ^ mask) for i in range(count)])]
    pallas_call x1, Pallas kernels: 9.63 us -> 7.93 us  [mixed_grad_phase(): pl.pallas_call(kernel, in_specs=[SMEM, SMEM, VMEM, HBM, VMEM, VMEM], out_...]
    unnamed x59, local copies, waits for them, and re-layouts: 7.4 us -> 5.83 us
    ppermute x23 -> x24, starting transfers between devices: 29.2 us -> 27.9 us  [swap(): return lax.ppermute(block, 'mp', [(i, i ^ mask) for i in range(count)])]
    pallas_call x4 -> x5, Pallas kernels: 5.42 us -> 5.25 us  [add_phase(): pl.pallas_call(kernel, in_specs=[VMEM] * 2 + [UNREAD] * len(after), out_s...]
  transfers between devices with their start and end apart: 24 -> 25, of which waited for: 14 -> 13; matrix products, arithmetic and copies ran while one was open for 2% -> 2% of each run, Pallas kernels for 18% -> 22%
where the time goes in v3:
time: 135 us; the launch traced here: 134 us
  Pallas kernels  56.1 us (42%)
  waiting for transfers between devices  39.7 us (29%)
  starting transfers between devices  29.4 us (22%)
  local copies, waits for them, and re-layouts  6.44 us (5%)
  between operations  1.8 us (1%)
    ppermute x24, waiting for transfers between devices, swap(): return lax.ppermute(block, 'mp', [(i, i ^ mask) for i in range(count)])  39.7 us
    ppermute x24, starting transfers between devices, swap(): return lax.ppermute(block, 'mp', [(i, i ^ mask) for i in range(count)])  27.9 us
    pallas_call x1, Pallas kernels, pick_phase(): pl.pallas_call(kernel, in_specs=[SMEM, VMEM, pl.BlockSpec(memory_space=pl...  9.13 us
    pallas_call x1, Pallas kernels, mixed_grad_phase(): pl.pallas_call(kernel, in_specs=[SMEM, SMEM, VMEM, HBM, VMEM, VMEM], out_...  7.93 us
    pallas_call x1, Pallas kernels, mix_phase(): pl.pallas_call(kernel, in_specs=[SMEM, SMEM] + [VMEM] * (2 + crossing) +...  7.77 us
    pallas_call x1, Pallas kernels, up_grad_phase(): pl.pallas_call(kernel, in_specs=[VMEM] * (3 + len(received)), out_specs=H...  6.66 us
    pallas_call x1, Pallas kernels, down_grad_phase(): pl.pallas_call(kernel, in_specs=[VMEM] * 2, out_specs=HBM, out_shape=jax....  6.46 us
    unnamed x59, local copies, waits for them, and re-layouts  5.83 us
  transfers between devices with their start and end apart: 25, of which 13 were waited for; matrix products, arithmetic and copies ran while one was open for 2% of the time, Pallas kernels for 22%

profile of v3, /device:TPU:0, one launch (start us, length us, event | category | flops | bytes accessed | tf_op | source)
XLA Modules:
  0.0 134.4 jit_solution(7444524118495856908)
XLA Ops:
  0.6 0.8 copy.17.ids_ref.refs_10_
  1.4 0.0 copy-start.5
  1.4 9.1 %pick_phase.1 = (s32[128,8]{1,0:T(8,128)S(1)}, f32[8,128]{1,0:T(8,128)S(1)}, bf16[256,4096]{1,0:T(8,128)(2,1)S(1)}, bf16[256,4096]{1,0:T(8,128)(2,1)}) custom-call(s32[1]{0:T(128)} %bitcast.me_ref, s32[128,8]{1,0:T(8,128)S(1)} %copy.17.ids_ref.refs_10_, bf16[2048,4096]{1,0:T(8,128)(2,1)} %vocab_ref.1), custom_call_target="tpu_custom_call" | custom-call | flops 4294967296 | bytes 16777216 | tf_op jit(solution)/shard_map/pick_phase/pallas_call | solution.py:539
  10.6 0.0 copy-start.6
  10.6 1.3 copy-done.6
  11.9 0.5 collective-permute-start.20
  12.4 0.1 copy.18.sc
  12.4 0.0 copy-start.20
  12.5 4.1 %up_phase.1 = (f32[128,1024]{1,0:T(8,128)S(1)}, bf16[128,1024]{1,0:T(8,128)(2,1)S(1)}) custom-call(bf16[128,4096]{1,0:T(8,128)(2,1)S(1)} %copy-done.5, bf16[4096,1024]{1,0:T(8,128)(2,1)} %val.1, s32[32,8]{1,0:T(8,128)S(1)} %copy.18.sc, f32[8,128]{1,0:T(8,128)S(1)} %get-tuple-element.82.refs_0_), custom_call_target="tpu_custom_call" | custom-call | flops 1073741824 | bytes 8388608 | tf_op jit(solution)/shard_map/up_phase/pallas_call | solution.py:144
  16.6 0.0 copy-start.16
  16.6 0.8 copy-done.16
  17.4 2.5 %collective-permute-start.16 = (bf16[128,1024]{1,0:T(8,128)(2,1)S(1)}, bf16[128,1024]{1,0:T(8,128)(2,1)S(1)}, u32[]{:S(2)}, u32[]{:S(2)}) collective-permute-start(bf16[128,1024]{1,0:T(8,128)(2,1)S(1)} %get-tuple-element.83.act_ref), channel_id=1, source_target_pairs={{0,2},{1,3},{2,0},{3,1},{4,6},{5,7},{6,4},{7,5},{8,10},{9,11},{10,... | collective-permute-start | bytes 786440 | tf_op jit(solution)/shard_map/ppermute | solution.py:32
  19.9 2.6 %collective-permute-start.18 = (bf16[128,1024]{1,0:T(8,128)(2,1)S(1)}, bf16[128,1024]{1,0:T(8,128)(2,1)S(1)}, u32[]{:S(2)}, u32[]{:S(2)}) collective-permute-start(bf16[128,1024]{1,0:T(8,128)(2,1)S(1)} %get-tuple-element.83.act_ref), channel_id=1, source_target_pairs={{0,8},{1,9},{2,10},{3,11},{4,12},{5,13},{6,14},{7,15},{8,0},{9,1},... | collective-permute-start | bytes 786440 | tf_op jit(solution)/shard_map/ppermute | solution.py:32
  22.5 1.5 %collective-permute-start.17 = (bf16[128,1024]{1,0:T(8,128)(2,1)S(1)}, bf16[128,1024]{1,0:T(8,128)(2,1)S(1)}, u32[]{:S(2)}, u32[]{:S(2)}) collective-permute-start(bf16[128,1024]{1,0:T(8,128)(2,1)S(1)} %get-tuple-element.83.act_ref), channel_id=1, source_target_pairs={{0,4},{1,5},{2,6},{3,7},{4,0},{5,1},{6,2},{7,3},{8,12},{9,13},{10,... | collective-permute-start | bytes 786440 | tf_op jit(solution)/shard_map/ppermute | solution.py:32
  24.0 1.1 own_mix_phase.1.own_ref.refs_0_
  25.1 1.8 %collective-permute-done.16.refs_1_ = bf16[128,1024]{1,0:T(8,128)(2,1)S(1)} collective-permute-done((bf16[128,1024]{1,0:T(8,128)(2,1)S(1)}, bf16[128,1024]{1,0:T(8,128)(2,1)S(1)}, u32[]{:S(2)}, u32[]{:S(2)}) %collective-permute-start.16) | collective-permute-done | bytes 262176 | tf_op jit(solution)/shard_map/ppermute | solution.py:32
  26.9 2.3 %add_phase.9 = (bf16[64,4096]{1,0:T(8,128)(2,1)S(1)}, bf16[64,4096]{1,0:T(8,128)(2,1)S(1)}, bf16[64,4096]{1,0:T(8,128)(2,1)S(1)}, bf16[64,4096]{1,0:T(8,128)(2,1)S(1)}) custom-call(bf16[256,4096]{1,0:T(8,128)(2,1)S(1)} %copy-done.7, bf16[256,4096]{1,0:T(8,128)(2,1)} %collective-permute-done.20.b, f32[128,1024]{1,0:T(8,128)S(1)} %own_mix_phase.1.own_ref.refs_0_, ...), custom_call_target="tpu_custom_call" | custom-call | tf_op jit(solution)/shard_map/add_phase/pallas_call | solution.py:281
  29.2 1.8 %collective-permute-start.21 = (bf16[64,4096]{1,0:T(8,128)(2,1)S(1)}, bf16[64,4096]{1,0:T(8,128)(2,1)S(1)}, u32[]{:S(2)}, u32[]{:S(2)}) collective-permute-start(bf16[64,4096]{1,0:T(8,128)(2,1)S(1)} %get-tuple-element.89), channel_id=1, source_target_pairs={{0,2},{1,3},{2,0},{3,1},{4,6},{5,7},{6,4},{7,5},{8,10},{9,11},{10,... | collective-permute-start | bytes 1572872 | tf_op jit(solution)/shard_map/ppermute | solution.py:32
  31.0 4.0 %collective-permute-done.18.refs_3_ = bf16[128,1024]{1,0:T(8,128)(2,1)S(1)} collective-permute-done((bf16[128,1024]{1,0:T(8,128)(2,1)S(1)}, bf16[128,1024]{1,0:T(8,128)(2,1)S(1)}, u32[]{:S(2)}, u32[]{:S(2)}) %collective-permute-start.18) | collective-permute-done | bytes 262176 | tf_op jit(solution)/shard_map/ppermute | solution.py:32
  35.0 0.2 collective-permute-done.17.refs_2_
  35.2 7.8 %mix_phase.1 = (bf16[128,1024]{1,0:T(8,128)(2,1)S(1)}, bf16[64,4096]{1,0:T(8,128)(2,1)S(1)}, bf16[64,4096]{1,0:T(8,128)(2,1)}) custom-call(s32[1]{0:T(128)} %bitcast.me_ref, s32[7,8]{1,0:T(8,128)S(1)} %copy-done.20, f32[128,1024]{1,0:T(8,128)} %copy-done.2, bf16[128,1024]{1,0:T(8,128)(2,1)S(1)} %collective-permute-done.15.refs_0_, ...), custom_call_target="tpu_custom_call" | custom-call | flops 1073741824 | bytes 8388608 | tf_op jit(solution)/shard_map/mix_phase/pallas_call | solution.py:254
  43.0 0.1 collective-permute-start.19
  43.0 0.4 collective-permute-start.23
  43.4 0.8 add_phase.10
  44.2 3.3 %collective-permute-start.26 = (bf16[32,4096]{1,0:T(8,128)(2,1)}, bf16[32,4096]{1,0:T(8,128)(2,1)S(1)}, u32[]{:S(2)}, u32[]{:S(2)}) collective-permute-start(bf16[32,4096]{1,0:T(8,128)(2,1)} %get-tuple-element.91.refs_1_), channel_id=1, source_target_pairs={{0,12},{1,13},{2,14},{3,15},{4,8},{5,9},{6,10},{7,11},{8,4},{9,5},... | collective-permute-start | bytes 786440 | tf_op jit(solution)/shard_map/ppermute | solution.py:32
  47.5 0.8 add_phase.11
  48.3 1.6 %collective-permute-start.22 = (bf16[32,4096]{1,0:T(8,128)(2,1)}, bf16[32,4096]{1,0:T(8,128)(2,1)S(1)}, u32[]{:S(2)}, u32[]{:S(2)}) collective-permute-start(bf16[32,4096]{1,0:T(8,128)(2,1)} %get-tuple-element.93), channel_id=1, source_target_pairs={{0,2},{1,3},{2,0},{3,1},{4,6},{5,7},{6,4},{7,5},{8,10},{9,11},{10,... | collective-permute-start | bytes 786440 | tf_op jit(solution)/shard_map/ppermute | solution.py:32
  49.9 8.0 %collective-permute-done.23.b = bf16[64,4096]{1,0:T(8,128)(2,1)S(1)} collective-permute-done((bf16[64,4096]{1,0:T(8,128)(2,1)S(1)}, bf16[64,4096]{1,0:T(8,128)(2,1)S(1)}, u32[]{:S(2)}, u32[]{:S(2)}) %collective-permute-start.23) | collective-permute-done | bytes 524320 | tf_op jit(solution)/shard_map/ppermute | solution.py:32
  57.8 0.8 add_phase.12
  58.6 1.4 %collective-permute-start.24 = (bf16[32,4096]{1,0:T(8,128)(2,1)}, bf16[32,4096]{1,0:T(8,128)(2,1)S(1)}, u32[]{:S(2)}, u32[]{:S(2)}) collective-permute-start(bf16[32,4096]{1,0:T(8,128)(2,1)} %get-tuple-element.96), channel_id=1, source_target_pairs={{0,4},{1,5},{2,6},{3,7},{4,0},{5,1},{6,2},{7,3},{8,12},{9,13},{10,... | collective-permute-start | bytes 786440 | tf_op jit(solution)/shard_map/ppermute | solution.py:32
  60.1 1.5 %collective-permute-start.14 = (f32[8,128]{1,0:T(8,128)S(1)}, f32[8,128]{1,0:T(8,128)}, u32[]{:S(2)}, u32[]{:S(2)}) collective-permute-start(f32[8,128]{1,0:T(8,128)S(1)} %get-tuple-element.82.refs_0_), channel_id=1, source_target_pairs={{0,16},{16,0},{1,17},{17,1},{2,18},{18,2},{3,19},{19,3},{4,20},{20... | collective-permute-start | bytes 12296 | tf_op jit(solution)/shard_map/ppermute | solution.py:857
  61.5 1.5 %collective-permute-done.22.b = bf16[32,4096]{1,0:T(8,128)(2,1)S(1)} collective-permute-done((bf16[32,4096]{1,0:T(8,128)(2,1)}, bf16[32,4096]{1,0:T(8,128)(2,1)S(1)}, u32[]{:S(2)}, u32[]{:S(2)}) %collective-permute-start.22) | collective-permute-done | bytes 262176 | tf_op jit(solution)/shard_map/ppermute | solution.py:32
  63.0 7.7 %collective-permute-done.25.refs_1_.refs_6_ = bf16[32,4096]{1,0:T(8,128)(2,1)S(1)} collective-permute-done((bf16[32,4096]{1,0:T(8,128)(2,1)S(1)}, bf16[32,4096]{1,0:T(8,128)(2,1)S(1)}, u32[]{:S(2)}, u32[]{:S(2)}) %collective-permute-start.25) | collective-permute-done | bytes 262176 | tf_op jit(solution)/shard_map/ppermute | solution.py:32
  70.7 1.1 collective-permute-done.24.refs_0_.refs_5_
  71.9 0.9 copy-done.19
  72.8 0.7 add_phase.13
  73.5 3.8 %collective-permute-start.28 = (bf16[8,4096]{1,0:T(8,128)(2,1)S(1)}, bf16[8,4096]{1,0:T(8,128)(2,1)S(1)}, u32[]{:S(2)}, u32[]{:S(2)}) collective-permute-start(bf16[8,4096]{1,0:T(8,128)(2,1)S(1)} %get-tuple-element.99), channel_id=1, source_target_pairs={{0,8},{1,9},{2,10},{3,11},{4,12},{5,13},{6,14},{7,15},{8,0},{9,1},... | collective-permute-start | bytes 196616 | tf_op jit(solution)/shard_map/ppermute | solution.py:32
  77.2 0.6 collective-permute-start.29
  77.9 0.8 copy.20.refs_12_
  78.7 0.7 add.18
  79.3 0.5 slice.3
  80.5 2.9 %collective-permute-done.29.refs_3_ = bf16[8,4096]{1,0:T(8,128)(2,1)} collective-permute-done((bf16[8,4096]{1,0:T(8,128)(2,1)S(1)}, bf16[8,4096]{1,0:T(8,128)(2,1)}, u32[]{:S(2)}, u32[]{:S(2)}) %collective-permute-start.29) | collective-permute-done | bytes 65568 | tf_op jit(solution)/shard_map/ppermute | solution.py:32
  83.4 2.3 %token_phase.1 = bf16[8,4224]{1,0:T(8,128)(2,1)S(1)} custom-call(s32[1]{0:T(128)} %bitcast.me_ref, bf16[8,4096]{1,0:T(8,128)(2,1)} %get-tuple-element.97.refs_0_, bf16[8,4096]{1,0:T(8,128)(2,1)S(1)} %collective-permute-done.27.refs_1_, bf16[8,4096]{1,0:T(8,128)(2,1)S(1)} %collective-permute-done.28.refs_2_, bf16[8,4096]{1,0:T(8,128)(2,1)} %collective-permute-done.29.refs_3_, ...), custom_call_target="tpu_custom_call" | custom-call | tf_op jit(solution)/shard_map/token_phase/pallas_call | solution.py:611
  85.8 0.2 conditional.1
  86.0 0.9 collective-permute-start.32
  86.8 3.6 %collective-permute-start.30 = (bf16[8,4224]{1,0:T(8,128)(2,1)S(1)}, bf16[8,4224]{1,0:T(8,128)(2,1)S(1)}, u32[]{:S(2)}, u32[]{:S(2)}) collective-permute-start(bf16[8,4224]{1,0:T(8,128)(2,1)S(1)} %get-tuple-element.144), channel_id=1, source_target_pairs={{0,4},{1,5},{2,6},{3,7},{4,0},{5,1},{6,2},{7,3},{8,12},{9,13},{10,... | collective-permute-start | bytes 202760 | tf_op jit(solution)/shard_map/ppermute | solution.py:32
  90.4 1.8 %collective-permute-done.32 = bf16[8,4224]{1,0:T(8,128)(2,1)S(1)} collective-permute-done((bf16[8,4224]{1,0:T(8,128)(2,1)S(1)}, bf16[8,4224]{1,0:T(8,128)(2,1)S(1)}, u32[]{:S(2)}, u32[]{:S(2)}) %collective-permute-start.32) | collective-permute-done | bytes 67616 | tf_op jit(solution)/shard_map/ppermute | solution.py:32
  92.2 1.2 collective-permute-done.31
  93.5 0.5 collective-permute-start.33
  94.1 6.0 %collective-permute-done.33 = bf16[32,4224]{1,0:T(8,128)(2,1)S(1)} collective-permute-done((bf16[32,4224]{1,0:T(8,128)(2,1)S(1)}, bf16[32,4224]{1,0:T(8,128)(2,1)S(1)}, u32[]{:S(2)}, u32[]{:S(2)}) %collective-permute-start.33) | collective-permute-done | bytes 270368 | tf_op jit(solution)/shard_map/ppermute | solution.py:32
  100.1 0.1 collective-permute-start.34
  100.1 1.9 %collective-permute-done.34 = bf16[64,4224]{1,0:T(8,128)(2,1)S(1)} collective-permute-done((bf16[64,4224]{1,0:T(8,128)(2,1)S(1)}, bf16[64,4224]{1,0:T(8,128)(2,1)S(1)}, u32[]{:S(2)}, u32[]{:S(2)}) %collective-permute-start.34) | collective-permute-done | bytes 540704 | tf_op jit(solution)/shard_map/ppermute | solution.py:32
  102.1 0.0 copy-start.3
  102.1 1.0 copy-done.3
  103.1 7.9 %mixed_grad_phase.1 = (f32[1,1]{1,0:T(1,128)}, bf16[128,1024]{1,0:T(8,128)(2,1)S(1)}, bf16[128,1024]{1,0:T(8,128)(2,1)S(1)}, bf16[128,1024]{1,0:T(8,128)(2,1)S(1...) custom-call(s32[1]{0:T(128)} %bitcast.me_ref, s32[7,8]{1,0:T(8,128)S(1)} %copy-done.20, ...), custom_call_target="tpu_custom_call" | custom-call | flops 1073741824 | bytes 8388608 | tf_op jit(solution)/shard_map/mixed_grad_phase/pallas_call | solution.py:671
  111.1 0.2 collective-permute-start.35
  111.3 0.5 collective-permute-start.36
  111.7 1.2 collective-permute-start.37
  113.0 0.9 collective-permute-start.38
  113.9 0.0 copy-start.4
  113.9 5.5 %block_grad_phase.1 = (f32[8,128,128]{2,1,0:T(8,128)}, f32[7,8,128,128]{3,2,1,0:T(8,128)}, f32[128,1024]{1,0:T(8,128)S(1)}) custom-call(s32[7,8]{1,0:T(8,128)S(1)} %copy-done.20, bf16[128,1024]{1,0:T(8,128)(2,1)S(1)} %copy-done.15, bf16[128,1024]{1,0:T(8,128)(2,1)S(1)} %get-tuple-element.105.mg, bf16[128,1024]{1,0:T(8,128)(2,1)S(1)} %copy-done.11, ...), custom_call_target="tpu_custom_call" | custom-call | flops 402653184 | bytes 12582912 | tf_op jit(solution)/shard_map/block_grad_phase/pallas_call | solution.py:716
  119.3 6.5 %down_grad_phase.1 = f32[1024,4096]{1,0:T(8,128)} custom-call(bf16[128,1024]{1,0:T(8,128)(2,1)S(1)} %get-tuple-element.111.mixed_ref, bf16[128,4224]{1,0:T(8,128)(2,1)S(1)} %copy-done.4), custom_call_target="tpu_custom_call" | custom-call | flops 1073741824 | bytes 16777216 | tf_op jit(solution)/shard_map/down_grad_phase/pallas_call | solution.py:758
  125.8 1.7 %collective-permute-done.38.refs_3_ = bf16[128,1024]{1,0:T(8,128)(2,1)S(1)} collective-permute-done((bf16[128,1024]{1,0:T(8,128)(2,1)S(1)}, bf16[128,1024]{1,0:T(8,128)(2,1)S(1)}, u32[]{:S(2)}, u32[]{:S(2)}) %collective-permute-start.38) | collective-permute-done | bytes 262176 | tf_op jit(solution)/shard_map/ppermute | solution.py:32
  127.5 6.7 %up_grad_phase.1 = f32[4096,1024]{1,0:T(8,128)} custom-call(bf16[128,4096]{1,0:T(8,128)(2,1)S(1)} %copy-done.5, f32[128,1024]{1,0:T(8,128)S(1)} %copy-done.17, f32[128,1024]{1,0:T(8,128)S(1)} %get-tuple-element.106.grad_ref, bf16[128,1024]{1,0:T(8,128)(2,1)S(1)} %collective-permute-done.35.refs_0_, bf16[128,1024]{1,0:T(8,128)(2,1)S(1)} %collective-permute-done.36.refs_1_, ...), custom_call_target="tpu_custom_call" | custom-call | flops 1073741824 | bytes 16777216 | tf_op jit(solution)/shard_map/up_grad_phase/pallas_call | solution.py:802
  (66 shorter events, 0.3 us)
Async XLA Ops:
  1.4 10.9 %copy-start.28 = (s32[32,8]{0,1:T(8,128)S(1)}, s32[32,8]{0,1:T(8,128)}, u32[]{:S(2)}) copy-start(s32[32,8]{0,1:T(8,128)} %param.16) | copy-start | bytes 3076
  1.4 11.0 %copy-start.5 = (bf16[128,4096]{1,0:T(8,128)(2,1)S(1)}, bf16[128,4096]{1,0:T(8,128)(2,1)}, u32[]{:S(2)}) copy-start(bf16[128,4096]{1,0:T(8,128)(2,1)} %tok.3) | copy-start | bytes 3145732
  10.6 1.3 copy-start.6
  11.9 15.0 %collective-permute-start.20 = (bf16[256,4096]{1,0:T(8,128)(2,1)}, bf16[256,4096]{1,0:T(8,128)(2,1)}, u32[]{:S(2)}, u32[]{:S(2)}) collective-permute-start(bf16[256,4096]{1,0:T(8,128)(2,1)} %get-tuple-element.87), channel_id=1, source_target_pairs={{0,1},{1,0},{2,3},{3,2},{4,5},{5,4},{6,7},{7,6},{8,9},{9,8},{10,11... | collective-permute-start | bytes 6291464 | tf_op jit(solution)/shard_map/ppermute | solution.py:32
  12.4 11.6 %copy-start = (bf16[7,8,128,128]{3,2,1,0:T(8,128)(2,1)S(1)}, bf16[7,8,128,128]{3,2,1,0:T(8,128)(2,1)}, u32[]{:S(2)}) copy-start(bf16[7,8,128,128]{3,2,1,0:T(8,128)(2,1)} %refs_5_.3) | copy-start | bytes 5505028
  12.4 11.6 %copy-start.12 = (bf16[8,128,128]{2,1,0:T(8,128)(2,1)S(1)}, bf16[8,128,128]{2,1,0:T(8,128)(2,1)}, u32[]{:S(2)}) copy-start(bf16[8,128,128]{2,1,0:T(8,128)(2,1)} %refs_4_.3) | copy-start | bytes 786436
  12.4 11.6 %copy-start.20 = (s32[7,8]{1,0:T(8,128)S(1)}, s32[7,8]{1,0:T(8,128)}, u32[]{:S(2)}) copy-start(s32[7,8]{1,0:T(8,128)} %pat.7) | copy-start | bytes 676
  16.6 0.8 copy-start.16
  17.4 7.7 %copy-start.14 = (bf16[128,1024]{1,0:T(8,128)(2,1)}, bf16[128,1024]{1,0:T(8,128)(2,1)S(1)}, u32[]{:S(2)}) copy-start(bf16[128,1024]{1,0:T(8,128)(2,1)S(1)} %get-tuple-element.83.act_ref) | copy-start | bytes 786436
  17.4 9.5 %copy-start.7 = (bf16[256,4096]{1,0:T(8,128)(2,1)S(1)}, bf16[256,4096]{1,0:T(8,128)(2,1)}, u32[]{:S(2)}) copy-start(bf16[256,4096]{1,0:T(8,128)(2,1)} %copy-done.6) | copy-start | bytes 6291460
  17.4 9.5 %collective-permute-start.16 = (bf16[128,1024]{1,0:T(8,128)(2,1)S(1)}, bf16[128,1024]{1,0:T(8,128)(2,1)S(1)}, u32[]{:S(2)}, u32[]{:S(2)}) collective-permute-start(bf16[128,1024]{1,0:T(8,128)(2,1)S(1)} %get-tuple-element.83.act_ref), channel_id=1, source_target_pairs={{0,2},{1,3},{2,0},{3,1},{4,6},{5,7},{6,4},{7,5},{8,10},{9,11},{10,... | collective-permute-start | bytes 786440 | tf_op jit(solution)/shard_map/ppermute | solution.py:32
  19.9 15.1 %collective-permute-start.18 = (bf16[128,1024]{1,0:T(8,128)(2,1)S(1)}, bf16[128,1024]{1,0:T(8,128)(2,1)S(1)}, u32[]{:S(2)}, u32[]{:S(2)}) collective-permute-start(bf16[128,1024]{1,0:T(8,128)(2,1)S(1)} %get-tuple-element.83.act_ref), channel_id=1, source_target_pairs={{0,8},{1,9},{2,10},{3,11},{4,12},{5,13},{6,14},{7,15},{8,0},{9,1},... | collective-permute-start | bytes 786440 | tf_op jit(solution)/shard_map/ppermute | solution.py:32
  22.5 12.7 %collective-permute-start.17 = (bf16[128,1024]{1,0:T(8,128)(2,1)S(1)}, bf16[128,1024]{1,0:T(8,128)(2,1)S(1)}, u32[]{:S(2)}, u32[]{:S(2)}) collective-permute-start(bf16[128,1024]{1,0:T(8,128)(2,1)S(1)} %get-tuple-element.83.act_ref), channel_id=1, source_target_pairs={{0,4},{1,5},{2,6},{3,7},{4,0},{5,1},{6,2},{7,3},{8,12},{9,13},{10,... | collective-permute-start | bytes 786440 | tf_op jit(solution)/shard_map/ppermute | solution.py:32
  24.0 11.2 %collective-permute-start.15 = (bf16[128,1024]{1,0:T(8,128)(2,1)S(1)}, bf16[128,1024]{1,0:T(8,128)(2,1)S(1)}, u32[]{:S(2)}, u32[]{:S(2)}) collective-permute-start(bf16[128,1024]{1,0:T(8,128)(2,1)S(1)} %get-tuple-element.83.act_ref), channel_id=1, source_target_pairs={{0,1},{1,0},{2,3},{3,2},{4,5},{5,4},{6,7},{7,6},{8,9},{9,8},{10,11... | collective-permute-start | bytes 786440 | tf_op jit(solution)/shard_map/ppermute | solution.py:32
  25.1 4.1 %copy-start.2 = (f32[128,1024]{1,0:T(8,128)}, f32[128,1024]{1,0:T(8,128)S(1)}, u32[]{:S(2)}) copy-start(f32[128,1024]{1,0:T(8,128)S(1)} %own_mix_phase.1.own_ref.refs_0_) | copy-start | bytes 1572868
  26.9 8.3 %copy-start.21 = (s32[8,32]{1,0:T(8,128)S(1)}, s32[8,32]{1,0:T(8,128)}, u32[]{:S(2)}) copy-start(s32[8,32]{1,0:T(8,128)} %sc.2) | copy-start | bytes 3076
  29.2 14.3 %collective-permute-start.21 = (bf16[64,4096]{1,0:T(8,128)(2,1)S(1)}, bf16[64,4096]{1,0:T(8,128)(2,1)S(1)}, u32[]{:S(2)}, u32[]{:S(2)}) collective-permute-start(bf16[64,4096]{1,0:T(8,128)(2,1)S(1)} %get-tuple-element.89), channel_id=1, source_target_pairs={{0,2},{1,3},{2,0},{3,1},{4,6},{5,7},{6,4},{7,5},{8,10},{9,11},{10,... | collective-permute-start | bytes 1572872 | tf_op jit(solution)/shard_map/ppermute | solution.py:32
  35.1 7.8 %copy-start.8 = (bf16[128,1024]{1,0:T(8,128)(2,1)}, bf16[128,1024]{1,0:T(8,128)(2,1)S(1)}, u32[]{:S(2)}) copy-start(bf16[128,1024]{1,0:T(8,128)(2,1)S(1)} %collective-permute-done.17.refs_2_) | copy-start | bytes 786436
  35.2 7.8 %copy-start.10 = (bf16[128,1024]{1,0:T(8,128)(2,1)}, bf16[128,1024]{1,0:T(8,128)(2,1)S(1)}, u32[]{:S(2)}) copy-start(bf16[128,1024]{1,0:T(8,128)(2,1)S(1)} %collective-permute-done.15.refs_0_) | copy-start | bytes 786436
  43.0 4.6 %collective-permute-start.19 = (bf16[64,4096]{1,0:T(8,128)(2,1)}, bf16[64,4096]{1,0:T(8,128)(2,1)S(1)}, u32[]{:S(2)}, u32[]{:S(2)}) collective-permute-start(bf16[64,4096]{1,0:T(8,128)(2,1)} %get-tuple-element.85), channel_id=1, source_target_pairs={{0,1},{1,0},{2,3},{3,2},{4,5},{5,4},{6,7},{7,6},{8,9},{9,8},{10,11... | collective-permute-start | bytes 1572872 | tf_op jit(solution)/shard_map/ppermute | solution.py:32
  43.0 14.8 %collective-permute-start.23 = (bf16[64,4096]{1,0:T(8,128)(2,1)S(1)}, bf16[64,4096]{1,0:T(8,128)(2,1)S(1)}, u32[]{:S(2)}, u32[]{:S(2)}) collective-permute-start(bf16[64,4096]{1,0:T(8,128)(2,1)S(1)} %get-tuple-element.95), channel_id=1, source_target_pairs={{0,2},{1,3},{2,0},{3,1},{4,6},{5,7},{6,4},{7,5},{8,10},{9,11},{10,... | collective-permute-start | bytes 1572872 | tf_op jit(solution)/shard_map/ppermute | solution.py:32
  44.2 18.8 %collective-permute-start.26 = (bf16[32,4096]{1,0:T(8,128)(2,1)}, bf16[32,4096]{1,0:T(8,128)(2,1)S(1)}, u32[]{:S(2)}, u32[]{:S(2)}) collective-permute-start(bf16[32,4096]{1,0:T(8,128)(2,1)} %get-tuple-element.91.refs_1_), channel_id=1, source_target_pairs={{0,12},{1,13},{2,14},{3,15},{4,8},{5,9},{6,10},{7,11},{8,4},{9,5},... | collective-permute-start | bytes 786440 | tf_op jit(solution)/shard_map/ppermute | solution.py:32
  47.5 23.2 %collective-permute-start.25 = (bf16[32,4096]{1,0:T(8,128)(2,1)S(1)}, bf16[32,4096]{1,0:T(8,128)(2,1)S(1)}, u32[]{:S(2)}, u32[]{:S(2)}) collective-permute-start(bf16[32,4096]{1,0:T(8,128)(2,1)S(1)} %get-tuple-element.90.refs_0_), channel_id=1, source_target_pairs={{0,8},{1,9},{2,10},{3,11},{4,12},{5,13},{6,14},{7,15},{8,0},{9,1},... | collective-permute-start | bytes 786440 | tf_op jit(solution)/shard_map/ppermute | solution.py:32
  48.3 10.3 %copy-start.18 = (bf16[32,4096]{1,0:T(8,128)(2,1)}, bf16[32,4096]{1,0:T(8,128)(2,1)S(1)}, u32[]{:S(2)}) copy-start(bf16[32,4096]{1,0:T(8,128)(2,1)S(1)} %get-tuple-element.92.a) | copy-start | bytes 786436
  48.3 14.7 %collective-permute-start.22 = (bf16[32,4096]{1,0:T(8,128)(2,1)}, bf16[32,4096]{1,0:T(8,128)(2,1)S(1)}, u32[]{:S(2)}, u32[]{:S(2)}) collective-permute-start(bf16[32,4096]{1,0:T(8,128)(2,1)} %get-tuple-element.93), channel_id=1, source_target_pairs={{0,2},{1,3},{2,0},{3,1},{4,6},{5,7},{6,4},{7,5},{8,10},{9,11},{10,... | collective-permute-start | bytes 786440 | tf_op jit(solution)/shard_map/ppermute | solution.py:32
  58.6 13.2 %collective-permute-start.24 = (bf16[32,4096]{1,0:T(8,128)(2,1)}, bf16[32,4096]{1,0:T(8,128)(2,1)S(1)}, u32[]{:S(2)}, u32[]{:S(2)}) collective-permute-start(bf16[32,4096]{1,0:T(8,128)(2,1)} %get-tuple-element.96), channel_id=1, source_target_pairs={{0,4},{1,5},{2,6},{3,7},{4,0},{5,1},{6,2},{7,3},{8,12},{9,13},{10,... | collective-permute-start | bytes 786440 | tf_op jit(solution)/shard_map/ppermute | solution.py:32
  60.1 18.6 %collective-permute-start.14 = (f32[8,128]{1,0:T(8,128)S(1)}, f32[8,128]{1,0:T(8,128)}, u32[]{:S(2)}, u32[]{:S(2)}) collective-permute-start(f32[8,128]{1,0:T(8,128)S(1)} %get-tuple-element.82.refs_0_), channel_id=1, source_target_pairs={{0,16},{16,0},{1,17},{17,1},{2,18},{18,2},{3,19},{19,3},{4,20},{20... | collective-permute-start | bytes 12296 | tf_op jit(solution)/shard_map/ppermute | solution.py:857
  71.9 1.0 copy-start.19
  73.5 12.3 %copy-start.22 = (bf16[8,4096]{1,0:T(8,128)(2,1)S(1)}, bf16[8,4096]{1,0:T(8,128)(2,1)}, u32[]{:S(2)}) copy-start(bf16[8,4096]{1,0:T(8,128)(2,1)} %get-tuple-element.97.refs_0_) | copy-start | bytes 196612
  73.5 12.3 %copy-start.26 = (s32[128,8]{0,1:T(8,128)S(1)}, s32[128,8]{0,1:T(8,128)}, u32[]{:S(2)}) copy-start(s32[128,8]{0,1:T(8,128)} %param.24) | copy-start | bytes 12292
  73.5 7.0 %collective-permute-start.27 = (bf16[8,4096]{1,0:T(8,128)(2,1)S(1)}, bf16[8,4096]{1,0:T(8,128)(2,1)S(1)}, u32[]{:S(2)}, u32[]{:S(2)}) collective-permute-start(bf16[8,4096]{1,0:T(8,128)(2,1)S(1)} %get-tuple-element.98), channel_id=1, source_target_pairs={{0,4},{1,5},{2,6},{3,7},{4,0},{5,1},{6,2},{7,3},{8,12},{9,13},{10,... | collective-permute-start | bytes 196616 | tf_op jit(solution)/shard_map/ppermute | solution.py:32
  73.5 7.1 %collective-permute-start.28 = (bf16[8,4096]{1,0:T(8,128)(2,1)S(1)}, bf16[8,4096]{1,0:T(8,128)(2,1)S(1)}, u32[]{:S(2)}, u32[]{:S(2)}) collective-permute-start(bf16[8,4096]{1,0:T(8,128)(2,1)S(1)} %get-tuple-element.99), channel_id=1, source_target_pairs={{0,8},{1,9},{2,10},{3,11},{4,12},{5,13},{6,14},{7,15},{8,0},{9,1},... | collective-permute-start | bytes 196616 | tf_op jit(solution)/shard_map/ppermute | solution.py:32
  77.2 6.2 %collective-permute-start.29 = (bf16[8,4096]{1,0:T(8,128)(2,1)S(1)}, bf16[8,4096]{1,0:T(8,128)(2,1)}, u32[]{:S(2)}, u32[]{:S(2)}) collective-permute-start(bf16[8,4096]{1,0:T(8,128)(2,1)S(1)} %get-tuple-element.100), channel_id=1, source_target_pairs={{0,12},{1,13},{2,14},{3,15},{4,8},{5,9},{6,10},{7,11},{8,4},{9,5},... | collective-permute-start | bytes 196616 | tf_op jit(solution)/shard_map/ppermute | solution.py:32
  80.5 5.2 %copy-start.23 = (f32[4096]{0:T(1024)S(1)}, f32[4096]{0:T(1024)}, u32[]{:S(2)}) copy-start(f32[4096]{0:T(1024)} %param.22) | copy-start | bytes 49156
  86.0 6.3 %collective-permute-start.32 = (bf16[8,4224]{1,0:T(8,128)(2,1)S(1)}, bf16[8,4224]{1,0:T(8,128)(2,1)S(1)}, u32[]{:S(2)}, u32[]{:S(2)}) collective-permute-start(bf16[8,4224]{1,0:T(8,128)(2,1)S(1)} %get-tuple-element.144), channel_id=1, source_target_pairs={{0,12},{1,13},{2,14},{3,15},{4,8},{5,9},{6,10},{7,11},{8,4},{9,5},... | collective-permute-start | bytes 202760 | tf_op jit(solution)/shard_map/ppermute | solution.py:32
  86.8 6.6 %collective-permute-start.31 = (bf16[8,4224]{1,0:T(8,128)(2,1)S(1)}, bf16[8,4224]{1,0:T(8,128)(2,1)S(1)}, u32[]{:S(2)}, u32[]{:S(2)}) collective-permute-start(bf16[8,4224]{1,0:T(8,128)(2,1)S(1)} %get-tuple-element.144), channel_id=1, source_target_pairs={{0,8},{1,9},{2,10},{3,11},{4,12},{5,13},{6,14},{7,15},{8,0},{9,1},... | collective-permute-start | bytes 202760 | tf_op jit(solution)/shard_map/ppermute | solution.py:32
  86.8 6.6 %collective-permute-start.30 = (bf16[8,4224]{1,0:T(8,128)(2,1)S(1)}, bf16[8,4224]{1,0:T(8,128)(2,1)S(1)}, u32[]{:S(2)}, u32[]{:S(2)}) collective-permute-start(bf16[8,4224]{1,0:T(8,128)(2,1)S(1)} %get-tuple-element.144), channel_id=1, source_target_pairs={{0,4},{1,5},{2,6},{3,7},{4,0},{5,1},{6,2},{7,3},{8,12},{9,13},{10,... | collective-permute-start | bytes 202760 | tf_op jit(solution)/shard_map/ppermute | solution.py:32
  93.5 6.5 %collective-permute-start.33 = (bf16[32,4224]{1,0:T(8,128)(2,1)S(1)}, bf16[32,4224]{1,0:T(8,128)(2,1)S(1)}, u32[]{:S(2)}, u32[]{:S(2)}) collective-permute-start(bf16[32,4224]{1,0:T(8,128)(2,1)S(1)} %pad_maximum_fusion.1), channel_id=1, source_target_pairs={{0,2},{1,3},{2,0},{3,1},{4,6},{5,7},{6,4},{7,5},{8,10},{9,11},{10,... | collective-permute-start | bytes 811016 | tf_op jit(solution)/shard_map/ppermute | solution.py:32
  100.1 2.0 %collective-permute-start.34 = (bf16[64,4224]{1,0:T(8,128)(2,1)S(1)}, bf16[64,4224]{1,0:T(8,128)(2,1)S(1)}, u32[]{:S(2)}, u32[]{:S(2)}) collective-permute-start(bf16[64,4224]{1,0:T(8,128)(2,1)S(1)} %get-tuple-element.134), channel_id=1, source_target_pairs={{0,1},{1,0},{2,3},{3,2},{4,5},{5,4},{6,7},{7,6},{8,9},{9,8},{10,11... | collective-permute-start | bytes 1622024 | tf_op jit(solution)/shard_map/ppermute | solution.py:32
  102.1 1.0 copy-start.3
  103.1 10.8 %copy-start.1 = (bf16[7,8,128,128]{3,2,1,0:T(8,128)(2,1)S(1)}, bf16[7,8,128,128]{3,2,1,0:T(8,128)(2,1)}, u32[]{:S(2)}) copy-start(bf16[7,8,128,128]{3,2,1,0:T(8,128)(2,1)} %refs_5_.3) | copy-start | bytes 5505028
  103.1 10.8 %copy-start.9 = (bf16[128,1024]{1,0:T(8,128)(2,1)S(1)}, bf16[128,1024]{1,0:T(8,128)(2,1)}, u32[]{:S(2)}) copy-start(bf16[128,1024]{1,0:T(8,128)(2,1)} %copy-done.8) | copy-start | bytes 786436
  103.1 10.8 %copy-start.11 = (bf16[128,1024]{1,0:T(8,128)(2,1)S(1)}, bf16[128,1024]{1,0:T(8,128)(2,1)}, u32[]{:S(2)}) copy-start(bf16[128,1024]{1,0:T(8,128)(2,1)} %copy-done.10) | copy-start | bytes 786436
  103.1 10.8 %copy-start.13 = (bf16[8,128,128]{2,1,0:T(8,128)(2,1)S(1)}, bf16[8,128,128]{2,1,0:T(8,128)(2,1)}, u32[]{:S(2)}) copy-start(bf16[8,128,128]{2,1,0:T(8,128)(2,1)} %refs_4_.3) | copy-start | bytes 786436
  103.1 10.8 %copy-start.15 = (bf16[128,1024]{1,0:T(8,128)(2,1)S(1)}, bf16[128,1024]{1,0:T(8,128)(2,1)}, u32[]{:S(2)}) copy-start(bf16[128,1024]{1,0:T(8,128)(2,1)} %copy-done.14) | copy-start | bytes 786436
  111.1 14.8 %collective-permute-start.35 = (bf16[128,1024]{1,0:T(8,128)(2,1)S(1)}, bf16[128,1024]{1,0:T(8,128)(2,1)S(1)}, u32[]{:S(2)}, u32[]{:S(2)}) collective-permute-start(bf16[128,1024]{1,0:T(8,128)(2,1)S(1)} %get-tuple-element.107), channel_id=1, source_target_pairs={{0,1},{1,0},{2,3},{3,2},{4,5},{5,4},{6,7},{7,6},{8,9},{9,8},{10,11... | collective-permute-start | bytes 786440 | tf_op jit(solution)/shard_map/ppermute | solution.py:32
  111.3 14.6 %collective-permute-start.36 = (bf16[128,1024]{1,0:T(8,128)(2,1)S(1)}, bf16[128,1024]{1,0:T(8,128)(2,1)S(1)}, u32[]{:S(2)}, u32[]{:S(2)}) collective-permute-start(bf16[128,1024]{1,0:T(8,128)(2,1)S(1)} %get-tuple-element.108), channel_id=1, source_target_pairs={{0,2},{1,3},{2,0},{3,1},{4,6},{5,7},{6,4},{7,5},{8,10},{9,11},{10,... | collective-permute-start | bytes 786440 | tf_op jit(solution)/shard_map/ppermute | solution.py:32
  111.7 14.1 %collective-permute-start.37 = (bf16[128,1024]{1,0:T(8,128)(2,1)S(1)}, bf16[128,1024]{1,0:T(8,128)(2,1)S(1)}, u32[]{:S(2)}, u32[]{:S(2)}) collective-permute-start(bf16[128,1024]{1,0:T(8,128)(2,1)S(1)} %get-tuple-element.109), channel_id=1, source_target_pairs={{0,4},{1,5},{2,6},{3,7},{4,0},{5,1},{6,2},{7,3},{8,12},{9,13},{10,... | collective-permute-start | bytes 786440 | tf_op jit(solution)/shard_map/ppermute | solution.py:32
  113.0 14.6 %collective-permute-start.38 = (bf16[128,1024]{1,0:T(8,128)(2,1)S(1)}, bf16[128,1024]{1,0:T(8,128)(2,1)S(1)}, u32[]{:S(2)}, u32[]{:S(2)}) collective-permute-start(bf16[128,1024]{1,0:T(8,128)(2,1)S(1)} %get-tuple-element.110), channel_id=1, source_target_pairs={{0,8},{1,9},{2,10},{3,11},{4,12},{5,13},{6,14},{7,15},{8,0},{9,1},... | collective-permute-start | bytes 786440 | tf_op jit(solution)/shard_map/ppermute | solution.py:32
  113.9 5.5 %copy-start.4 = (bf16[128,4224]{1,0:T(8,128)(2,1)S(1)}, bf16[128,4224]{1,0:T(8,128)(2,1)}, u32[]{:S(2)}) copy-start(bf16[128,4224]{1,0:T(8,128)(2,1)} %copy-done.3) | copy-start | bytes 3244036
  119.3 8.2 %copy-start.17 = (f32[128,1024]{1,0:T(8,128)S(1)}, f32[128,1024]{1,0:T(8,128)}, u32[]{:S(2)}) copy-start(f32[128,1024]{1,0:T(8,128)} %copy-done.16) | copy-start | bytes 1572868

commit v4 on v3

--- a/solution.py
+++ b/solution.py
@@ -154,7 +154,7 @@
             pltpu.VMEM((steps, chunk, hidden), BF16),
             pltpu.SemaphoreType.DMA((steps,)),
         ],
-        compiler_params=params(52),
+        compiler_params=params(48),
         cost_estimate=cost(2 * token_count * depth * hidden, depth * hidden * 2),
         name="up_phase",
     )(tokens, values, scale, *after)
@@ -262,27 +262,28 @@
             pltpu.VMEM((steps, hidden, chunk), BF16),
             pltpu.SemaphoreType.DMA((steps,)),
         ],
-        compiler_params=params(52),
+        compiler_params=params(50),
         cost_estimate=cost(2 * token_count * features * hidden, features * hidden * 2),
         name="mix_phase",
     )(me, pattern, own, *received, partner, down, scale, *after)
 
 
-def add_phase(keep, received, parts, after):
+def add_phase(keep, received, parts, after, wanted=None):
+    wanted = range(parts) if wanted is None else wanted
     rows, features = keep.shape
     rows //= parts
 
     def kernel(a, b, *refs):
         outs = refs[len(after) :]
-        for n, out in enumerate(outs):
+        for n, out in zip(wanted, outs):
             here = slice(n * rows, (n + 1) * rows)
             out[...] = (a[here, :].astype(F32) + b[here, :].astype(F32)).astype(BF16)
 
     return pl.pallas_call(
         kernel,
         in_specs=[VMEM] * 2 + [UNREAD] * len(after),
-        out_specs=[VMEM] * parts,
-        out_shape=[jax.ShapeDtypeStruct((rows, features), BF16)] * parts,
+        out_specs=[VMEM] * len(wanted),
+        out_shape=[jax.ShapeDtypeStruct((rows, features), BF16)] * len(wanted),
         compiler_params=params(),
         name="add_phase",
     )(keep, received, *after)
@@ -472,7 +473,7 @@
             fetch(c).start()
 
         mine = me_ref[0]
-        wanted = ids_ref[...]
+        wanted = ids_ref[...].T
         shard = wanted // entries
         lane = iota((token_count, wide), 1)
         sharer = jnp.full((token_count, wide), -1, jnp.int32)
@@ -506,23 +507,20 @@
         index = wanted - mine * entries + 1
         owner = iota((token_count, picks), 0) // rows
         target = slot_of(owner ^ mine, count, groups) * SLOTS + rank.astype(jnp.int32) + 1
-        source_high = jnp.zeros((HELD, 1), F32)
-        source_low = jnp.zeros((HELD, 1), F32)
-        target_high = jnp.zeros((1, HELD), F32)
-        target_low = jnp.zeros((1, HELD), F32)
-        for j in range(picks):
-            at = ones(place[:, j : j + 1] == iota((token_count, HELD), 1))
-            one = slice(j, j + 1)
-
-            def part(value):
-                return value[:, one].astype(F32).astype(BF16)
-
-            source_high += dot_tn(at, part(index >> 7))
-            source_low += dot_tn(at, part(index & 127))
-            target_high += dot_tn(part(target >> 7), at)
-            target_low += dot_tn(part(target & 127), at)
-        source = (source_high * 128 + source_low).astype(jnp.int32) - 1
-        aim = (target_high * 128 + target_low).astype(jnp.int32) - 1
+        at = jnp.concatenate(
+            [ones(place[:, j : j + 1] == iota((token_count, HELD), 1)) for j in range(picks)], 0
+        )
+        values = [index >> 7, index & 127, target >> 7, target & 127]
+        values = jnp.concatenate([v.astype(F32).astype(BF16) for v in values], 1)
+        lane = iota(values.shape, 1) % picks
+        values = jnp.concatenate(
+            [jnp.where(lane == j, values.astype(F32), 0.0).astype(BF16) for j in range(picks)], 0
+        )
+        found = dot_tn(at, values[:, : 2 * picks])
+        source = jnp.sum(found[:, :picks] * 128 + found[:, picks:], axis=1, keepdims=True)
+        source = source.astype(jnp.int32) - 1
+        aim = dot_tn(values[:, 2 * picks :], at)
+        aim = jnp.sum(aim[:picks] * 128 + aim[picks:], axis=0, keepdims=True).astype(jnp.int32) - 1
         chosen[...] = ones(source == iota((HELD, entries), 1))
         layout[...] = ones(iota((2 * half, HELD), 0) == aim)
 
@@ -554,7 +552,7 @@
         compiler_params=params(32),
         cost_estimate=cost(4 * token_count * features * entries, features * entries * 2),
         name="pick_phase",
-    )(me, ids, vocab)
+    )(me, ids.T, vocab)
 
 
 def token_phase(me, terms, own, gain, picked, ids, rank, logits, entries):
@@ -680,7 +678,7 @@
             pltpu.VMEM((blocks // pair, pair * width, features), BF16),
             pltpu.SemaphoreType.DMA((blocks // pair,)),
         ],
-        compiler_params=params(52),
+        compiler_params=params(50),
         cost_estimate=cost(2 * token_count * features * hidden, features * hidden * 2),
         name="mixed_grad_phase",
     )(me, pattern, grad, down, scale, partner)
@@ -848,9 +846,9 @@
         pre, act = up_phase(tokens, up_values, up_scale, width, [flag])
         received = [swap(act, 1 << k - local) for k in range(local, levels)]
         own_mix = own_mix_phase(pattern, act, diag_blocks, partner_blocks, local, ())
-        near, far, near_sent, far_sent = add_phase(
-            kept, swap(sent, group_masks(groups[0])[1]), 4, [own_mix, *received[1:2]]
-        )
+        given = swap(sent, group_masks(groups[0])[1])
+        (far_sent,) = add_phase(kept, given, 4, [own_mix, *received[1:2]], [3])
+        near, far, near_sent = add_phase(kept, given, 4, [far_sent], [0, 1, 2])
         parts = lax.axis_size("groups")
         turned = flag
         for _ in range(parts - 1):
@@ -863,15 +861,16 @@
         pre, act = up_phase(tokens, up_values, up_scale, width, [])
         received = [swap(act, 1 << k - local) for k in range(local, levels)]
         own_mix = own_mix_phase(pattern, act, diag_blocks, partner_blocks, local, ())
+    early = [near_sent] if sparse else []
     mixed, keep, send = mix_phase(
-        me, pattern, own_mix, received, partner_blocks, down_values, down_scale, rows, groups, []
+        me, pattern, own_mix, received, partner_blocks, down_values, down_scale, rows, groups, early
     )
     if sparse:
         masks = group_masks(groups[SHARED])
         far = add_phase(far, far_laid, len(masks) // 2, [])
         near = add_phase(near, near_laid, len(masks) // 2, far[:1])
         picked = [swap(piece, m) for piece, m in zip([*near, *far], masks)]
-        terms = reduce_rows(keep, send, groups, [far, picked[1:]])
+        terms = reduce_rows(keep, send, groups, [far, picked[2:]])
     else:
         terms = reduce_rows(keep, send, groups)
 

time: 135 us -> 128 us (0.948)
  waiting for transfers between devices: 39.7 us -> 32.5 us
  local copies, waits for them, and re-layouts: 6.44 us -> 3.07 us
  starting transfers between devices: 29.4 us -> 32.3 us
  Pallas kernels: 56.1 us -> 58 us
    ppermute x24, waiting for transfers between devices: 39.7 us -> 32.5 us  [swap(): return lax.ppermute(block, 'mp', [(i, i ^ mask) for i in range(count)])]
    pallas_call x5 -> x6, Pallas kernels: 5.25 us -> 8.74 us  [add_phase(): pl.pallas_call(kernel, in_specs=[VMEM] * 2 + [UNREAD] * len(after), out_s...]
    unnamed x59 -> x57, local copies, waits for them, and re-layouts: 5.83 us -> 2.46 us
    ppermute x24, starting transfers between devices: 27.9 us -> 30.9 us  [swap(): return lax.ppermute(block, 'mp', [(i, i ^ mask) for i in range(count)])]
  transfers between devices with their start and end apart: 25 -> 25, of which waited for: 13 -> 12; matrix products, arithmetic and copies ran while one was open for 2% -> 1% of each run, Pallas kernels for 22% -> 26%
where the time goes in v4:
time: 128 us
  Pallas kernels  58 us (45%)
  waiting for transfers between devices  32.5 us (25%)
  starting transfers between devices  32.3 us (25%)
  local copies, waits for them, and re-layouts  3.07 us (2%)
  between operations  1.82 us (1%)
    ppermute x24, waiting for transfers between devices, swap(): return lax.ppermute(block, 'mp', [(i, i ^ mask) for i in range(count)])  32.5 us
    ppermute x24, starting transfers between devices, swap(): return lax.ppermute(block, 'mp', [(i, i ^ mask) for i in range(count)])  30.9 us
    pallas_call x1, Pallas kernels, pick_phase(): pl.pallas_call(kernel, in_specs=[SMEM, VMEM, pl.BlockSpec(memory_space=pl...  9.54 us
    pallas_call x6, Pallas kernels, add_phase(): pl.pallas_call(kernel, in_specs=[VMEM] * 2 + [UNREAD] * len(after), out_s...  8.74 us
    pallas_call x1, Pallas kernels, mixed_grad_phase(): pl.pallas_call(kernel, in_specs=[SMEM, SMEM, VMEM, HBM, VMEM, VMEM], out_...  7.54 us
    pallas_call x1, Pallas kernels, mix_phase(): pl.pallas_call(kernel, in_specs=[SMEM, SMEM] + [VMEM] * (2 + crossing) +...  7.05 us
    pallas_call x1, Pallas kernels, up_grad_phase(): pl.pallas_call(kernel, in_specs=[VMEM] * (3 + len(received)), out_specs=H...  6.66 us
    pallas_call x1, Pallas kernels, down_grad_phase(): pl.pallas_call(kernel, in_specs=[VMEM] * 2, out_specs=HBM, out_shape=jax....  6.46 us
  transfers between devices with their start and end apart: 25, of which 12 were waited for; matrix products, arithmetic and copies ran while one was open for 1% of the time, Pallas kernels for 26%

profile of v4, /device:TPU:0, one launch (start us, length us, event | category | flops | bytes accessed | tf_op | source)
XLA Modules:
  0.0 128.0 jit_solution(10869421925412800992)
XLA Ops:
  0.7 9.5 %pick_phase.1 = (s32[128,8]{1,0:T(8,128)S(1)}, f32[8,128]{1,0:T(8,128)S(1)}, bf16[256,4096]{1,0:T(8,128)(2,1)S(1)}, bf16[256,4096]{1,0:T(8,128)(2,1)}) custom-call(s32[1]{0:T(128)} %bitcast.me_ref, s32[8,128]{1,0:T(8,128)} %bitcast.7, bf16[2048,4096]{1,0:T(8,128)(2,1)} %vocab_ref.1), custom_call_target="tpu_custom_call" | custom-call | flops 4294967296 | bytes 16777216 | tf_op jit(solution)/shard_map/pick_phase/pallas_call | solution.py:537
  10.2 0.0 copy-start.2
  10.2 1.3 %copy-done.2 = bf16[256,4096]{1,0:T(8,128)(2,1)} copy-done((bf16[256,4096]{1,0:T(8,128)(2,1)}, bf16[256,4096]{1,0:T(8,128)(2,1)S(1)}, u32[]{:S(2)}) %copy-start.2) | copy-done | bytes 2097176
  11.5 0.5 collective-permute-start.19
  12.0 0.1 copy.17.sc
  12.1 0.0 copy-start.19
  12.1 4.1 %up_phase.1 = (f32[128,1024]{1,0:T(8,128)S(1)}, bf16[128,1024]{1,0:T(8,128)(2,1)S(1)}) custom-call(bf16[128,4096]{1,0:T(8,128)(2,1)S(1)} %copy-done.4, bf16[4096,1024]{1,0:T(8,128)(2,1)} %val.1, s32[32,8]{1,0:T(8,128)S(1)} %copy.17.sc, f32[8,128]{1,0:T(8,128)S(1)} %get-tuple-element.81.refs_0_), custom_call_target="tpu_custom_call" | custom-call | flops 1073741824 | bytes 8388608 | tf_op jit(solution)/shard_map/up_phase/pallas_call | solution.py:144
  16.2 0.0 copy-start.13
  16.2 0.0 copy-start.3
  16.2 2.6 %collective-permute-start.16 = (bf16[128,1024]{1,0:T(8,128)(2,1)S(1)}, bf16[128,1024]{1,0:T(8,128)(2,1)S(1)}, u32[]{:S(2)}, u32[]{:S(2)}) collective-permute-start(bf16[128,1024]{1,0:T(8,128)(2,1)S(1)} %get-tuple-element.82.act_ref), channel_id=1, source_target_pairs={{0,2},{1,3},{2,0},{3,1},{4,6},{5,7},{6,4},{7,5},{8,10},{9,11},{10,... | collective-permute-start | bytes 786440 | tf_op jit(solution)/shard_map/ppermute | solution.py:32
  18.8 2.5 %collective-permute-start.18 = (bf16[128,1024]{1,0:T(8,128)(2,1)S(1)}, bf16[128,1024]{1,0:T(8,128)(2,1)S(1)}, u32[]{:S(2)}, u32[]{:S(2)}) collective-permute-start(bf16[128,1024]{1,0:T(8,128)(2,1)S(1)} %get-tuple-element.82.act_ref), channel_id=1, source_target_pairs={{0,8},{1,9},{2,10},{3,11},{4,12},{5,13},{6,14},{7,15},{8,0},{9,1},... | collective-permute-start | bytes 786440 | tf_op jit(solution)/shard_map/ppermute | solution.py:32
  21.3 1.6 %collective-permute-start.17 = (bf16[128,1024]{1,0:T(8,128)(2,1)S(1)}, bf16[128,1024]{1,0:T(8,128)(2,1)S(1)}, u32[]{:S(2)}, u32[]{:S(2)}) collective-permute-start(bf16[128,1024]{1,0:T(8,128)(2,1)S(1)} %get-tuple-element.82.act_ref), channel_id=1, source_target_pairs={{0,4},{1,5},{2,6},{3,7},{4,0},{5,1},{6,2},{7,3},{8,12},{9,13},{10,... | collective-permute-start | bytes 786440 | tf_op jit(solution)/shard_map/ppermute | solution.py:32
  23.0 1.1 own_mix_phase.1.refs_0_.own_ref
  24.1 1.7 %collective-permute-done.16.refs_1_ = bf16[128,1024]{1,0:T(8,128)(2,1)S(1)} collective-permute-done((bf16[128,1024]{1,0:T(8,128)(2,1)S(1)}, bf16[128,1024]{1,0:T(8,128)(2,1)S(1)}, u32[]{:S(2)}, u32[]{:S(2)}) %collective-permute-start.16) | collective-permute-done | bytes 262176 | tf_op jit(solution)/shard_map/ppermute | solution.py:32
  25.8 1.8 %add_phase.10.refs_0_ = bf16[64,4096]{1,0:T(8,128)(2,1)S(1)} custom-call(bf16[256,4096]{1,0:T(8,128)(2,1)S(1)} %copy-done.3, bf16[256,4096]{1,0:T(8,128)(2,1)} %collective-permute-done.19.b, f32[128,1024]{1,0:T(8,128)S(1)} %own_mix_phase.1.refs_0_.own_ref, bf16[128,1024]{1,0:T(8,128)(2,1)S(1)} %collective-permute-done.16.refs_1_), custom_call_target="tpu_custom_call" | custom-call | tf_op jit(solution)/shard_map/add_phase/pallas_call | solution.py:282
  27.6 0.0 copy-start.20
  27.6 1.8 %collective-permute-start.21 = (bf16[64,4096]{1,0:T(8,128)(2,1)S(1)}, bf16[64,4096]{1,0:T(8,128)(2,1)S(1)}, u32[]{:S(2)}, u32[]{:S(2)}) collective-permute-start(bf16[64,4096]{1,0:T(8,128)(2,1)S(1)} %add_phase.10.refs_0_), channel_id=1, source_target_pairs={{0,2},{1,3},{2,0},{3,1},{4,6},{5,7},{6,4},{7,5},{8,10},{9,11},{10,... | collective-permute-start | bytes 1572872 | tf_op jit(solution)/shard_map/ppermute | solution.py:32
  29.4 2.6 %add_phase.11 = (bf16[64,4096]{1,0:T(8,128)(2,1)S(1)}, bf16[64,4096]{1,0:T(8,128)(2,1)S(1)}, bf16[64,4096]{1,0:T(8,128)(2,1)}) custom-call(bf16[256,4096]{1,0:T(8,128)(2,1)S(1)} %copy-done.3, bf16[256,4096]{1,0:T(8,128)(2,1)} %collective-permute-done.19.b, bf16[64,4096]{1,0:T(8,128)(2,1)S(1)} %add_phase.10.refs_0_), custom_call_target="tpu_custom_call" | custom-call | tf_op jit(solution)/shard_map/add_phase/pallas_call | solution.py:282
  31.9 1.9 %collective-permute-done.18.refs_3_ = bf16[128,1024]{1,0:T(8,128)(2,1)S(1)} collective-permute-done((bf16[128,1024]{1,0:T(8,128)(2,1)S(1)}, bf16[128,1024]{1,0:T(8,128)(2,1)S(1)}, u32[]{:S(2)}, u32[]{:S(2)}) %collective-permute-start.18) | collective-permute-done | bytes 262176 | tf_op jit(solution)/shard_map/ppermute | solution.py:32
  33.9 0.1 collective-permute-done.17.refs_2_
  34.0 7.1 %mix_phase.1 = (bf16[128,1024]{1,0:T(8,128)(2,1)S(1)}, bf16[64,4096]{1,0:T(8,128)(2,1)S(1)}, bf16[64,4096]{1,0:T(8,128)(2,1)S(1)}) custom-call(s32[1]{0:T(128)} %bitcast.me_ref, s32[7,8]{1,0:T(8,128)S(1)} %copy-done.19, f32[128,1024]{1,0:T(8,128)S(1)} %own_mix_phase.1.refs_0_.own_ref, bf16[128,1024]{1,0:T(8,128)(2,1)S(1)} %collective-permute-done.15.refs_0_, ...), custom_call_target="tpu_custom_call" | custom-call | flops 1073741824 | bytes 8388608 | tf_op jit(solution)/shard_map/mix_phase/pallas_call | solution.py:254
  41.1 0.1 collective-permute-start.20
  41.2 0.6 collective-permute-start.28
  41.8 0.8 add_phase.12
  42.6 3.2 %collective-permute-start.24 = (bf16[32,4096]{1,0:T(8,128)(2,1)}, bf16[32,4096]{1,0:T(8,128)(2,1)S(1)}, u32[]{:S(2)}, u32[]{:S(2)}) collective-permute-start(bf16[32,4096]{1,0:T(8,128)(2,1)} %get-tuple-element.90.refs_1_), channel_id=1, source_target_pairs={{0,12},{1,13},{2,14},{3,15},{4,8},{5,9},{6,10},{7,11},{8,4},{9,5},... | collective-permute-start | bytes 786440 | tf_op jit(solution)/shard_map/ppermute | solution.py:32
  45.8 0.8 add_phase.13
  46.6 0.7 copy-done.17
  47.3 1.5 %collective-permute-start.22 = (bf16[32,4096]{1,0:T(8,128)(2,1)}, bf16[32,4096]{1,0:T(8,128)(2,1)}, u32[]{:S(2)}, u32[]{:S(2)}) collective-permute-start(bf16[32,4096]{1,0:T(8,128)(2,1)} %get-tuple-element.92), channel_id=1, source_target_pairs={{0,2},{1,3},{2,0},{3,1},{4,6},{5,7},{6,4},{7,5},{8,10},{9,11},{10,... | collective-permute-start | bytes 786440 | tf_op jit(solution)/shard_map/ppermute | solution.py:32
  48.8 1.5 %collective-permute-start.14 = (f32[8,128]{1,0:T(8,128)S(1)}, f32[8,128]{1,0:T(8,128)S(1)}, u32[]{:S(2)}, u32[]{:S(2)}) collective-permute-start(f32[8,128]{1,0:T(8,128)S(1)} %get-tuple-element.81.refs_0_), channel_id=1, source_target_pairs={{0,16},{16,0},{1,17},{17,1},{2,18},{18,2},{3,19},{19,3},{4,20},{20... | collective-permute-start | bytes 12296 | tf_op jit(solution)/shard_map/ppermute | solution.py:855
  50.3 6.0 %collective-permute-done.28.b = bf16[64,4096]{1,0:T(8,128)(2,1)} collective-permute-done((bf16[64,4096]{1,0:T(8,128)(2,1)}, bf16[64,4096]{1,0:T(8,128)(2,1)}, u32[]{:S(2)}, u32[]{:S(2)}) %collective-permute-start.28) | collective-permute-done | bytes 524320 | tf_op jit(solution)/shard_map/ppermute | solution.py:32
  56.3 1.8 %add_phase.15 = (bf16[32,4096]{1,0:T(8,128)(2,1)S(1)}, bf16[32,4096]{1,0:T(8,128)(2,1)}) custom-call(bf16[64,4096]{1,0:T(8,128)(2,1)S(1)} %get-tuple-element.97.a, bf16[64,4096]{1,0:T(8,128)(2,1)} %collective-permute-done.28.b, bf16[32,4096]{1,0:T(8,128)(2,1)S(1)} %get-tuple-element.89.refs_0_), custom_call_target="tpu_custom_call" | custom-call | tf_op jit(solution)/shard_map/add_phase/pallas_call | solution.py:282
  58.1 1.4 %collective-permute-start.29 = (bf16[32,4096]{1,0:T(8,128)(2,1)}, bf16[32,4096]{1,0:T(8,128)(2,1)S(1)}, u32[]{:S(2)}, u32[]{:S(2)}) collective-permute-start(bf16[32,4096]{1,0:T(8,128)(2,1)} %get-tuple-element.99), channel_id=1, source_target_pairs={{0,4},{1,5},{2,6},{3,7},{4,0},{5,1},{6,2},{7,3},{8,12},{9,13},{10,... | collective-permute-start | bytes 786440 | tf_op jit(solution)/shard_map/ppermute | solution.py:32
  59.6 9.4 %collective-permute-done.23.refs_0_.refs_6_ = bf16[32,4096]{1,0:T(8,128)(2,1)S(1)} collective-permute-done((bf16[32,4096]{1,0:T(8,128)(2,1)S(1)}, bf16[32,4096]{1,0:T(8,128)(2,1)S(1)}, u32[]{:S(2)}, u32[]{:S(2)}) %collective-permute-start.23) | collective-permute-done | bytes 262176 | tf_op jit(solution)/shard_map/ppermute | solution.py:32
  69.0 1.0 add_phase.14
  70.1 0.1 collective-permute-start.25
  70.1 1.9 %collective-permute-start.26 = (bf16[8,4096]{1,0:T(8,128)(2,1)S(1)}, bf16[8,4096]{1,0:T(8,128)(2,1)S(1)}, u32[]{:S(2)}, u32[]{:S(2)}) collective-permute-start(bf16[8,4096]{1,0:T(8,128)(2,1)S(1)} %get-tuple-element.95), channel_id=1, source_target_pairs={{0,8},{1,9},{2,10},{3,11},{4,12},{5,13},{6,14},{7,15},{8,0},{9,1},... | collective-permute-start | bytes 196616 | tf_op jit(solution)/shard_map/ppermute | solution.py:32
  72.0 2.5 %collective-permute-start.27 = (bf16[8,4096]{1,0:T(8,128)(2,1)S(1)}, bf16[8,4096]{1,0:T(8,128)(2,1)S(1)}, u32[]{:S(2)}, u32[]{:S(2)}) collective-permute-start(bf16[8,4096]{1,0:T(8,128)(2,1)S(1)} %get-tuple-element.96), channel_id=1, source_target_pairs={{0,12},{1,13},{2,14},{3,15},{4,8},{5,9},{6,10},{7,11},{8,4},{9,5},... | collective-permute-start | bytes 196616 | tf_op jit(solution)/shard_map/ppermute | solution.py:32
  74.5 0.1 copy.18.refs_10_
  74.6 0.1 copy.19.refs_12_
  74.7 0.5 slice.3
  75.9 1.3 collective-permute-done.26.refs_2_
  77.2 1.0 collective-permute-done.27.refs_3_
  78.2 1.4 %token_phase.1 = bf16[8,4224]{1,0:T(8,128)(2,1)S(1)} custom-call(s32[1]{0:T(128)} %bitcast.me_ref, bf16[8,4096]{1,0:T(8,128)(2,1)S(1)} %get-tuple-element.93.refs_0_, bf16[8,4096]{1,0:T(8,128)(2,1)S(1)} %collective-permute-done.25.refs_1_, bf16[8,4096]{1,0:T(8,128)(2,1)S(1)} %collective-permute-done.26.refs_2_, ...), custom_call_target="tpu_custom_call" | custom-call | tf_op jit(solution)/shard_map/token_phase/pallas_call | solution.py:609
  79.6 0.2 conditional.1
  79.8 2.5 %collective-permute-start.32 = (bf16[8,4224]{1,0:T(8,128)(2,1)S(1)}, bf16[8,4224]{1,0:T(8,128)(2,1)S(1)}, u32[]{:S(2)}, u32[]{:S(2)}) collective-permute-start(bf16[8,4224]{1,0:T(8,128)(2,1)S(1)} %get-tuple-element.142), channel_id=1, source_target_pairs={{0,12},{1,13},{2,14},{3,15},{4,8},{5,9},{6,10},{7,11},{8,4},{9,5},... | collective-permute-start | bytes 202760 | tf_op jit(solution)/shard_map/ppermute | solution.py:32
  82.3 0.0 collective-permute-start.31
  82.3 1.9 %collective-permute-start.30 = (bf16[8,4224]{1,0:T(8,128)(2,1)S(1)}, bf16[8,4224]{1,0:T(8,128)(2,1)S(1)}, u32[]{:S(2)}, u32[]{:S(2)}) collective-permute-start(bf16[8,4224]{1,0:T(8,128)(2,1)S(1)} %get-tuple-element.142), channel_id=1, source_target_pairs={{0,4},{1,5},{2,6},{3,7},{4,0},{5,1},{6,2},{7,3},{8,12},{9,13},{10,... | collective-permute-start | bytes 202760 | tf_op jit(solution)/shard_map/ppermute | solution.py:32
  84.3 2.0 %collective-permute-done.32 = bf16[8,4224]{1,0:T(8,128)(2,1)S(1)} collective-permute-done((bf16[8,4224]{1,0:T(8,128)(2,1)S(1)}, bf16[8,4224]{1,0:T(8,128)(2,1)S(1)}, u32[]{:S(2)}, u32[]{:S(2)}) %collective-permute-start.32) | collective-permute-done | bytes 67616 | tf_op jit(solution)/shard_map/ppermute | solution.py:32
  86.3 1.4 %collective-permute-done.31 = bf16[8,4224]{1,0:T(8,128)(2,1)S(1)} collective-permute-done((bf16[8,4224]{1,0:T(8,128)(2,1)S(1)}, bf16[8,4224]{1,0:T(8,128)(2,1)S(1)}, u32[]{:S(2)}, u32[]{:S(2)}) %collective-permute-start.31) | collective-permute-done | bytes 67616 | tf_op jit(solution)/shard_map/ppermute | solution.py:32
  87.7 1.6 %collective-permute-start.33 = (bf16[32,4224]{1,0:T(8,128)(2,1)S(1)}, bf16[32,4224]{1,0:T(8,128)(2,1)S(1)}, u32[]{:S(2)}, u32[]{:S(2)}) collective-permute-start(bf16[32,4224]{1,0:T(8,128)(2,1)S(1)} %pad_maximum_fusion.1), channel_id=1, source_target_pairs={{0,2},{1,3},{2,0},{3,1},{4,6},{5,7},{6,4},{7,5},{8,10},{9,11},{10,... | collective-permute-start | bytes 811016 | tf_op jit(solution)/shard_map/ppermute | solution.py:32
  89.4 4.8 %collective-permute-done.33 = bf16[32,4224]{1,0:T(8,128)(2,1)S(1)} collective-permute-done((bf16[32,4224]{1,0:T(8,128)(2,1)S(1)}, bf16[32,4224]{1,0:T(8,128)(2,1)S(1)}, u32[]{:S(2)}, u32[]{:S(2)}) %collective-permute-start.33) | collective-permute-done | bytes 270368 | tf_op jit(solution)/shard_map/ppermute | solution.py:32
  94.3 0.1 collective-permute-start.34
  94.4 1.9 %collective-permute-done.34 = bf16[64,4224]{1,0:T(8,128)(2,1)S(1)} collective-permute-done((bf16[64,4224]{1,0:T(8,128)(2,1)S(1)}, bf16[64,4224]{1,0:T(8,128)(2,1)S(1)}, u32[]{:S(2)}, u32[]{:S(2)}) %collective-permute-start.34) | collective-permute-done | bytes 540704 | tf_op jit(solution)/shard_map/ppermute | solution.py:32
  96.3 0.0 copy-start.1
  96.4 0.0 copy-start.10
  96.4 7.5 %mixed_grad_phase.1 = (f32[1,1]{1,0:T(1,128)}, bf16[128,1024]{1,0:T(8,128)(2,1)S(1)}, bf16[128,1024]{1,0:T(8,128)(2,1)S(1)}, bf16[128,1024]{1,0:T(8,128)(2,1)S(1...) custom-call(s32[1]{0:T(128)} %bitcast.me_ref, s32[7,8]{1,0:T(8,128)S(1)} %copy-done.19, ...), custom_call_target="tpu_custom_call" | custom-call | flops 1073741824 | bytes 8388608 | tf_op jit(solution)/shard_map/mixed_grad_phase/pallas_call | solution.py:669
  103.9 0.2 collective-permute-start.35
  104.1 1.6 %collective-permute-start.36 = (bf16[128,1024]{1,0:T(8,128)(2,1)S(1)}, bf16[128,1024]{1,0:T(8,128)(2,1)S(1)}, u32[]{:S(2)}, u32[]{:S(2)}) collective-permute-start(bf16[128,1024]{1,0:T(8,128)(2,1)S(1)} %get-tuple-element.106), channel_id=1, source_target_pairs={{0,2},{1,3},{2,0},{3,1},{4,6},{5,7},{6,4},{7,5},{8,10},{9,11},{10,... | collective-permute-start | bytes 786440 | tf_op jit(solution)/shard_map/ppermute | solution.py:32
  105.7 0.9 collective-permute-start.37
  106.6 1.7 %collective-permute-start.38 = (bf16[128,1024]{1,0:T(8,128)(2,1)S(1)}, bf16[128,1024]{1,0:T(8,128)(2,1)S(1)}, u32[]{:S(2)}, u32[]{:S(2)}) collective-permute-start(bf16[128,1024]{1,0:T(8,128)(2,1)S(1)} %get-tuple-element.108), channel_id=1, source_target_pairs={{0,8},{1,9},{2,10},{3,11},{4,12},{5,13},{6,14},{7,15},{8,0},{9,1},... | collective-permute-start | bytes 786440 | tf_op jit(solution)/shard_map/ppermute | solution.py:32
  108.4 5.5 %block_grad_phase.1 = (f32[8,128,128]{2,1,0:T(8,128)}, f32[7,8,128,128]{3,2,1,0:T(8,128)}, f32[128,1024]{1,0:T(8,128)S(1)}) custom-call(s32[7,8]{1,0:T(8,128)S(1)} %copy-done.19, bf16[128,1024]{1,0:T(8,128)(2,1)S(1)} %copy-done.12, bf16[128,1024]{1,0:T(8,128)(2,1)S(1)} %get-tuple-element.103.mg, bf16[128,1024]{1,0:T(8,128)(2,1)S(1)} %copy-done.8, ...), custom_call_target="tpu_custom_call" | custom-call | flops 402653184 | bytes 12582912 | tf_op jit(solution)/shard_map/block_grad_phase/pallas_call | solution.py:714
  113.8 6.5 %down_grad_phase.1 = f32[1024,4096]{1,0:T(8,128)} custom-call(bf16[128,1024]{1,0:T(8,128)(2,1)S(1)} %copy-done.16, bf16[128,4224]{1,0:T(8,128)(2,1)S(1)} %constant_dynamic-update-slice_fusion.16.grad_ref), custom_call_target="tpu_custom_call" | custom-call | flops 1073741824 | bytes 16777216 | tf_op jit(solution)/shard_map/down_grad_phase/pallas_call | solution.py:756
  120.3 0.8 collective-permute-done.38.refs_3_
  121.2 6.7 %up_grad_phase.1 = f32[4096,1024]{1,0:T(8,128)} custom-call(bf16[128,4096]{1,0:T(8,128)(2,1)S(1)} %copy-done.4, f32[128,1024]{1,0:T(8,128)S(1)} %copy-done.14, f32[128,1024]{1,0:T(8,128)S(1)} %get-tuple-element.104.grad_ref, bf16[128,1024]{1,0:T(8,128)(2,1)S(1)} %collective-permute-done.35.refs_0_, bf16[128,1024]{1,0:T(8,128)(2,1)S(1)} %collective-permute-done.36.refs_1_, ...), custom_call_target="tpu_custom_call" | custom-call | flops 1073741824 | bytes 16777216 | tf_op jit(solution)/shard_map/up_grad_phase/pallas_call | solution.py:800
  (65 shorter events, 0.3 us)
Async XLA Ops:
  0.6 11.3 %copy-start.26 = (s32[32,8]{0,1:T(8,128)S(1)}, s32[32,8]{0,1:T(8,128)}, u32[]{:S(2)}) copy-start(s32[32,8]{0,1:T(8,128)} %param.16) | copy-start | bytes 3076
  0.6 11.4 %copy-start.4 = (bf16[128,4096]{1,0:T(8,128)(2,1)S(1)}, bf16[128,4096]{1,0:T(8,128)(2,1)}, u32[]{:S(2)}) copy-start(bf16[128,4096]{1,0:T(8,128)(2,1)} %tok.3) | copy-start | bytes 3145732
  10.2 1.3 %copy-start.2 = (bf16[256,4096]{1,0:T(8,128)(2,1)}, bf16[256,4096]{1,0:T(8,128)(2,1)S(1)}, u32[]{:S(2)}) copy-start(bf16[256,4096]{1,0:T(8,128)(2,1)S(1)} %get-tuple-element.83.a) | copy-start | bytes 6291460
  11.5 14.3 %collective-permute-start.19 = (bf16[256,4096]{1,0:T(8,128)(2,1)}, bf16[256,4096]{1,0:T(8,128)(2,1)}, u32[]{:S(2)}, u32[]{:S(2)}) collective-permute-start(bf16[256,4096]{1,0:T(8,128)(2,1)} %get-tuple-element.84), channel_id=1, source_target_pairs={{0,1},{1,0},{2,3},{3,2},{4,5},{5,4},{6,7},{7,6},{8,9},{9,8},{10,11... | collective-permute-start | bytes 6291464 | tf_op jit(solution)/shard_map/ppermute | solution.py:32
  12.1 10.9 %copy-start = (bf16[7,8,128,128]{3,2,1,0:T(8,128)(2,1)S(1)}, bf16[7,8,128,128]{3,2,1,0:T(8,128)(2,1)}, u32[]{:S(2)}) copy-start(bf16[7,8,128,128]{3,2,1,0:T(8,128)(2,1)} %refs_5_.3) | copy-start | bytes 5505028
  12.1 10.9 %copy-start.9 = (bf16[8,128,128]{2,1,0:T(8,128)(2,1)S(1)}, bf16[8,128,128]{2,1,0:T(8,128)(2,1)}, u32[]{:S(2)}) copy-start(bf16[8,128,128]{2,1,0:T(8,128)(2,1)} %refs_4_.3) | copy-start | bytes 786436
  12.1 10.9 %copy-start.19 = (s32[7,8]{1,0:T(8,128)S(1)}, s32[7,8]{1,0:T(8,128)}, u32[]{:S(2)}) copy-start(s32[7,8]{1,0:T(8,128)} %pat.7) | copy-start | bytes 676
  16.2 7.9 %copy-start.11 = (bf16[128,1024]{1,0:T(8,128)(2,1)}, bf16[128,1024]{1,0:T(8,128)(2,1)S(1)}, u32[]{:S(2)}) copy-start(bf16[128,1024]{1,0:T(8,128)(2,1)S(1)} %get-tuple-element.82.act_ref) | copy-start | bytes 786436
  16.2 7.9 %copy-start.13 = (f32[128,1024]{1,0:T(8,128)}, f32[128,1024]{1,0:T(8,128)S(1)}, u32[]{:S(2)}) copy-start(f32[128,1024]{1,0:T(8,128)S(1)} %get-tuple-element.102.pre_ref) | copy-start | bytes 1572868
  16.2 9.6 %copy-start.3 = (bf16[256,4096]{1,0:T(8,128)(2,1)S(1)}, bf16[256,4096]{1,0:T(8,128)(2,1)}, u32[]{:S(2)}) copy-start(bf16[256,4096]{1,0:T(8,128)(2,1)} %copy-done.2) | copy-start | bytes 6291460
  16.2 9.6 %collective-permute-start.16 = (bf16[128,1024]{1,0:T(8,128)(2,1)S(1)}, bf16[128,1024]{1,0:T(8,128)(2,1)S(1)}, u32[]{:S(2)}, u32[]{:S(2)}) collective-permute-start(bf16[128,1024]{1,0:T(8,128)(2,1)S(1)} %get-tuple-element.82.act_ref), channel_id=1, source_target_pairs={{0,2},{1,3},{2,0},{3,1},{4,6},{5,7},{6,4},{7,5},{8,10},{9,11},{10,... | collective-permute-start | bytes 786440 | tf_op jit(solution)/shard_map/ppermute | solution.py:32
  18.8 15.1 %collective-permute-start.18 = (bf16[128,1024]{1,0:T(8,128)(2,1)S(1)}, bf16[128,1024]{1,0:T(8,128)(2,1)S(1)}, u32[]{:S(2)}, u32[]{:S(2)}) collective-permute-start(bf16[128,1024]{1,0:T(8,128)(2,1)S(1)} %get-tuple-element.82.act_ref), channel_id=1, source_target_pairs={{0,8},{1,9},{2,10},{3,11},{4,12},{5,13},{6,14},{7,15},{8,0},{9,1},... | collective-permute-start | bytes 786440 | tf_op jit(solution)/shard_map/ppermute | solution.py:32
  21.3 12.7 %collective-permute-start.17 = (bf16[128,1024]{1,0:T(8,128)(2,1)S(1)}, bf16[128,1024]{1,0:T(8,128)(2,1)S(1)}, u32[]{:S(2)}, u32[]{:S(2)}) collective-permute-start(bf16[128,1024]{1,0:T(8,128)(2,1)S(1)} %get-tuple-element.82.act_ref), channel_id=1, source_target_pairs={{0,4},{1,5},{2,6},{3,7},{4,0},{5,1},{6,2},{7,3},{8,12},{9,13},{10,... | collective-permute-start | bytes 786440 | tf_op jit(solution)/shard_map/ppermute | solution.py:32
  23.0 11.0 %collective-permute-start.15 = (bf16[128,1024]{1,0:T(8,128)(2,1)S(1)}, bf16[128,1024]{1,0:T(8,128)(2,1)S(1)}, u32[]{:S(2)}, u32[]{:S(2)}) collective-permute-start(bf16[128,1024]{1,0:T(8,128)(2,1)S(1)} %get-tuple-element.82.act_ref), channel_id=1, source_target_pairs={{0,1},{1,0},{2,3},{3,2},{4,5},{5,4},{6,7},{7,6},{8,9},{9,8},{10,11... | collective-permute-start | bytes 786440 | tf_op jit(solution)/shard_map/ppermute | solution.py:32
  27.6 6.5 %copy-start.20 = (s32[8,32]{1,0:T(8,128)S(1)}, s32[8,32]{1,0:T(8,128)}, u32[]{:S(2)}) copy-start(s32[8,32]{1,0:T(8,128)} %sc.2) | copy-start | bytes 3076
  27.6 14.3 %collective-permute-start.21 = (bf16[64,4096]{1,0:T(8,128)(2,1)S(1)}, bf16[64,4096]{1,0:T(8,128)(2,1)S(1)}, u32[]{:S(2)}, u32[]{:S(2)}) collective-permute-start(bf16[64,4096]{1,0:T(8,128)(2,1)S(1)} %add_phase.10.refs_0_), channel_id=1, source_target_pairs={{0,2},{1,3},{2,0},{3,1},{4,6},{5,7},{6,4},{7,5},{8,10},{9,11},{10,... | collective-permute-start | bytes 1572872 | tf_op jit(solution)/shard_map/ppermute | solution.py:32
  34.0 7.1 %copy-start.5 = (bf16[128,1024]{1,0:T(8,128)(2,1)}, bf16[128,1024]{1,0:T(8,128)(2,1)S(1)}, u32[]{:S(2)}) copy-start(bf16[128,1024]{1,0:T(8,128)(2,1)S(1)} %collective-permute-done.17.refs_2_) | copy-start | bytes 786436
  34.0 7.1 %copy-start.7 = (bf16[128,1024]{1,0:T(8,128)(2,1)}, bf16[128,1024]{1,0:T(8,128)(2,1)S(1)}, u32[]{:S(2)}) copy-start(bf16[128,1024]{1,0:T(8,128)(2,1)S(1)} %collective-permute-done.15.refs_0_) | copy-start | bytes 786436
  41.1 5.5 %copy-start.15 = (bf16[128,1024]{1,0:T(8,128)(2,1)}, bf16[128,1024]{1,0:T(8,128)(2,1)S(1)}, u32[]{:S(2)}) copy-start(bf16[128,1024]{1,0:T(8,128)(2,1)S(1)} %get-tuple-element.109.mixed_ref) | copy-start | bytes 786436
  41.1 4.7 %collective-permute-start.20 = (bf16[64,4096]{1,0:T(8,128)(2,1)S(1)}, bf16[64,4096]{1,0:T(8,128)(2,1)S(1)}, u32[]{:S(2)}, u32[]{:S(2)}) collective-permute-start(bf16[64,4096]{1,0:T(8,128)(2,1)S(1)} %get-tuple-element.87), channel_id=1, source_target_pairs={{0,1},{1,0},{2,3},{3,2},{4,5},{5,4},{6,7},{7,6},{8,9},{9,8},{10,11... | collective-permute-start | bytes 1572872 | tf_op jit(solution)/shard_map/ppermute | solution.py:32
  41.2 15.1 %collective-permute-start.28 = (bf16[64,4096]{1,0:T(8,128)(2,1)}, bf16[64,4096]{1,0:T(8,128)(2,1)}, u32[]{:S(2)}, u32[]{:S(2)}) collective-permute-start(bf16[64,4096]{1,0:T(8,128)(2,1)} %get-tuple-element.85.refs_7_), channel_id=1, source_target_pairs={{0,2},{1,3},{2,0},{3,1},{4,6},{5,7},{6,4},{7,5},{8,10},{9,11},{10,... | collective-permute-start | bytes 1572872 | tf_op jit(solution)/shard_map/ppermute | solution.py:32
  42.6 17.0 %collective-permute-start.24 = (bf16[32,4096]{1,0:T(8,128)(2,1)}, bf16[32,4096]{1,0:T(8,128)(2,1)S(1)}, u32[]{:S(2)}, u32[]{:S(2)}) collective-permute-start(bf16[32,4096]{1,0:T(8,128)(2,1)} %get-tuple-element.90.refs_1_), channel_id=1, source_target_pairs={{0,12},{1,13},{2,14},{3,15},{4,8},{5,9},{6,10},{7,11},{8,4},{9,5},... | collective-permute-start | bytes 786440 | tf_op jit(solution)/shard_map/ppermute | solution.py:32
  45.8 23.2 %collective-permute-start.23 = (bf16[32,4096]{1,0:T(8,128)(2,1)S(1)}, bf16[32,4096]{1,0:T(8,128)(2,1)S(1)}, u32[]{:S(2)}, u32[]{:S(2)}) collective-permute-start(bf16[32,4096]{1,0:T(8,128)(2,1)S(1)} %get-tuple-element.89.refs_0_), channel_id=1, source_target_pairs={{0,8},{1,9},{2,10},{3,11},{4,12},{5,13},{6,14},{7,15},{8,0},{9,1},... | collective-permute-start | bytes 786440 | tf_op jit(solution)/shard_map/ppermute | solution.py:32
  46.6 0.7 copy-start.17
  47.3 21.7 %collective-permute-start.22 = (bf16[32,4096]{1,0:T(8,128)(2,1)}, bf16[32,4096]{1,0:T(8,128)(2,1)}, u32[]{:S(2)}, u32[]{:S(2)}) collective-permute-start(bf16[32,4096]{1,0:T(8,128)(2,1)} %get-tuple-element.92), channel_id=1, source_target_pairs={{0,2},{1,3},{2,0},{3,1},{4,6},{5,7},{6,4},{7,5},{8,10},{9,11},{10,... | collective-permute-start | bytes 786440 | tf_op jit(solution)/shard_map/ppermute | solution.py:32
  48.8 25.9 %collective-permute-start.14 = (f32[8,128]{1,0:T(8,128)S(1)}, f32[8,128]{1,0:T(8,128)S(1)}, u32[]{:S(2)}, u32[]{:S(2)}) collective-permute-start(f32[8,128]{1,0:T(8,128)S(1)} %get-tuple-element.81.refs_0_), channel_id=1, source_target_pairs={{0,16},{16,0},{1,17},{17,1},{2,18},{18,2},{3,19},{19,3},{4,20},{20... | collective-permute-start | bytes 12296 | tf_op jit(solution)/shard_map/ppermute | solution.py:855
  50.3 18.7 %copy-start.18 = (bf16[32,4096]{1,0:T(8,128)(2,1)S(1)}, bf16[32,4096]{1,0:T(8,128)(2,1)}, u32[]{:S(2)}) copy-start(bf16[32,4096]{1,0:T(8,128)(2,1)} %copy-done.17) | copy-start | bytes 786436
  56.3 18.2 %copy-start.24 = (s32[128,8]{0,1:T(8,128)S(1)}, s32[128,8]{0,1:T(8,128)}, u32[]{:S(2)}) copy-start(s32[128,8]{0,1:T(8,128)} %param.24) | copy-start | bytes 12292
  56.3 18.3 %copy-start.25 = (f32[128,8]{0,1:T(8,128)S(1)}, f32[128,8]{0,1:T(8,128)}, u32[]{:S(2)}) copy-start(f32[128,8]{0,1:T(8,128)} %param.25) | copy-start | bytes 12292
  56.3 21.9 %copy-start.21 = (f32[4096]{0:T(1024)S(1)}, f32[4096]{0:T(1024)}, u32[]{:S(2)}) copy-start(f32[4096]{0:T(1024)} %param.22) | copy-start | bytes 49156
  58.1 20.0 %collective-permute-start.29 = (bf16[32,4096]{1,0:T(8,128)(2,1)}, bf16[32,4096]{1,0:T(8,128)(2,1)S(1)}, u32[]{:S(2)}, u32[]{:S(2)}) collective-permute-start(bf16[32,4096]{1,0:T(8,128)(2,1)} %get-tuple-element.99), channel_id=1, source_target_pairs={{0,4},{1,5},{2,6},{3,7},{4,0},{5,1},{6,2},{7,3},{8,12},{9,13},{10,... | collective-permute-start | bytes 786440 | tf_op jit(solution)/shard_map/ppermute | solution.py:32
  70.1 5.9 %collective-permute-start.25 = (bf16[8,4096]{1,0:T(8,128)(2,1)S(1)}, bf16[8,4096]{1,0:T(8,128)(2,1)S(1)}, u32[]{:S(2)}, u32[]{:S(2)}) collective-permute-start(bf16[8,4096]{1,0:T(8,128)(2,1)S(1)} %get-tuple-element.94), channel_id=1, source_target_pairs={{0,4},{1,5},{2,6},{3,7},{4,0},{5,1},{6,2},{7,3},{8,12},{9,13},{10,... | collective-permute-start | bytes 196616 | tf_op jit(solution)/shard_map/ppermute | solution.py:32
  70.1 7.0 %collective-permute-start.26 = (bf16[8,4096]{1,0:T(8,128)(2,1)S(1)}, bf16[8,4096]{1,0:T(8,128)(2,1)S(1)}, u32[]{:S(2)}, u32[]{:S(2)}) collective-permute-start(bf16[8,4096]{1,0:T(8,128)(2,1)S(1)} %get-tuple-element.95), channel_id=1, source_target_pairs={{0,8},{1,9},{2,10},{3,11},{4,12},{5,13},{6,14},{7,15},{8,0},{9,1},... | collective-permute-start | bytes 196616 | tf_op jit(solution)/shard_map/ppermute | solution.py:32
  72.0 6.2 %collective-permute-start.27 = (bf16[8,4096]{1,0:T(8,128)(2,1)S(1)}, bf16[8,4096]{1,0:T(8,128)(2,1)S(1)}, u32[]{:S(2)}, u32[]{:S(2)}) collective-permute-start(bf16[8,4096]{1,0:T(8,128)(2,1)S(1)} %get-tuple-element.96), channel_id=1, source_target_pairs={{0,12},{1,13},{2,14},{3,15},{4,8},{5,9},{6,10},{7,11},{8,4},{9,5},... | collective-permute-start | bytes 196616 | tf_op jit(solution)/shard_map/ppermute | solution.py:32
  79.8 6.5 %collective-permute-start.32 = (bf16[8,4224]{1,0:T(8,128)(2,1)S(1)}, bf16[8,4224]{1,0:T(8,128)(2,1)S(1)}, u32[]{:S(2)}, u32[]{:S(2)}) collective-permute-start(bf16[8,4224]{1,0:T(8,128)(2,1)S(1)} %get-tuple-element.142), channel_id=1, source_target_pairs={{0,12},{1,13},{2,14},{3,15},{4,8},{5,9},{6,10},{7,11},{8,4},{9,5},... | collective-permute-start | bytes 202760 | tf_op jit(solution)/shard_map/ppermute | solution.py:32
  82.3 5.4 %collective-permute-start.31 = (bf16[8,4224]{1,0:T(8,128)(2,1)S(1)}, bf16[8,4224]{1,0:T(8,128)(2,1)S(1)}, u32[]{:S(2)}, u32[]{:S(2)}) collective-permute-start(bf16[8,4224]{1,0:T(8,128)(2,1)S(1)} %get-tuple-element.142), channel_id=1, source_target_pairs={{0,8},{1,9},{2,10},{3,11},{4,12},{5,13},{6,14},{7,15},{8,0},{9,1},... | collective-permute-start | bytes 202760 | tf_op jit(solution)/shard_map/ppermute | solution.py:32
  82.3 5.4 %collective-permute-start.30 = (bf16[8,4224]{1,0:T(8,128)(2,1)S(1)}, bf16[8,4224]{1,0:T(8,128)(2,1)S(1)}, u32[]{:S(2)}, u32[]{:S(2)}) collective-permute-start(bf16[8,4224]{1,0:T(8,128)(2,1)S(1)} %get-tuple-element.142), channel_id=1, source_target_pairs={{0,4},{1,5},{2,6},{3,7},{4,0},{5,1},{6,2},{7,3},{8,12},{9,13},{10,... | collective-permute-start | bytes 202760 | tf_op jit(solution)/shard_map/ppermute | solution.py:32
  87.7 6.5 %collective-permute-start.33 = (bf16[32,4224]{1,0:T(8,128)(2,1)S(1)}, bf16[32,4224]{1,0:T(8,128)(2,1)S(1)}, u32[]{:S(2)}, u32[]{:S(2)}) collective-permute-start(bf16[32,4224]{1,0:T(8,128)(2,1)S(1)} %pad_maximum_fusion.1), channel_id=1, source_target_pairs={{0,2},{1,3},{2,0},{3,1},{4,6},{5,7},{6,4},{7,5},{8,10},{9,11},{10,... | collective-permute-start | bytes 811016 | tf_op jit(solution)/shard_map/ppermute | solution.py:32
  94.3 2.0 %collective-permute-start.34 = (bf16[64,4224]{1,0:T(8,128)(2,1)S(1)}, bf16[64,4224]{1,0:T(8,128)(2,1)S(1)}, u32[]{:S(2)}, u32[]{:S(2)}) collective-permute-start(bf16[64,4224]{1,0:T(8,128)(2,1)S(1)} %get-tuple-element.132), channel_id=1, source_target_pairs={{0,1},{1,0},{2,3},{3,2},{4,5},{5,4},{6,7},{7,6},{8,9},{9,8},{10,11... | collective-permute-start | bytes 1622024 | tf_op jit(solution)/shard_map/ppermute | solution.py:32
  96.3 12.0 %copy-start.1 = (bf16[7,8,128,128]{3,2,1,0:T(8,128)(2,1)S(1)}, bf16[7,8,128,128]{3,2,1,0:T(8,128)(2,1)}, u32[]{:S(2)}) copy-start(bf16[7,8,128,128]{3,2,1,0:T(8,128)(2,1)} %refs_5_.3) | copy-start | bytes 5505028
  96.4 12.0 %copy-start.6 = (bf16[128,1024]{1,0:T(8,128)(2,1)S(1)}, bf16[128,1024]{1,0:T(8,128)(2,1)}, u32[]{:S(2)}) copy-start(bf16[128,1024]{1,0:T(8,128)(2,1)} %copy-done.5) | copy-start | bytes 786436
  96.4 12.0 %copy-start.8 = (bf16[128,1024]{1,0:T(8,128)(2,1)S(1)}, bf16[128,1024]{1,0:T(8,128)(2,1)}, u32[]{:S(2)}) copy-start(bf16[128,1024]{1,0:T(8,128)(2,1)} %copy-done.7) | copy-start | bytes 786436
  96.4 12.0 %copy-start.10 = (bf16[8,128,128]{2,1,0:T(8,128)(2,1)S(1)}, bf16[8,128,128]{2,1,0:T(8,128)(2,1)}, u32[]{:S(2)}) copy-start(bf16[8,128,128]{2,1,0:T(8,128)(2,1)} %refs_4_.3) | copy-start | bytes 786436
  96.4 11.9 %copy-start.12 = (bf16[128,1024]{1,0:T(8,128)(2,1)S(1)}, bf16[128,1024]{1,0:T(8,128)(2,1)}, u32[]{:S(2)}) copy-start(bf16[128,1024]{1,0:T(8,128)(2,1)} %copy-done.11) | copy-start | bytes 786436
  103.9 16.3 %collective-permute-start.35 = (bf16[128,1024]{1,0:T(8,128)(2,1)S(1)}, bf16[128,1024]{1,0:T(8,128)(2,1)S(1)}, u32[]{:S(2)}, u32[]{:S(2)}) collective-permute-start(bf16[128,1024]{1,0:T(8,128)(2,1)S(1)} %get-tuple-element.105), channel_id=1, source_target_pairs={{0,1},{1,0},{2,3},{3,2},{4,5},{5,4},{6,7},{7,6},{8,9},{9,8},{10,11... | collective-permute-start | bytes 786440 | tf_op jit(solution)/shard_map/ppermute | solution.py:32
  104.1 16.2 %collective-permute-start.36 = (bf16[128,1024]{1,0:T(8,128)(2,1)S(1)}, bf16[128,1024]{1,0:T(8,128)(2,1)S(1)}, u32[]{:S(2)}, u32[]{:S(2)}) collective-permute-start(bf16[128,1024]{1,0:T(8,128)(2,1)S(1)} %get-tuple-element.106), channel_id=1, source_target_pairs={{0,2},{1,3},{2,0},{3,1},{4,6},{5,7},{6,4},{7,5},{8,10},{9,11},{10,... | collective-permute-start | bytes 786440 | tf_op jit(solution)/shard_map/ppermute | solution.py:32
  105.7 14.6 %collective-permute-start.37 = (bf16[128,1024]{1,0:T(8,128)(2,1)S(1)}, bf16[128,1024]{1,0:T(8,128)(2,1)S(1)}, u32[]{:S(2)}, u32[]{:S(2)}) collective-permute-start(bf16[128,1024]{1,0:T(8,128)(2,1)S(1)} %get-tuple-element.107), channel_id=1, source_target_pairs={{0,4},{1,5},{2,6},{3,7},{4,0},{5,1},{6,2},{7,3},{8,12},{9,13},{10,... | collective-permute-start | bytes 786440 | tf_op jit(solution)/shard_map/ppermute | solution.py:32
  106.6 14.6 %collective-permute-start.38 = (bf16[128,1024]{1,0:T(8,128)(2,1)S(1)}, bf16[128,1024]{1,0:T(8,128)(2,1)S(1)}, u32[]{:S(2)}, u32[]{:S(2)}) collective-permute-start(bf16[128,1024]{1,0:T(8,128)(2,1)S(1)} %get-tuple-element.108), channel_id=1, source_target_pairs={{0,8},{1,9},{2,10},{3,11},{4,12},{5,13},{6,14},{7,15},{8,0},{9,1},... | collective-permute-start | bytes 786440 | tf_op jit(solution)/shard_map/ppermute | solution.py:32
  108.3 5.5 %copy-start.16 = (bf16[128,1024]{1,0:T(8,128)(2,1)S(1)}, bf16[128,1024]{1,0:T(8,128)(2,1)}, u32[]{:S(2)}) copy-start(bf16[128,1024]{1,0:T(8,128)(2,1)} %copy-done.15) | copy-start | bytes 786436
  113.8 7.4 %copy-start.14 = (f32[128,1024]{1,0:T(8,128)S(1)}, f32[128,1024]{1,0:T(8,128)}, u32[]{:S(2)}) copy-start(f32[128,1024]{1,0:T(8,128)} %copy-done.13) | copy-start | bytes 1572868

commit v5 on v4

--- a/solution.py
+++ b/solution.py
@@ -735,7 +735,7 @@
 
 def down_grad_phase(mixed, grad, features):
     token_count, hidden = mixed.shape
-    chunk = min(512, features)
+    chunk = min(256, features)
     steps = features // chunk
 
     def kernel(mixed_ref, grad_ref, out, turned, table, left):
@@ -772,7 +772,7 @@
 def up_grad_phase(tokens, pre, act_grad, received):
     token_count, depth = tokens.shape
     hidden = pre.shape[1]
-    chunk = min(512, depth)
+    chunk = min(256, depth)
     steps = depth // chunk
 
     def kernel(tok, pre_ref, grad_ref, *refs):
@@ -870,7 +870,7 @@
         far = add_phase(far, far_laid, len(masks) // 2, [])
         near = add_phase(near, near_laid, len(masks) // 2, far[:1])
         picked = [swap(piece, m) for piece, m in zip([*near, *far], masks)]
-        terms = reduce_rows(keep, send, groups, [far, picked[2:]])
+        terms = reduce_rows(keep, send, groups, [far, picked[2:3]])
     else:
         terms = reduce_rows(keep, send, groups)
 

time: 128 us -> 127 us (level)
  waiting for transfers between devices: 32.5 us -> 30.2 us
    ppermute x24, waiting for transfers between devices: 32.5 us -> 30.2 us  [swap(): return lax.ppermute(block, 'mp', [(i, i ^ mask) for i in range(count)])]
    pallas_call x6, Pallas kernels: 8.74 us -> 7.12 us  [add_phase(): pl.pallas_call(kernel, in_specs=[VMEM] * 2 + [UNREAD] * len(after), out_s...]
    unnamed x57 -> x59, local copies, waits for them, and re-layouts: 2.46 us -> 3.4 us
  transfers between devices with their start and end apart: 25 -> 25, of which waited for: 12 -> 11; matrix products, arithmetic and copies ran while one was open for 1% -> 1% of each run, Pallas kernels for 26% -> 25%
where the time goes in v5:
time: 127 us
  Pallas kernels  57 us (45%)
  starting transfers between devices  33.4 us (26%)
  waiting for transfers between devices  30.2 us (24%)
  local copies, waits for them, and re-layouts  4.01 us (3%)
  between operations  1.83 us (1%)
    ppermute x24, starting transfers between devices, swap(): return lax.ppermute(block, 'mp', [(i, i ^ mask) for i in range(count)])  31.9 us
    ppermute x24, waiting for transfers between devices, swap(): return lax.ppermute(block, 'mp', [(i, i ^ mask) for i in range(count)])  30.2 us
    pallas_call x1, Pallas kernels, pick_phase(): pl.pallas_call(kernel, in_specs=[SMEM, VMEM, pl.BlockSpec(memory_space=pl...  9.54 us
    pallas_call x1, Pallas kernels, mixed_grad_phase(): pl.pallas_call(kernel, in_specs=[SMEM, SMEM, VMEM, HBM, VMEM, VMEM], out_...  7.53 us
    pallas_call x6, Pallas kernels, add_phase(): pl.pallas_call(kernel, in_specs=[VMEM] * 2 + [UNREAD] * len(after), out_s...  7.12 us
    pallas_call x1, Pallas kernels, mix_phase(): pl.pallas_call(kernel, in_specs=[SMEM, SMEM] + [VMEM] * (2 + crossing) +...  7.02 us
    pallas_call x1, Pallas kernels, up_grad_phase(): pl.pallas_call(kernel, in_specs=[VMEM] * (3 + len(received)), out_specs=H...  6.59 us
    pallas_call x1, Pallas kernels, down_grad_phase(): pl.pallas_call(kernel, in_specs=[VMEM] * 2, out_specs=HBM, out_shape=jax....  6.36 us
  transfers between devices with their start and end apart: 25, of which 11 were waited for; matrix products, arithmetic and copies ran while one was open for 1% of the time, Pallas kernels for 25%

profile of v5, /device:TPU:0, one launch (start us, length us, event | category | flops | bytes accessed | tf_op | source)
XLA Modules:
  0.0 126.7 jit_solution(4986026305353486545)
XLA Ops:
  0.7 9.5 %pick_phase.1 = (s32[128,8]{1,0:T(8,128)S(1)}, f32[8,128]{1,0:T(8,128)S(1)}, bf16[256,4096]{1,0:T(8,128)(2,1)S(1)}, bf16[256,4096]{1,0:T(8,128)(2,1)}) custom-call(s32[1]{0:T(128)} %bitcast.me_ref, s32[8,128]{1,0:T(8,128)} %bitcast.7, bf16[2048,4096]{1,0:T(8,128)(2,1)} %vocab_ref.1), custom_call_target="tpu_custom_call" | custom-call | flops 4294967296 | bytes 16777216 | tf_op jit(solution)/shard_map/pick_phase/pallas_call | solution.py:537
  10.2 0.0 copy-start.2
  10.2 1.3 %copy-done.2 = bf16[256,4096]{1,0:T(8,128)(2,1)} copy-done((bf16[256,4096]{1,0:T(8,128)(2,1)}, bf16[256,4096]{1,0:T(8,128)(2,1)S(1)}, u32[]{:S(2)}) %copy-start.2) | copy-done | bytes 2097176
  11.5 0.5 collective-permute-start.19
  12.0 0.1 copy.17.sc
  12.1 0.0 copy-start.20
  12.1 4.1 %up_phase.1 = (f32[128,1024]{1,0:T(8,128)S(1)}, bf16[128,1024]{1,0:T(8,128)(2,1)S(1)}) custom-call(bf16[128,4096]{1,0:T(8,128)(2,1)S(1)} %copy-done.4, bf16[4096,1024]{1,0:T(8,128)(2,1)} %val.1, s32[32,8]{1,0:T(8,128)S(1)} %copy.17.sc, f32[8,128]{1,0:T(8,128)S(1)} %get-tuple-element.81.refs_0_), custom_call_target="tpu_custom_call" | custom-call | flops 1073741824 | bytes 8388608 | tf_op jit(solution)/shard_map/up_phase/pallas_call | solution.py:144
  16.2 0.0 copy-start.13
  16.2 0.0 copy-start.3
  16.2 2.6 %collective-permute-start.16 = (bf16[128,1024]{1,0:T(8,128)(2,1)S(1)}, bf16[128,1024]{1,0:T(8,128)(2,1)S(1)}, u32[]{:S(2)}, u32[]{:S(2)}) collective-permute-start(bf16[128,1024]{1,0:T(8,128)(2,1)S(1)} %get-tuple-element.82.act_ref), channel_id=1, source_target_pairs={{0,2},{1,3},{2,0},{3,1},{4,6},{5,7},{6,4},{7,5},{8,10},{9,11},{10,... | collective-permute-start | bytes 786440 | tf_op jit(solution)/shard_map/ppermute | solution.py:32
  18.8 2.5 %collective-permute-start.18 = (bf16[128,1024]{1,0:T(8,128)(2,1)S(1)}, bf16[128,1024]{1,0:T(8,128)(2,1)S(1)}, u32[]{:S(2)}, u32[]{:S(2)}) collective-permute-start(bf16[128,1024]{1,0:T(8,128)(2,1)S(1)} %get-tuple-element.82.act_ref), channel_id=1, source_target_pairs={{0,8},{1,9},{2,10},{3,11},{4,12},{5,13},{6,14},{7,15},{8,0},{9,1},... | collective-permute-start | bytes 786440 | tf_op jit(solution)/shard_map/ppermute | solution.py:32
  21.3 1.6 %collective-permute-start.17 = (bf16[128,1024]{1,0:T(8,128)(2,1)S(1)}, bf16[128,1024]{1,0:T(8,128)(2,1)S(1)}, u32[]{:S(2)}, u32[]{:S(2)}) collective-permute-start(bf16[128,1024]{1,0:T(8,128)(2,1)S(1)} %get-tuple-element.82.act_ref), channel_id=1, source_target_pairs={{0,4},{1,5},{2,6},{3,7},{4,0},{5,1},{6,2},{7,3},{8,12},{9,13},{10,... | collective-permute-start | bytes 786440 | tf_op jit(solution)/shard_map/ppermute | solution.py:32
  23.0 1.1 own_mix_phase.1.refs_0_.own_ref
  24.1 1.7 %collective-permute-done.16.refs_1_ = bf16[128,1024]{1,0:T(8,128)(2,1)S(1)} collective-permute-done((bf16[128,1024]{1,0:T(8,128)(2,1)S(1)}, bf16[128,1024]{1,0:T(8,128)(2,1)S(1)}, u32[]{:S(2)}, u32[]{:S(2)}) %collective-permute-start.16) | collective-permute-done | bytes 262176 | tf_op jit(solution)/shard_map/ppermute | solution.py:32
  25.8 1.8 %add_phase.10.refs_0_ = bf16[64,4096]{1,0:T(8,128)(2,1)S(1)} custom-call(bf16[256,4096]{1,0:T(8,128)(2,1)S(1)} %copy-done.3, bf16[256,4096]{1,0:T(8,128)(2,1)} %collective-permute-done.19.b, f32[128,1024]{1,0:T(8,128)S(1)} %own_mix_phase.1.refs_0_.own_ref, bf16[128,1024]{1,0:T(8,128)(2,1)S(1)} %collective-permute-done.16.refs_1_), custom_call_target="tpu_custom_call" | custom-call | tf_op jit(solution)/shard_map/add_phase/pallas_call | solution.py:282
  27.6 0.0 copy-start.21
  27.6 1.8 %collective-permute-start.21 = (bf16[64,4096]{1,0:T(8,128)(2,1)S(1)}, bf16[64,4096]{1,0:T(8,128)(2,1)S(1)}, u32[]{:S(2)}, u32[]{:S(2)}) collective-permute-start(bf16[64,4096]{1,0:T(8,128)(2,1)S(1)} %add_phase.10.refs_0_), channel_id=1, source_target_pairs={{0,2},{1,3},{2,0},{3,1},{4,6},{5,7},{6,4},{7,5},{8,10},{9,11},{10,... | collective-permute-start | bytes 1572872 | tf_op jit(solution)/shard_map/ppermute | solution.py:32
  29.4 2.6 %add_phase.11 = (bf16[64,4096]{1,0:T(8,128)(2,1)S(1)}, bf16[64,4096]{1,0:T(8,128)(2,1)S(1)}, bf16[64,4096]{1,0:T(8,128)(2,1)}) custom-call(bf16[256,4096]{1,0:T(8,128)(2,1)S(1)} %copy-done.3, bf16[256,4096]{1,0:T(8,128)(2,1)} %collective-permute-done.19.b, bf16[64,4096]{1,0:T(8,128)(2,1)S(1)} %add_phase.10.refs_0_), custom_call_target="tpu_custom_call" | custom-call | tf_op jit(solution)/shard_map/add_phase/pallas_call | solution.py:282
  31.9 1.9 %collective-permute-done.18.refs_3_ = bf16[128,1024]{1,0:T(8,128)(2,1)S(1)} collective-permute-done((bf16[128,1024]{1,0:T(8,128)(2,1)S(1)}, bf16[128,1024]{1,0:T(8,128)(2,1)S(1)}, u32[]{:S(2)}, u32[]{:S(2)}) %collective-permute-start.18) | collective-permute-done | bytes 262176 | tf_op jit(solution)/shard_map/ppermute | solution.py:32
  33.9 0.1 collective-permute-done.17.refs_2_
  34.0 7.0 %mix_phase.1 = (bf16[128,1024]{1,0:T(8,128)(2,1)S(1)}, bf16[64,4096]{1,0:T(8,128)(2,1)S(1)}, bf16[64,4096]{1,0:T(8,128)(2,1)S(1)}) custom-call(s32[1]{0:T(128)} %bitcast.me_ref, s32[7,8]{1,0:T(8,128)S(1)} %copy-done.20, f32[128,1024]{1,0:T(8,128)S(1)} %own_mix_phase.1.refs_0_.own_ref, bf16[128,1024]{1,0:T(8,128)(2,1)S(1)} %collective-permute-done.15.refs_0_, ...), custom_call_target="tpu_custom_call" | custom-call | flops 1073741824 | bytes 8388608 | tf_op jit(solution)/shard_map/mix_phase/pallas_call | solution.py:254
  41.1 0.1 collective-permute-start.20
  41.1 0.6 collective-permute-start.27
  41.8 0.1 add_phase.12
  41.9 2.3 %collective-permute-start.23 = (bf16[32,4096]{1,0:T(8,128)(2,1)S(1)}, bf16[32,4096]{1,0:T(8,128)(2,1)S(1)}, u32[]{:S(2)}, u32[]{:S(2)}) collective-permute-start(bf16[32,4096]{1,0:T(8,128)(2,1)S(1)} %get-tuple-element.89.refs_0_), channel_id=1, source_target_pairs={{0,8},{1,9},{2,10},{3,11},{4,12},{5,13},{6,14},{7,15},{8,0},{9,1},... | collective-permute-start | bytes 786440 | tf_op jit(solution)/shard_map/ppermute | solution.py:32
  44.2 0.8 add_phase.13
  45.0 0.7 copy-done.15
  45.7 1.4 %collective-permute-start.22 = (bf16[32,4096]{1,0:T(8,128)(2,1)}, bf16[32,4096]{1,0:T(8,128)(2,1)S(1)}, u32[]{:S(2)}, u32[]{:S(2)}) collective-permute-start(bf16[32,4096]{1,0:T(8,128)(2,1)} %get-tuple-element.92), channel_id=1, source_target_pairs={{0,2},{1,3},{2,0},{3,1},{4,6},{5,7},{6,4},{7,5},{8,10},{9,11},{10,... | collective-permute-start | bytes 786440 | tf_op jit(solution)/shard_map/ppermute | solution.py:32
  47.1 1.6 %collective-permute-start.14 = (f32[8,128]{1,0:T(8,128)S(1)}, f32[8,128]{1,0:T(8,128)S(1)}, u32[]{:S(2)}, u32[]{:S(2)}) collective-permute-start(f32[8,128]{1,0:T(8,128)S(1)} %get-tuple-element.81.refs_0_), channel_id=1, source_target_pairs={{0,16},{16,0},{1,17},{17,1},{2,18},{18,2},{3,19},{19,3},{4,20},{20... | collective-permute-start | bytes 12296 | tf_op jit(solution)/shard_map/ppermute | solution.py:855
  48.7 1.6 %collective-permute-start.29 = (bf16[32,4096]{1,0:T(8,128)(2,1)}, bf16[32,4096]{1,0:T(8,128)(2,1)}, u32[]{:S(2)}, u32[]{:S(2)}) collective-permute-start(bf16[32,4096]{1,0:T(8,128)(2,1)} %copy-done.17), channel_id=1, source_target_pairs={{0,12},{1,13},{2,14},{3,15},{4,8},{5,9},{6,10},{7,11},{8,4},{9,5},... | collective-permute-start | bytes 786440 | tf_op jit(solution)/shard_map/ppermute | solution.py:32
  50.3 6.0 %collective-permute-done.27.b = bf16[64,4096]{1,0:T(8,128)(2,1)} collective-permute-done((bf16[64,4096]{1,0:T(8,128)(2,1)}, bf16[64,4096]{1,0:T(8,128)(2,1)}, u32[]{:S(2)}, u32[]{:S(2)}) %collective-permute-start.27) | collective-permute-done | bytes 524320 | tf_op jit(solution)/shard_map/ppermute | solution.py:32
  56.3 1.8 %add_phase.15 = (bf16[32,4096]{1,0:T(8,128)(2,1)S(1)}, bf16[32,4096]{1,0:T(8,128)(2,1)}) custom-call(bf16[64,4096]{1,0:T(8,128)(2,1)S(1)} %get-tuple-element.97.a, bf16[64,4096]{1,0:T(8,128)(2,1)} %collective-permute-done.27.b, bf16[32,4096]{1,0:T(8,128)(2,1)S(1)} %get-tuple-element.89.refs_0_), custom_call_target="tpu_custom_call" | custom-call | tf_op jit(solution)/shard_map/add_phase/pallas_call | solution.py:282
  58.1 1.4 %collective-permute-start.28 = (bf16[32,4096]{1,0:T(8,128)(2,1)}, bf16[32,4096]{1,0:T(8,128)(2,1)S(1)}, u32[]{:S(2)}, u32[]{:S(2)}) collective-permute-start(bf16[32,4096]{1,0:T(8,128)(2,1)} %get-tuple-element.99), channel_id=1, source_target_pairs={{0,4},{1,5},{2,6},{3,7},{4,0},{5,1},{6,2},{7,3},{8,12},{9,13},{10,... | collective-permute-start | bytes 786440 | tf_op jit(solution)/shard_map/ppermute | solution.py:32
  59.5 3.7 %collective-permute-done.23.refs_0_.refs_6_ = bf16[32,4096]{1,0:T(8,128)(2,1)S(1)} collective-permute-done((bf16[32,4096]{1,0:T(8,128)(2,1)S(1)}, bf16[32,4096]{1,0:T(8,128)(2,1)S(1)}, u32[]{:S(2)}, u32[]{:S(2)}) %collective-permute-start.23) | collective-permute-done | bytes 262176 | tf_op jit(solution)/shard_map/ppermute | solution.py:32
  63.3 0.1 add_phase.14
  63.3 0.1 collective-permute-start.24
  63.4 2.0 %collective-permute-start.25 = (bf16[8,4096]{1,0:T(8,128)(2,1)S(1)}, bf16[8,4096]{1,0:T(8,128)(2,1)S(1)}, u32[]{:S(2)}, u32[]{:S(2)}) collective-permute-start(bf16[8,4096]{1,0:T(8,128)(2,1)S(1)} %get-tuple-element.95), channel_id=1, source_target_pairs={{0,8},{1,9},{2,10},{3,11},{4,12},{5,13},{6,14},{7,15},{8,0},{9,1},... | collective-permute-start | bytes 196616 | tf_op jit(solution)/shard_map/ppermute | solution.py:32
  65.5 2.3 %collective-permute-start.26 = (bf16[8,4096]{1,0:T(8,128)(2,1)S(1)}, bf16[8,4096]{1,0:T(8,128)(2,1)S(1)}, u32[]{:S(2)}, u32[]{:S(2)}) collective-permute-start(bf16[8,4096]{1,0:T(8,128)(2,1)S(1)} %get-tuple-element.96), channel_id=1, source_target_pairs={{0,12},{1,13},{2,14},{3,15},{4,8},{5,9},{6,10},{7,11},{8,4},{9,5},... | collective-permute-start | bytes 196616 | tf_op jit(solution)/shard_map/ppermute | solution.py:32
  67.8 0.1 copy.18.refs_10_
  67.9 0.1 copy.19.refs_12_
  68.0 0.5 slice.3
  69.2 2.4 %collective-permute-done.24.refs_1_ = bf16[8,4096]{1,0:T(8,128)(2,1)S(1)} collective-permute-done((bf16[8,4096]{1,0:T(8,128)(2,1)S(1)}, bf16[8,4096]{1,0:T(8,128)(2,1)S(1)}, u32[]{:S(2)}, u32[]{:S(2)}) %collective-permute-start.24) | collective-permute-done | bytes 65568 | tf_op jit(solution)/shard_map/ppermute | solution.py:32
  71.6 1.4 %collective-permute-done.25.refs_2_ = bf16[8,4096]{1,0:T(8,128)(2,1)S(1)} collective-permute-done((bf16[8,4096]{1,0:T(8,128)(2,1)S(1)}, bf16[8,4096]{1,0:T(8,128)(2,1)S(1)}, u32[]{:S(2)}, u32[]{:S(2)}) %collective-permute-start.25) | collective-permute-done | bytes 65568 | tf_op jit(solution)/shard_map/ppermute | solution.py:32
  73.1 0.9 copy-done.19
  74.0 2.3 %token_phase.1 = bf16[8,4224]{1,0:T(8,128)(2,1)S(1)} custom-call(s32[1]{0:T(128)} %bitcast.me_ref, bf16[8,4096]{1,0:T(8,128)(2,1)S(1)} %get-tuple-element.93.refs_0_, bf16[8,4096]{1,0:T(8,128)(2,1)S(1)} %collective-permute-done.24.refs_1_, bf16[8,4096]{1,0:T(8,128)(2,1)S(1)} %collective-permute-done.25.refs_2_, ...), custom_call_target="tpu_custom_call" | custom-call | tf_op jit(solution)/shard_map/token_phase/pallas_call | solution.py:609
  76.3 0.2 conditional.1
  76.5 1.6 %collective-permute-start.32 = (bf16[8,4224]{1,0:T(8,128)(2,1)S(1)}, bf16[8,4224]{1,0:T(8,128)(2,1)S(1)}, u32[]{:S(2)}, u32[]{:S(2)}) collective-permute-start(bf16[8,4224]{1,0:T(8,128)(2,1)S(1)} %get-tuple-element.142), channel_id=1, source_target_pairs={{0,12},{1,13},{2,14},{3,15},{4,8},{5,9},{6,10},{7,11},{8,4},{9,5},... | collective-permute-start | bytes 202760 | tf_op jit(solution)/shard_map/ppermute | solution.py:32
  78.1 1.2 collective-permute-start.31
  79.3 1.7 %collective-permute-start.30 = (bf16[8,4224]{1,0:T(8,128)(2,1)S(1)}, bf16[8,4224]{1,0:T(8,128)(2,1)S(1)}, u32[]{:S(2)}, u32[]{:S(2)}) collective-permute-start(bf16[8,4224]{1,0:T(8,128)(2,1)S(1)} %get-tuple-element.142), channel_id=1, source_target_pairs={{0,4},{1,5},{2,6},{3,7},{4,0},{5,1},{6,2},{7,3},{8,12},{9,13},{10,... | collective-permute-start | bytes 202760 | tf_op jit(solution)/shard_map/ppermute | solution.py:32
  80.9 2.5 %collective-permute-done.32 = bf16[8,4224]{1,0:T(8,128)(2,1)S(1)} collective-permute-done((bf16[8,4224]{1,0:T(8,128)(2,1)S(1)}, bf16[8,4224]{1,0:T(8,128)(2,1)S(1)}, u32[]{:S(2)}, u32[]{:S(2)}) %collective-permute-start.32) | collective-permute-done | bytes 67616 | tf_op jit(solution)/shard_map/ppermute | solution.py:32
  83.4 1.8 %collective-permute-done.31 = bf16[8,4224]{1,0:T(8,128)(2,1)S(1)} collective-permute-done((bf16[8,4224]{1,0:T(8,128)(2,1)S(1)}, bf16[8,4224]{1,0:T(8,128)(2,1)S(1)}, u32[]{:S(2)}, u32[]{:S(2)}) %collective-permute-start.31) | collective-permute-done | bytes 67616 | tf_op jit(solution)/shard_map/ppermute | solution.py:32
  85.2 1.5 %collective-permute-start.33 = (bf16[32,4224]{1,0:T(8,128)(2,1)S(1)}, bf16[32,4224]{1,0:T(8,128)(2,1)S(1)}, u32[]{:S(2)}, u32[]{:S(2)}) collective-permute-start(bf16[32,4224]{1,0:T(8,128)(2,1)S(1)} %pad_maximum_fusion.1), channel_id=1, source_target_pairs={{0,2},{1,3},{2,0},{3,1},{4,6},{5,7},{6,4},{7,5},{8,10},{9,11},{10,... | collective-permute-start | bytes 811016 | tf_op jit(solution)/shard_map/ppermute | solution.py:32
  86.8 6.6 %collective-permute-done.33 = bf16[32,4224]{1,0:T(8,128)(2,1)S(1)} collective-permute-done((bf16[32,4224]{1,0:T(8,128)(2,1)S(1)}, bf16[32,4224]{1,0:T(8,128)(2,1)S(1)}, u32[]{:S(2)}, u32[]{:S(2)}) %collective-permute-start.33) | collective-permute-done | bytes 270368 | tf_op jit(solution)/shard_map/ppermute | solution.py:32
  93.4 0.1 collective-permute-start.34
  93.5 1.9 %collective-permute-done.34 = bf16[64,4224]{1,0:T(8,128)(2,1)S(1)} collective-permute-done((bf16[64,4224]{1,0:T(8,128)(2,1)S(1)}, bf16[64,4224]{1,0:T(8,128)(2,1)S(1)}, u32[]{:S(2)}, u32[]{:S(2)}) %collective-permute-start.34) | collective-permute-done | bytes 540704 | tf_op jit(solution)/shard_map/ppermute | solution.py:32
  95.5 7.5 %mixed_grad_phase.1 = (f32[1,1]{1,0:T(1,128)}, bf16[128,1024]{1,0:T(8,128)(2,1)S(1)}, bf16[128,1024]{1,0:T(8,128)(2,1)S(1)}, bf16[128,1024]{1,0:T(8,128)(2,1)S(1...) custom-call(s32[1]{0:T(128)} %bitcast.me_ref, s32[7,8]{1,0:T(8,128)S(1)} %copy-done.20, ...), custom_call_target="tpu_custom_call" | custom-call | flops 1073741824 | bytes 8388608 | tf_op jit(solution)/shard_map/mixed_grad_phase/pallas_call | solution.py:669
  103.1 0.2 collective-permute-start.35
  103.3 1.2 collective-permute-start.36
  104.5 0.1 collective-permute-start.37
  104.6 3.4 %collective-permute-start.38 = (bf16[128,1024]{1,0:T(8,128)(2,1)S(1)}, bf16[128,1024]{1,0:T(8,128)(2,1)S(1)}, u32[]{:S(2)}, u32[]{:S(2)}) collective-permute-start(bf16[128,1024]{1,0:T(8,128)(2,1)S(1)} %get-tuple-element.108), channel_id=1, source_target_pairs={{0,8},{1,9},{2,10},{3,11},{4,12},{5,13},{6,14},{7,15},{8,0},{9,1},... | collective-permute-start | bytes 786440 | tf_op jit(solution)/shard_map/ppermute | solution.py:32
  108.0 5.5 %block_grad_phase.1 = (f32[8,128,128]{2,1,0:T(8,128)}, f32[7,8,128,128]{3,2,1,0:T(8,128)}, f32[128,1024]{1,0:T(8,128)S(1)}) custom-call(s32[7,8]{1,0:T(8,128)S(1)} %copy-done.20, bf16[128,1024]{1,0:T(8,128)(2,1)S(1)} %copy-done.12, bf16[128,1024]{1,0:T(8,128)(2,1)S(1)} %get-tuple-element.103.mg, bf16[128,1024]{1,0:T(8,128)(2,1)S(1)} %copy-done.8, ...), custom_call_target="tpu_custom_call" | custom-call | flops 402653184 | bytes 12582912 | tf_op jit(solution)/shard_map/block_grad_phase/pallas_call | solution.py:714
  113.5 6.4 %down_grad_phase.1 = f32[1024,4096]{1,0:T(8,128)} custom-call(bf16[128,1024]{1,0:T(8,128)(2,1)S(1)} %get-tuple-element.109.mixed_ref, bf16[128,4224]{1,0:T(8,128)(2,1)S(1)} %constant_dynamic-update-slice_fusion.16.grad_ref), custom_call_target="tpu_custom_call" | custom-call | flops 1073741824 | bytes 16777216 | tf_op jit(solution)/shard_map/down_grad_phase/pallas_call | solution.py:756
  119.9 0.0 collective-permute-done.38.refs_3_
  119.9 6.6 %up_grad_phase.1 = f32[4096,1024]{1,0:T(8,128)} custom-call(bf16[128,4096]{1,0:T(8,128)(2,1)S(1)} %copy-done.4, f32[128,1024]{1,0:T(8,128)S(1)} %copy-done.14, f32[128,1024]{1,0:T(8,128)S(1)} %get-tuple-element.104.grad_ref, bf16[128,1024]{1,0:T(8,128)(2,1)S(1)} %collective-permute-done.35.refs_0_, bf16[128,1024]{1,0:T(8,128)(2,1)S(1)} %collective-permute-done.36.refs_1_, ...), custom_call_target="tpu_custom_call" | custom-call | flops 1073741824 | bytes 16777216 | tf_op jit(solution)/shard_map/up_grad_phase/pallas_call | solution.py:800
  (67 shorter events, 0.3 us)
Async XLA Ops:
  0.6 11.3 %copy-start.27 = (s32[32,8]{0,1:T(8,128)S(1)}, s32[32,8]{0,1:T(8,128)}, u32[]{:S(2)}) copy-start(s32[32,8]{0,1:T(8,128)} %param.16) | copy-start | bytes 3076
  0.6 11.4 %copy-start.4 = (bf16[128,4096]{1,0:T(8,128)(2,1)S(1)}, bf16[128,4096]{1,0:T(8,128)(2,1)}, u32[]{:S(2)}) copy-start(bf16[128,4096]{1,0:T(8,128)(2,1)} %tok.3) | copy-start | bytes 3145732
  10.2 1.3 %copy-start.2 = (bf16[256,4096]{1,0:T(8,128)(2,1)}, bf16[256,4096]{1,0:T(8,128)(2,1)S(1)}, u32[]{:S(2)}) copy-start(bf16[256,4096]{1,0:T(8,128)(2,1)S(1)} %get-tuple-element.83.a) | copy-start | bytes 6291460
  11.5 14.3 %collective-permute-start.19 = (bf16[256,4096]{1,0:T(8,128)(2,1)}, bf16[256,4096]{1,0:T(8,128)(2,1)}, u32[]{:S(2)}, u32[]{:S(2)}) collective-permute-start(bf16[256,4096]{1,0:T(8,128)(2,1)} %get-tuple-element.84), channel_id=1, source_target_pairs={{0,1},{1,0},{2,3},{3,2},{4,5},{5,4},{6,7},{7,6},{8,9},{9,8},{10,11... | collective-permute-start | bytes 6291464 | tf_op jit(solution)/shard_map/ppermute | solution.py:32
  12.1 10.9 %copy-start = (bf16[7,8,128,128]{3,2,1,0:T(8,128)(2,1)S(1)}, bf16[7,8,128,128]{3,2,1,0:T(8,128)(2,1)}, u32[]{:S(2)}) copy-start(bf16[7,8,128,128]{3,2,1,0:T(8,128)(2,1)} %refs_5_.3) | copy-start | bytes 5505028
  12.1 10.9 %copy-start.9 = (bf16[8,128,128]{2,1,0:T(8,128)(2,1)S(1)}, bf16[8,128,128]{2,1,0:T(8,128)(2,1)}, u32[]{:S(2)}) copy-start(bf16[8,128,128]{2,1,0:T(8,128)(2,1)} %refs_4_.3) | copy-start | bytes 786436
  12.1 10.9 %copy-start.20 = (s32[7,8]{1,0:T(8,128)S(1)}, s32[7,8]{1,0:T(8,128)}, u32[]{:S(2)}) copy-start(s32[7,8]{1,0:T(8,128)} %pat.7) | copy-start | bytes 676
  16.2 7.9 %copy-start.11 = (bf16[128,1024]{1,0:T(8,128)(2,1)}, bf16[128,1024]{1,0:T(8,128)(2,1)S(1)}, u32[]{:S(2)}) copy-start(bf16[128,1024]{1,0:T(8,128)(2,1)S(1)} %get-tuple-element.82.act_ref) | copy-start | bytes 786436
  16.2 7.9 %copy-start.13 = (f32[128,1024]{1,0:T(8,128)}, f32[128,1024]{1,0:T(8,128)S(1)}, u32[]{:S(2)}) copy-start(f32[128,1024]{1,0:T(8,128)S(1)} %get-tuple-element.102.pre_ref) | copy-start | bytes 1572868
  16.2 9.6 %copy-start.3 = (bf16[256,4096]{1,0:T(8,128)(2,1)S(1)}, bf16[256,4096]{1,0:T(8,128)(2,1)}, u32[]{:S(2)}) copy-start(bf16[256,4096]{1,0:T(8,128)(2,1)} %copy-done.2) | copy-start | bytes 6291460
  16.2 9.6 %collective-permute-start.16 = (bf16[128,1024]{1,0:T(8,128)(2,1)S(1)}, bf16[128,1024]{1,0:T(8,128)(2,1)S(1)}, u32[]{:S(2)}, u32[]{:S(2)}) collective-permute-start(bf16[128,1024]{1,0:T(8,128)(2,1)S(1)} %get-tuple-element.82.act_ref), channel_id=1, source_target_pairs={{0,2},{1,3},{2,0},{3,1},{4,6},{5,7},{6,4},{7,5},{8,10},{9,11},{10,... | collective-permute-start | bytes 786440 | tf_op jit(solution)/shard_map/ppermute | solution.py:32
  18.8 15.1 %collective-permute-start.18 = (bf16[128,1024]{1,0:T(8,128)(2,1)S(1)}, bf16[128,1024]{1,0:T(8,128)(2,1)S(1)}, u32[]{:S(2)}, u32[]{:S(2)}) collective-permute-start(bf16[128,1024]{1,0:T(8,128)(2,1)S(1)} %get-tuple-element.82.act_ref), channel_id=1, source_target_pairs={{0,8},{1,9},{2,10},{3,11},{4,12},{5,13},{6,14},{7,15},{8,0},{9,1},... | collective-permute-start | bytes 786440 | tf_op jit(solution)/shard_map/ppermute | solution.py:32
  21.3 12.7 %collective-permute-start.17 = (bf16[128,1024]{1,0:T(8,128)(2,1)S(1)}, bf16[128,1024]{1,0:T(8,128)(2,1)S(1)}, u32[]{:S(2)}, u32[]{:S(2)}) collective-permute-start(bf16[128,1024]{1,0:T(8,128)(2,1)S(1)} %get-tuple-element.82.act_ref), channel_id=1, source_target_pairs={{0,4},{1,5},{2,6},{3,7},{4,0},{5,1},{6,2},{7,3},{8,12},{9,13},{10,... | collective-permute-start | bytes 786440 | tf_op jit(solution)/shard_map/ppermute | solution.py:32
  23.0 11.0 %collective-permute-start.15 = (bf16[128,1024]{1,0:T(8,128)(2,1)S(1)}, bf16[128,1024]{1,0:T(8,128)(2,1)S(1)}, u32[]{:S(2)}, u32[]{:S(2)}) collective-permute-start(bf16[128,1024]{1,0:T(8,128)(2,1)S(1)} %get-tuple-element.82.act_ref), channel_id=1, source_target_pairs={{0,1},{1,0},{2,3},{3,2},{4,5},{5,4},{6,7},{7,6},{8,9},{9,8},{10,11... | collective-permute-start | bytes 786440 | tf_op jit(solution)/shard_map/ppermute | solution.py:32
  27.6 6.5 %copy-start.21 = (s32[8,32]{1,0:T(8,128)S(1)}, s32[8,32]{1,0:T(8,128)}, u32[]{:S(2)}) copy-start(s32[8,32]{1,0:T(8,128)} %sc.2) | copy-start | bytes 3076
  27.6 14.2 %collective-permute-start.21 = (bf16[64,4096]{1,0:T(8,128)(2,1)S(1)}, bf16[64,4096]{1,0:T(8,128)(2,1)S(1)}, u32[]{:S(2)}, u32[]{:S(2)}) collective-permute-start(bf16[64,4096]{1,0:T(8,128)(2,1)S(1)} %add_phase.10.refs_0_), channel_id=1, source_target_pairs={{0,2},{1,3},{2,0},{3,1},{4,6},{5,7},{6,4},{7,5},{8,10},{9,11},{10,... | collective-permute-start | bytes 1572872 | tf_op jit(solution)/shard_map/ppermute | solution.py:32
  34.0 7.0 %copy-start.5 = (bf16[128,1024]{1,0:T(8,128)(2,1)}, bf16[128,1024]{1,0:T(8,128)(2,1)S(1)}, u32[]{:S(2)}) copy-start(bf16[128,1024]{1,0:T(8,128)(2,1)S(1)} %collective-permute-done.17.refs_2_) | copy-start | bytes 786436
  34.0 7.0 %copy-start.7 = (bf16[128,1024]{1,0:T(8,128)(2,1)}, bf16[128,1024]{1,0:T(8,128)(2,1)S(1)}, u32[]{:S(2)}) copy-start(bf16[128,1024]{1,0:T(8,128)(2,1)S(1)} %collective-permute-done.15.refs_0_) | copy-start | bytes 786436
  41.1 3.1 %collective-permute-start.20 = (bf16[64,4096]{1,0:T(8,128)(2,1)S(1)}, bf16[64,4096]{1,0:T(8,128)(2,1)S(1)}, u32[]{:S(2)}, u32[]{:S(2)}) collective-permute-start(bf16[64,4096]{1,0:T(8,128)(2,1)S(1)} %get-tuple-element.87), channel_id=1, source_target_pairs={{0,1},{1,0},{2,3},{3,2},{4,5},{5,4},{6,7},{7,6},{8,9},{9,8},{10,11... | collective-permute-start | bytes 1572872 | tf_op jit(solution)/shard_map/ppermute | solution.py:32
  41.1 15.1 %collective-permute-start.27 = (bf16[64,4096]{1,0:T(8,128)(2,1)}, bf16[64,4096]{1,0:T(8,128)(2,1)}, u32[]{:S(2)}, u32[]{:S(2)}) collective-permute-start(bf16[64,4096]{1,0:T(8,128)(2,1)} %get-tuple-element.85.refs_7_), channel_id=1, source_target_pairs={{0,2},{1,3},{2,0},{3,1},{4,6},{5,7},{6,4},{7,5},{8,10},{9,11},{10,... | collective-permute-start | bytes 1572872 | tf_op jit(solution)/shard_map/ppermute | solution.py:32
  41.9 3.1 %copy-start.17 = (bf16[32,4096]{1,0:T(8,128)(2,1)}, bf16[32,4096]{1,0:T(8,128)(2,1)S(1)}, u32[]{:S(2)}) copy-start(bf16[32,4096]{1,0:T(8,128)(2,1)S(1)} %get-tuple-element.90.refs_1_) | copy-start | bytes 786436
  41.9 21.4 %collective-permute-start.23 = (bf16[32,4096]{1,0:T(8,128)(2,1)S(1)}, bf16[32,4096]{1,0:T(8,128)(2,1)S(1)}, u32[]{:S(2)}, u32[]{:S(2)}) collective-permute-start(bf16[32,4096]{1,0:T(8,128)(2,1)S(1)} %get-tuple-element.89.refs_0_), channel_id=1, source_target_pairs={{0,8},{1,9},{2,10},{3,11},{4,12},{5,13},{6,14},{7,15},{8,0},{9,1},... | collective-permute-start | bytes 786440 | tf_op jit(solution)/shard_map/ppermute | solution.py:32
  45.0 0.7 copy-start.15
  45.7 17.6 %copy-start.16 = (bf16[32,4096]{1,0:T(8,128)(2,1)S(1)}, bf16[32,4096]{1,0:T(8,128)(2,1)}, u32[]{:S(2)}) copy-start(bf16[32,4096]{1,0:T(8,128)(2,1)} %copy-done.15) | copy-start | bytes 786436
  45.7 17.6 %collective-permute-start.22 = (bf16[32,4096]{1,0:T(8,128)(2,1)}, bf16[32,4096]{1,0:T(8,128)(2,1)S(1)}, u32[]{:S(2)}, u32[]{:S(2)}) collective-permute-start(bf16[32,4096]{1,0:T(8,128)(2,1)} %get-tuple-element.92), channel_id=1, source_target_pairs={{0,2},{1,3},{2,0},{3,1},{4,6},{5,7},{6,4},{7,5},{8,10},{9,11},{10,... | collective-permute-start | bytes 786440 | tf_op jit(solution)/shard_map/ppermute | solution.py:32
  47.1 18.3 %collective-permute-start.14 = (f32[8,128]{1,0:T(8,128)S(1)}, f32[8,128]{1,0:T(8,128)S(1)}, u32[]{:S(2)}, u32[]{:S(2)}) collective-permute-start(f32[8,128]{1,0:T(8,128)S(1)} %get-tuple-element.81.refs_0_), channel_id=1, source_target_pairs={{0,16},{16,0},{1,17},{17,1},{2,18},{18,2},{3,19},{19,3},{4,20},{20... | collective-permute-start | bytes 12296 | tf_op jit(solution)/shard_map/ppermute | solution.py:855
  48.7 24.4 %collective-permute-start.29 = (bf16[32,4096]{1,0:T(8,128)(2,1)}, bf16[32,4096]{1,0:T(8,128)(2,1)}, u32[]{:S(2)}, u32[]{:S(2)}) collective-permute-start(bf16[32,4096]{1,0:T(8,128)(2,1)} %copy-done.17), channel_id=1, source_target_pairs={{0,12},{1,13},{2,14},{3,15},{4,8},{5,9},{6,10},{7,11},{8,4},{9,5},... | collective-permute-start | bytes 786440 | tf_op jit(solution)/shard_map/ppermute | solution.py:32
  56.2 11.6 %copy-start.25 = (s32[128,8]{0,1:T(8,128)S(1)}, s32[128,8]{0,1:T(8,128)}, u32[]{:S(2)}) copy-start(s32[128,8]{0,1:T(8,128)} %param.24) | copy-start | bytes 12292
  56.3 11.7 %copy-start.26 = (f32[128,8]{0,1:T(8,128)S(1)}, f32[128,8]{0,1:T(8,128)}, u32[]{:S(2)}) copy-start(f32[128,8]{0,1:T(8,128)} %param.25) | copy-start | bytes 12292
  56.3 16.8 %copy-start.22 = (f32[4096]{0:T(1024)S(1)}, f32[4096]{0:T(1024)}, u32[]{:S(2)}) copy-start(f32[4096]{0:T(1024)} %param.22) | copy-start | bytes 49156
  58.1 9.7 %copy-start.18 = (bf16[32,4096]{1,0:T(8,128)(2,1)}, bf16[32,4096]{1,0:T(8,128)(2,1)S(1)}, u32[]{:S(2)}) copy-start(bf16[32,4096]{1,0:T(8,128)(2,1)S(1)} %get-tuple-element.98.refs_4_) | copy-start | bytes 786436
  58.1 14.9 %collective-permute-start.28 = (bf16[32,4096]{1,0:T(8,128)(2,1)}, bf16[32,4096]{1,0:T(8,128)(2,1)S(1)}, u32[]{:S(2)}, u32[]{:S(2)}) collective-permute-start(bf16[32,4096]{1,0:T(8,128)(2,1)} %get-tuple-element.99), channel_id=1, source_target_pairs={{0,4},{1,5},{2,6},{3,7},{4,0},{5,1},{6,2},{7,3},{8,12},{9,13},{10,... | collective-permute-start | bytes 786440 | tf_op jit(solution)/shard_map/ppermute | solution.py:32
  63.3 8.3 %collective-permute-start.24 = (bf16[8,4096]{1,0:T(8,128)(2,1)S(1)}, bf16[8,4096]{1,0:T(8,128)(2,1)S(1)}, u32[]{:S(2)}, u32[]{:S(2)}) collective-permute-start(bf16[8,4096]{1,0:T(8,128)(2,1)S(1)} %get-tuple-element.94), channel_id=1, source_target_pairs={{0,4},{1,5},{2,6},{3,7},{4,0},{5,1},{6,2},{7,3},{8,12},{9,13},{10,... | collective-permute-start | bytes 196616 | tf_op jit(solution)/shard_map/ppermute | solution.py:32
  63.4 9.6 %collective-permute-start.25 = (bf16[8,4096]{1,0:T(8,128)(2,1)S(1)}, bf16[8,4096]{1,0:T(8,128)(2,1)S(1)}, u32[]{:S(2)}, u32[]{:S(2)}) collective-permute-start(bf16[8,4096]{1,0:T(8,128)(2,1)S(1)} %get-tuple-element.95), channel_id=1, source_target_pairs={{0,8},{1,9},{2,10},{3,11},{4,12},{5,13},{6,14},{7,15},{8,0},{9,1},... | collective-permute-start | bytes 196616 | tf_op jit(solution)/shard_map/ppermute | solution.py:32
  65.5 7.6 %collective-permute-start.26 = (bf16[8,4096]{1,0:T(8,128)(2,1)S(1)}, bf16[8,4096]{1,0:T(8,128)(2,1)S(1)}, u32[]{:S(2)}, u32[]{:S(2)}) collective-permute-start(bf16[8,4096]{1,0:T(8,128)(2,1)S(1)} %get-tuple-element.96), channel_id=1, source_target_pairs={{0,12},{1,13},{2,14},{3,15},{4,8},{5,9},{6,10},{7,11},{8,4},{9,5},... | collective-permute-start | bytes 196616 | tf_op jit(solution)/shard_map/ppermute | solution.py:32
  73.1 1.0 copy-start.19
  76.5 6.9 %collective-permute-start.32 = (bf16[8,4224]{1,0:T(8,128)(2,1)S(1)}, bf16[8,4224]{1,0:T(8,128)(2,1)S(1)}, u32[]{:S(2)}, u32[]{:S(2)}) collective-permute-start(bf16[8,4224]{1,0:T(8,128)(2,1)S(1)} %get-tuple-element.142), channel_id=1, source_target_pairs={{0,12},{1,13},{2,14},{3,15},{4,8},{5,9},{6,10},{7,11},{8,4},{9,5},... | collective-permute-start | bytes 202760 | tf_op jit(solution)/shard_map/ppermute | solution.py:32
  78.1 7.1 %collective-permute-start.31 = (bf16[8,4224]{1,0:T(8,128)(2,1)S(1)}, bf16[8,4224]{1,0:T(8,128)(2,1)S(1)}, u32[]{:S(2)}, u32[]{:S(2)}) collective-permute-start(bf16[8,4224]{1,0:T(8,128)(2,1)S(1)} %get-tuple-element.142), channel_id=1, source_target_pairs={{0,8},{1,9},{2,10},{3,11},{4,12},{5,13},{6,14},{7,15},{8,0},{9,1},... | collective-permute-start | bytes 202760 | tf_op jit(solution)/shard_map/ppermute | solution.py:32
  79.3 5.9 %collective-permute-start.30 = (bf16[8,4224]{1,0:T(8,128)(2,1)S(1)}, bf16[8,4224]{1,0:T(8,128)(2,1)S(1)}, u32[]{:S(2)}, u32[]{:S(2)}) collective-permute-start(bf16[8,4224]{1,0:T(8,128)(2,1)S(1)} %get-tuple-element.142), channel_id=1, source_target_pairs={{0,4},{1,5},{2,6},{3,7},{4,0},{5,1},{6,2},{7,3},{8,12},{9,13},{10,... | collective-permute-start | bytes 202760 | tf_op jit(solution)/shard_map/ppermute | solution.py:32
  85.2 8.2 %collective-permute-start.33 = (bf16[32,4224]{1,0:T(8,128)(2,1)S(1)}, bf16[32,4224]{1,0:T(8,128)(2,1)S(1)}, u32[]{:S(2)}, u32[]{:S(2)}) collective-permute-start(bf16[32,4224]{1,0:T(8,128)(2,1)S(1)} %pad_maximum_fusion.1), channel_id=1, source_target_pairs={{0,2},{1,3},{2,0},{3,1},{4,6},{5,7},{6,4},{7,5},{8,10},{9,11},{10,... | collective-permute-start | bytes 811016 | tf_op jit(solution)/shard_map/ppermute | solution.py:32
  93.4 2.0 %collective-permute-start.34 = (bf16[64,4224]{1,0:T(8,128)(2,1)S(1)}, bf16[64,4224]{1,0:T(8,128)(2,1)S(1)}, u32[]{:S(2)}, u32[]{:S(2)}) collective-permute-start(bf16[64,4224]{1,0:T(8,128)(2,1)S(1)} %get-tuple-element.132), channel_id=1, source_target_pairs={{0,1},{1,0},{2,3},{3,2},{4,5},{5,4},{6,7},{7,6},{8,9},{9,8},{10,11... | collective-permute-start | bytes 1622024 | tf_op jit(solution)/shard_map/ppermute | solution.py:32
  95.5 12.5 %copy-start.1 = (bf16[7,8,128,128]{3,2,1,0:T(8,128)(2,1)S(1)}, bf16[7,8,128,128]{3,2,1,0:T(8,128)(2,1)}, u32[]{:S(2)}) copy-start(bf16[7,8,128,128]{3,2,1,0:T(8,128)(2,1)} %refs_5_.3) | copy-start | bytes 5505028
  95.5 12.5 %copy-start.6 = (bf16[128,1024]{1,0:T(8,128)(2,1)S(1)}, bf16[128,1024]{1,0:T(8,128)(2,1)}, u32[]{:S(2)}) copy-start(bf16[128,1024]{1,0:T(8,128)(2,1)} %copy-done.5) | copy-start | bytes 786436
  95.5 12.5 %copy-start.8 = (bf16[128,1024]{1,0:T(8,128)(2,1)S(1)}, bf16[128,1024]{1,0:T(8,128)(2,1)}, u32[]{:S(2)}) copy-start(bf16[128,1024]{1,0:T(8,128)(2,1)} %copy-done.7) | copy-start | bytes 786436
  95.5 12.5 %copy-start.10 = (bf16[8,128,128]{2,1,0:T(8,128)(2,1)S(1)}, bf16[8,128,128]{2,1,0:T(8,128)(2,1)}, u32[]{:S(2)}) copy-start(bf16[8,128,128]{2,1,0:T(8,128)(2,1)} %refs_4_.3) | copy-start | bytes 786436
  95.5 12.5 %copy-start.12 = (bf16[128,1024]{1,0:T(8,128)(2,1)S(1)}, bf16[128,1024]{1,0:T(8,128)(2,1)}, u32[]{:S(2)}) copy-start(bf16[128,1024]{1,0:T(8,128)(2,1)} %copy-done.11) | copy-start | bytes 786436
  103.1 16.8 %collective-permute-start.35 = (bf16[128,1024]{1,0:T(8,128)(2,1)S(1)}, bf16[128,1024]{1,0:T(8,128)(2,1)S(1)}, u32[]{:S(2)}, u32[]{:S(2)}) collective-permute-start(bf16[128,1024]{1,0:T(8,128)(2,1)S(1)} %get-tuple-element.105), channel_id=1, source_target_pairs={{0,1},{1,0},{2,3},{3,2},{4,5},{5,4},{6,7},{7,6},{8,9},{9,8},{10,11... | collective-permute-start | bytes 786440 | tf_op jit(solution)/shard_map/ppermute | solution.py:32
  103.3 16.6 %collective-permute-start.36 = (bf16[128,1024]{1,0:T(8,128)(2,1)S(1)}, bf16[128,1024]{1,0:T(8,128)(2,1)S(1)}, u32[]{:S(2)}, u32[]{:S(2)}) collective-permute-start(bf16[128,1024]{1,0:T(8,128)(2,1)S(1)} %get-tuple-element.106), channel_id=1, source_target_pairs={{0,2},{1,3},{2,0},{3,1},{4,6},{5,7},{6,4},{7,5},{8,10},{9,11},{10,... | collective-permute-start | bytes 786440 | tf_op jit(solution)/shard_map/ppermute | solution.py:32
  104.5 15.4 %collective-permute-start.37 = (bf16[128,1024]{1,0:T(8,128)(2,1)S(1)}, bf16[128,1024]{1,0:T(8,128)(2,1)S(1)}, u32[]{:S(2)}, u32[]{:S(2)}) collective-permute-start(bf16[128,1024]{1,0:T(8,128)(2,1)S(1)} %get-tuple-element.107), channel_id=1, source_target_pairs={{0,4},{1,5},{2,6},{3,7},{4,0},{5,1},{6,2},{7,3},{8,12},{9,13},{10,... | collective-permute-start | bytes 786440 | tf_op jit(solution)/shard_map/ppermute | solution.py:32
  104.6 15.3 %collective-permute-start.38 = (bf16[128,1024]{1,0:T(8,128)(2,1)S(1)}, bf16[128,1024]{1,0:T(8,128)(2,1)S(1)}, u32[]{:S(2)}, u32[]{:S(2)}) collective-permute-start(bf16[128,1024]{1,0:T(8,128)(2,1)S(1)} %get-tuple-element.108), channel_id=1, source_target_pairs={{0,8},{1,9},{2,10},{3,11},{4,12},{5,13},{6,14},{7,15},{8,0},{9,1},... | collective-permute-start | bytes 786440 | tf_op jit(solution)/shard_map/ppermute | solution.py:32
  113.5 6.5 %copy-start.14 = (f32[128,1024]{1,0:T(8,128)S(1)}, f32[128,1024]{1,0:T(8,128)}, u32[]{:S(2)}) copy-start(f32[128,1024]{1,0:T(8,128)} %copy-done.13) | copy-start | bytes 1572868

commit v6 on v5

--- a/solution.py
+++ b/solution.py
@@ -896,7 +896,7 @@
     loss, mixed_grad, *outgoing = mixed_grad_phase(
         me, pattern, grad, down_values, down_scale, partner_blocks, rows, groups, local
     )
-    incoming = [swap(block, 1 << n) for n, block in enumerate(outgoing)]
+    incoming = [swap(block, 1 << n) for n, block in reversed(list(enumerate(outgoing)))]
     grad_diag, grad_partner, act_grad = block_grad_phase(
         pattern, act, received, mixed_grad, diag_blocks, partner_blocks
     )

time: 127 us -> 127 us (level)
  no operation moved by 1% of the time
where the time goes in v6:
time: 127 us
  Pallas kernels  57 us (45%)
  starting transfers between devices  33.3 us (26%)
  waiting for transfers between devices  30.1 us (24%)
  local copies, waits for them, and re-layouts  4.01 us (3%)
  between operations  1.86 us (1%)
    ppermute x24, starting transfers between devices, swap(): return lax.ppermute(block, 'mp', [(i, i ^ mask) for i in range(count)])  31.7 us
    ppermute x24, waiting for transfers between devices, swap(): return lax.ppermute(block, 'mp', [(i, i ^ mask) for i in range(count)])  30.1 us
    pallas_call x1, Pallas kernels, pick_phase(): pl.pallas_call(kernel, in_specs=[SMEM, VMEM, pl.BlockSpec(memory_space=pl...  9.54 us
    pallas_call x1, Pallas kernels, mixed_grad_phase(): pl.pallas_call(kernel, in_specs=[SMEM, SMEM, VMEM, HBM, VMEM, VMEM], out_...  7.53 us
    pallas_call x6, Pallas kernels, add_phase(): pl.pallas_call(kernel, in_specs=[VMEM] * 2 + [UNREAD] * len(after), out_s...  7.12 us
    pallas_call x1, Pallas kernels, mix_phase(): pl.pallas_call(kernel, in_specs=[SMEM, SMEM] + [VMEM] * (2 + crossing) +...  7.02 us
    pallas_call x1, Pallas kernels, up_grad_phase(): pl.pallas_call(kernel, in_specs=[VMEM] * (3 + len(received)), out_specs=H...  6.58 us
    pallas_call x1, Pallas kernels, down_grad_phase(): pl.pallas_call(kernel, in_specs=[VMEM] * 2, out_specs=HBM, out_shape=jax....  6.36 us
  transfers between devices with their start and end apart: 25, of which 11 were waited for; matrix products, arithmetic and copies ran while one was open for 1% of the time, Pallas kernels for 25%

profile of v6, /device:TPU:0, one launch (start us, length us, event | category | flops | bytes accessed | tf_op | source)
XLA Modules:
  0.0 126.5 jit_solution(16845234322123512646)
XLA Ops:
  0.7 9.5 %pick_phase.1 = (s32[128,8]{1,0:T(8,128)S(1)}, f32[8,128]{1,0:T(8,128)S(1)}, bf16[256,4096]{1,0:T(8,128)(2,1)S(1)}, bf16[256,4096]{1,0:T(8,128)(2,1)}) custom-call(s32[1]{0:T(128)} %bitcast.me_ref, s32[8,128]{1,0:T(8,128)} %bitcast.7, bf16[2048,4096]{1,0:T(8,128)(2,1)} %vocab_ref.1), custom_call_target="tpu_custom_call" | custom-call | flops 4294967296 | bytes 16777216 | tf_op jit(solution)/shard_map/pick_phase/pallas_call | solution.py:537
  10.2 0.0 copy-start.2
  10.2 1.3 %copy-done.2 = bf16[256,4096]{1,0:T(8,128)(2,1)} copy-done((bf16[256,4096]{1,0:T(8,128)(2,1)}, bf16[256,4096]{1,0:T(8,128)(2,1)S(1)}, u32[]{:S(2)}) %copy-start.2) | copy-done | bytes 2097176
  11.5 0.5 collective-permute-start.19
  12.0 0.1 copy.17.sc
  12.1 0.0 copy-start.20
  12.1 4.1 %up_phase.1 = (f32[128,1024]{1,0:T(8,128)S(1)}, bf16[128,1024]{1,0:T(8,128)(2,1)S(1)}) custom-call(bf16[128,4096]{1,0:T(8,128)(2,1)S(1)} %copy-done.4, bf16[4096,1024]{1,0:T(8,128)(2,1)} %val.1, s32[32,8]{1,0:T(8,128)S(1)} %copy.17.sc, f32[8,128]{1,0:T(8,128)S(1)} %get-tuple-element.81.refs_0_), custom_call_target="tpu_custom_call" | custom-call | flops 1073741824 | bytes 8388608 | tf_op jit(solution)/shard_map/up_phase/pallas_call | solution.py:144
  16.2 0.0 copy-start.13
  16.2 0.0 copy-start.3
  16.2 2.6 %collective-permute-start.16 = (bf16[128,1024]{1,0:T(8,128)(2,1)S(1)}, bf16[128,1024]{1,0:T(8,128)(2,1)S(1)}, u32[]{:S(2)}, u32[]{:S(2)}) collective-permute-start(bf16[128,1024]{1,0:T(8,128)(2,1)S(1)} %get-tuple-element.82.act_ref), channel_id=1, source_target_pairs={{0,2},{1,3},{2,0},{3,1},{4,6},{5,7},{6,4},{7,5},{8,10},{9,11},{10,... | collective-permute-start | bytes 786440 | tf_op jit(solution)/shard_map/ppermute | solution.py:32
  18.8 2.5 %collective-permute-start.18 = (bf16[128,1024]{1,0:T(8,128)(2,1)S(1)}, bf16[128,1024]{1,0:T(8,128)(2,1)S(1)}, u32[]{:S(2)}, u32[]{:S(2)}) collective-permute-start(bf16[128,1024]{1,0:T(8,128)(2,1)S(1)} %get-tuple-element.82.act_ref), channel_id=1, source_target_pairs={{0,8},{1,9},{2,10},{3,11},{4,12},{5,13},{6,14},{7,15},{8,0},{9,1},... | collective-permute-start | bytes 786440 | tf_op jit(solution)/shard_map/ppermute | solution.py:32
  21.3 1.6 %collective-permute-start.17 = (bf16[128,1024]{1,0:T(8,128)(2,1)S(1)}, bf16[128,1024]{1,0:T(8,128)(2,1)S(1)}, u32[]{:S(2)}, u32[]{:S(2)}) collective-permute-start(bf16[128,1024]{1,0:T(8,128)(2,1)S(1)} %get-tuple-element.82.act_ref), channel_id=1, source_target_pairs={{0,4},{1,5},{2,6},{3,7},{4,0},{5,1},{6,2},{7,3},{8,12},{9,13},{10,... | collective-permute-start | bytes 786440 | tf_op jit(solution)/shard_map/ppermute | solution.py:32
  23.0 1.1 own_mix_phase.1.refs_0_.own_ref
  24.1 1.7 %collective-permute-done.16.refs_1_ = bf16[128,1024]{1,0:T(8,128)(2,1)S(1)} collective-permute-done((bf16[128,1024]{1,0:T(8,128)(2,1)S(1)}, bf16[128,1024]{1,0:T(8,128)(2,1)S(1)}, u32[]{:S(2)}, u32[]{:S(2)}) %collective-permute-start.16) | collective-permute-done | bytes 262176 | tf_op jit(solution)/shard_map/ppermute | solution.py:32
  25.8 1.8 %add_phase.10.refs_0_ = bf16[64,4096]{1,0:T(8,128)(2,1)S(1)} custom-call(bf16[256,4096]{1,0:T(8,128)(2,1)S(1)} %copy-done.3, bf16[256,4096]{1,0:T(8,128)(2,1)} %collective-permute-done.19.b, f32[128,1024]{1,0:T(8,128)S(1)} %own_mix_phase.1.refs_0_.own_ref, bf16[128,1024]{1,0:T(8,128)(2,1)S(1)} %collective-permute-done.16.refs_1_), custom_call_target="tpu_custom_call" | custom-call | tf_op jit(solution)/shard_map/add_phase/pallas_call | solution.py:282
  27.6 0.0 copy-start.21
  27.6 1.8 %collective-permute-start.21 = (bf16[64,4096]{1,0:T(8,128)(2,1)S(1)}, bf16[64,4096]{1,0:T(8,128)(2,1)S(1)}, u32[]{:S(2)}, u32[]{:S(2)}) collective-permute-start(bf16[64,4096]{1,0:T(8,128)(2,1)S(1)} %add_phase.10.refs_0_), channel_id=1, source_target_pairs={{0,2},{1,3},{2,0},{3,1},{4,6},{5,7},{6,4},{7,5},{8,10},{9,11},{10,... | collective-permute-start | bytes 1572872 | tf_op jit(solution)/shard_map/ppermute | solution.py:32
  29.4 2.6 %add_phase.11 = (bf16[64,4096]{1,0:T(8,128)(2,1)S(1)}, bf16[64,4096]{1,0:T(8,128)(2,1)S(1)}, bf16[64,4096]{1,0:T(8,128)(2,1)}) custom-call(bf16[256,4096]{1,0:T(8,128)(2,1)S(1)} %copy-done.3, bf16[256,4096]{1,0:T(8,128)(2,1)} %collective-permute-done.19.b, bf16[64,4096]{1,0:T(8,128)(2,1)S(1)} %add_phase.10.refs_0_), custom_call_target="tpu_custom_call" | custom-call | tf_op jit(solution)/shard_map/add_phase/pallas_call | solution.py:282
  31.9 1.9 %collective-permute-done.18.refs_3_ = bf16[128,1024]{1,0:T(8,128)(2,1)S(1)} collective-permute-done((bf16[128,1024]{1,0:T(8,128)(2,1)S(1)}, bf16[128,1024]{1,0:T(8,128)(2,1)S(1)}, u32[]{:S(2)}, u32[]{:S(2)}) %collective-permute-start.18) | collective-permute-done | bytes 262176 | tf_op jit(solution)/shard_map/ppermute | solution.py:32
  33.9 0.1 collective-permute-done.17.refs_2_
  34.0 7.0 %mix_phase.1 = (bf16[128,1024]{1,0:T(8,128)(2,1)S(1)}, bf16[64,4096]{1,0:T(8,128)(2,1)S(1)}, bf16[64,4096]{1,0:T(8,128)(2,1)S(1)}) custom-call(s32[1]{0:T(128)} %bitcast.me_ref, s32[7,8]{1,0:T(8,128)S(1)} %copy-done.20, f32[128,1024]{1,0:T(8,128)S(1)} %own_mix_phase.1.refs_0_.own_ref, bf16[128,1024]{1,0:T(8,128)(2,1)S(1)} %collective-permute-done.15.refs_0_, ...), custom_call_target="tpu_custom_call" | custom-call | flops 1073741824 | bytes 8388608 | tf_op jit(solution)/shard_map/mix_phase/pallas_call | solution.py:254
  41.1 0.1 collective-permute-start.20
  41.1 0.6 collective-permute-start.27
  41.8 0.1 add_phase.12
  41.9 2.3 %collective-permute-start.23 = (bf16[32,4096]{1,0:T(8,128)(2,1)S(1)}, bf16[32,4096]{1,0:T(8,128)(2,1)S(1)}, u32[]{:S(2)}, u32[]{:S(2)}) collective-permute-start(bf16[32,4096]{1,0:T(8,128)(2,1)S(1)} %get-tuple-element.89.refs_0_), channel_id=1, source_target_pairs={{0,8},{1,9},{2,10},{3,11},{4,12},{5,13},{6,14},{7,15},{8,0},{9,1},... | collective-permute-start | bytes 786440 | tf_op jit(solution)/shard_map/ppermute | solution.py:32
  44.2 0.8 add_phase.13
  45.0 0.7 copy-done.15
  45.7 1.4 %collective-permute-start.22 = (bf16[32,4096]{1,0:T(8,128)(2,1)}, bf16[32,4096]{1,0:T(8,128)(2,1)S(1)}, u32[]{:S(2)}, u32[]{:S(2)}) collective-permute-start(bf16[32,4096]{1,0:T(8,128)(2,1)} %get-tuple-element.92), channel_id=1, source_target_pairs={{0,2},{1,3},{2,0},{3,1},{4,6},{5,7},{6,4},{7,5},{8,10},{9,11},{10,... | collective-permute-start | bytes 786440 | tf_op jit(solution)/shard_map/ppermute | solution.py:32
  47.1 1.6 %collective-permute-start.14 = (f32[8,128]{1,0:T(8,128)S(1)}, f32[8,128]{1,0:T(8,128)S(1)}, u32[]{:S(2)}, u32[]{:S(2)}) collective-permute-start(f32[8,128]{1,0:T(8,128)S(1)} %get-tuple-element.81.refs_0_), channel_id=1, source_target_pairs={{0,16},{16,0},{1,17},{17,1},{2,18},{18,2},{3,19},{19,3},{4,20},{20... | collective-permute-start | bytes 12296 | tf_op jit(solution)/shard_map/ppermute | solution.py:855
  48.7 1.6 %collective-permute-start.29 = (bf16[32,4096]{1,0:T(8,128)(2,1)}, bf16[32,4096]{1,0:T(8,128)(2,1)}, u32[]{:S(2)}, u32[]{:S(2)}) collective-permute-start(bf16[32,4096]{1,0:T(8,128)(2,1)} %copy-done.17), channel_id=1, source_target_pairs={{0,12},{1,13},{2,14},{3,15},{4,8},{5,9},{6,10},{7,11},{8,4},{9,5},... | collective-permute-start | bytes 786440 | tf_op jit(solution)/shard_map/ppermute | solution.py:32
  50.3 6.0 %collective-permute-done.27.b = bf16[64,4096]{1,0:T(8,128)(2,1)} collective-permute-done((bf16[64,4096]{1,0:T(8,128)(2,1)}, bf16[64,4096]{1,0:T(8,128)(2,1)}, u32[]{:S(2)}, u32[]{:S(2)}) %collective-permute-start.27) | collective-permute-done | bytes 524320 | tf_op jit(solution)/shard_map/ppermute | solution.py:32
  56.3 1.8 %add_phase.15 = (bf16[32,4096]{1,0:T(8,128)(2,1)S(1)}, bf16[32,4096]{1,0:T(8,128)(2,1)}) custom-call(bf16[64,4096]{1,0:T(8,128)(2,1)S(1)} %get-tuple-element.97.a, bf16[64,4096]{1,0:T(8,128)(2,1)} %collective-permute-done.27.b, bf16[32,4096]{1,0:T(8,128)(2,1)S(1)} %get-tuple-element.89.refs_0_), custom_call_target="tpu_custom_call" | custom-call | tf_op jit(solution)/shard_map/add_phase/pallas_call | solution.py:282
  58.1 1.4 %collective-permute-start.28 = (bf16[32,4096]{1,0:T(8,128)(2,1)}, bf16[32,4096]{1,0:T(8,128)(2,1)S(1)}, u32[]{:S(2)}, u32[]{:S(2)}) collective-permute-start(bf16[32,4096]{1,0:T(8,128)(2,1)} %get-tuple-element.99), channel_id=1, source_target_pairs={{0,4},{1,5},{2,6},{3,7},{4,0},{5,1},{6,2},{7,3},{8,12},{9,13},{10,... | collective-permute-start | bytes 786440 | tf_op jit(solution)/shard_map/ppermute | solution.py:32
  59.5 3.7 %collective-permute-done.23.refs_0_.refs_6_ = bf16[32,4096]{1,0:T(8,128)(2,1)S(1)} collective-permute-done((bf16[32,4096]{1,0:T(8,128)(2,1)S(1)}, bf16[32,4096]{1,0:T(8,128)(2,1)S(1)}, u32[]{:S(2)}, u32[]{:S(2)}) %collective-permute-start.23) | collective-permute-done | bytes 262176 | tf_op jit(solution)/shard_map/ppermute | solution.py:32
  63.3 0.1 add_phase.14
  63.3 0.1 collective-permute-start.24
  63.4 2.0 %collective-permute-start.25 = (bf16[8,4096]{1,0:T(8,128)(2,1)S(1)}, bf16[8,4096]{1,0:T(8,128)(2,1)S(1)}, u32[]{:S(2)}, u32[]{:S(2)}) collective-permute-start(bf16[8,4096]{1,0:T(8,128)(2,1)S(1)} %get-tuple-element.95), channel_id=1, source_target_pairs={{0,8},{1,9},{2,10},{3,11},{4,12},{5,13},{6,14},{7,15},{8,0},{9,1},... | collective-permute-start | bytes 196616 | tf_op jit(solution)/shard_map/ppermute | solution.py:32
  65.5 2.3 %collective-permute-start.26 = (bf16[8,4096]{1,0:T(8,128)(2,1)S(1)}, bf16[8,4096]{1,0:T(8,128)(2,1)S(1)}, u32[]{:S(2)}, u32[]{:S(2)}) collective-permute-start(bf16[8,4096]{1,0:T(8,128)(2,1)S(1)} %get-tuple-element.96), channel_id=1, source_target_pairs={{0,12},{1,13},{2,14},{3,15},{4,8},{5,9},{6,10},{7,11},{8,4},{9,5},... | collective-permute-start | bytes 196616 | tf_op jit(solution)/shard_map/ppermute | solution.py:32
  67.8 0.1 copy.18.refs_10_
  67.9 0.1 copy.19.refs_12_
  68.0 0.5 slice.3
  69.2 2.4 %collective-permute-done.24.refs_1_ = bf16[8,4096]{1,0:T(8,128)(2,1)S(1)} collective-permute-done((bf16[8,4096]{1,0:T(8,128)(2,1)S(1)}, bf16[8,4096]{1,0:T(8,128)(2,1)S(1)}, u32[]{:S(2)}, u32[]{:S(2)}) %collective-permute-start.24) | collective-permute-done | bytes 65568 | tf_op jit(solution)/shard_map/ppermute | solution.py:32
  71.6 1.4 %collective-permute-done.25.refs_2_ = bf16[8,4096]{1,0:T(8,128)(2,1)S(1)} collective-permute-done((bf16[8,4096]{1,0:T(8,128)(2,1)S(1)}, bf16[8,4096]{1,0:T(8,128)(2,1)S(1)}, u32[]{:S(2)}, u32[]{:S(2)}) %collective-permute-start.25) | collective-permute-done | bytes 65568 | tf_op jit(solution)/shard_map/ppermute | solution.py:32
  73.1 0.9 copy-done.19
  74.0 2.3 %token_phase.1 = bf16[8,4224]{1,0:T(8,128)(2,1)S(1)} custom-call(s32[1]{0:T(128)} %bitcast.me_ref, bf16[8,4096]{1,0:T(8,128)(2,1)S(1)} %get-tuple-element.93.refs_0_, bf16[8,4096]{1,0:T(8,128)(2,1)S(1)} %collective-permute-done.24.refs_1_, bf16[8,4096]{1,0:T(8,128)(2,1)S(1)} %collective-permute-done.25.refs_2_, ...), custom_call_target="tpu_custom_call" | custom-call | tf_op jit(solution)/shard_map/token_phase/pallas_call | solution.py:609
  76.3 0.2 conditional.1
  76.5 1.6 %collective-permute-start.32 = (bf16[8,4224]{1,0:T(8,128)(2,1)S(1)}, bf16[8,4224]{1,0:T(8,128)(2,1)S(1)}, u32[]{:S(2)}, u32[]{:S(2)}) collective-permute-start(bf16[8,4224]{1,0:T(8,128)(2,1)S(1)} %get-tuple-element.142), channel_id=1, source_target_pairs={{0,12},{1,13},{2,14},{3,15},{4,8},{5,9},{6,10},{7,11},{8,4},{9,5},... | collective-permute-start | bytes 202760 | tf_op jit(solution)/shard_map/ppermute | solution.py:32
  78.1 1.2 collective-permute-start.31
  79.3 1.7 %collective-permute-start.30 = (bf16[8,4224]{1,0:T(8,128)(2,1)S(1)}, bf16[8,4224]{1,0:T(8,128)(2,1)S(1)}, u32[]{:S(2)}, u32[]{:S(2)}) collective-permute-start(bf16[8,4224]{1,0:T(8,128)(2,1)S(1)} %get-tuple-element.142), channel_id=1, source_target_pairs={{0,4},{1,5},{2,6},{3,7},{4,0},{5,1},{6,2},{7,3},{8,12},{9,13},{10,... | collective-permute-start | bytes 202760 | tf_op jit(solution)/shard_map/ppermute | solution.py:32
  80.9 2.5 %collective-permute-done.32 = bf16[8,4224]{1,0:T(8,128)(2,1)S(1)} collective-permute-done((bf16[8,4224]{1,0:T(8,128)(2,1)S(1)}, bf16[8,4224]{1,0:T(8,128)(2,1)S(1)}, u32[]{:S(2)}, u32[]{:S(2)}) %collective-permute-start.32) | collective-permute-done | bytes 67616 | tf_op jit(solution)/shard_map/ppermute | solution.py:32
  83.4 1.8 %collective-permute-done.31 = bf16[8,4224]{1,0:T(8,128)(2,1)S(1)} collective-permute-done((bf16[8,4224]{1,0:T(8,128)(2,1)S(1)}, bf16[8,4224]{1,0:T(8,128)(2,1)S(1)}, u32[]{:S(2)}, u32[]{:S(2)}) %collective-permute-start.31) | collective-permute-done | bytes 67616 | tf_op jit(solution)/shard_map/ppermute | solution.py:32
  85.2 1.5 %collective-permute-start.33 = (bf16[32,4224]{1,0:T(8,128)(2,1)S(1)}, bf16[32,4224]{1,0:T(8,128)(2,1)S(1)}, u32[]{:S(2)}, u32[]{:S(2)}) collective-permute-start(bf16[32,4224]{1,0:T(8,128)(2,1)S(1)} %pad_maximum_fusion.1), channel_id=1, source_target_pairs={{0,2},{1,3},{2,0},{3,1},{4,6},{5,7},{6,4},{7,5},{8,10},{9,11},{10,... | collective-permute-start | bytes 811016 | tf_op jit(solution)/shard_map/ppermute | solution.py:32
  86.8 6.6 %collective-permute-done.33 = bf16[32,4224]{1,0:T(8,128)(2,1)S(1)} collective-permute-done((bf16[32,4224]{1,0:T(8,128)(2,1)S(1)}, bf16[32,4224]{1,0:T(8,128)(2,1)S(1)}, u32[]{:S(2)}, u32[]{:S(2)}) %collective-permute-start.33) | collective-permute-done | bytes 270368 | tf_op jit(solution)/shard_map/ppermute | solution.py:32
  93.4 0.1 collective-permute-start.34
  93.5 1.9 %collective-permute-done.34 = bf16[64,4224]{1,0:T(8,128)(2,1)S(1)} collective-permute-done((bf16[64,4224]{1,0:T(8,128)(2,1)S(1)}, bf16[64,4224]{1,0:T(8,128)(2,1)S(1)}, u32[]{:S(2)}, u32[]{:S(2)}) %collective-permute-start.34) | collective-permute-done | bytes 540704 | tf_op jit(solution)/shard_map/ppermute | solution.py:32
  95.5 0.0 copy-start.1
  95.5 0.0 copy-start.10
  95.5 7.5 %mixed_grad_phase.1 = (f32[1,1]{1,0:T(1,128)}, bf16[128,1024]{1,0:T(8,128)(2,1)S(1)}, bf16[128,1024]{1,0:T(8,128)(2,1)S(1)}, bf16[128,1024]{1,0:T(8,128)(2,1)S(1...) custom-call(s32[1]{0:T(128)} %bitcast.me_ref, s32[7,8]{1,0:T(8,128)S(1)} %copy-done.20, ...), custom_call_target="tpu_custom_call" | custom-call | flops 1073741824 | bytes 8388608 | tf_op jit(solution)/shard_map/mixed_grad_phase/pallas_call | solution.py:669
  103.1 0.4 collective-permute-start.35
  103.5 2.8 %collective-permute-start.36 = (bf16[128,1024]{1,0:T(8,128)(2,1)S(1)}, bf16[128,1024]{1,0:T(8,128)(2,1)S(1)}, u32[]{:S(2)}, u32[]{:S(2)}) collective-permute-start(bf16[128,1024]{1,0:T(8,128)(2,1)S(1)} %get-tuple-element.106), channel_id=1, source_target_pairs={{0,4},{1,5},{2,6},{3,7},{4,0},{5,1},{6,2},{7,3},{8,12},{9,13},{10,... | collective-permute-start | bytes 786440 | tf_op jit(solution)/shard_map/ppermute | solution.py:32
  106.3 1.6 %collective-permute-start.37 = (bf16[128,1024]{1,0:T(8,128)(2,1)S(1)}, bf16[128,1024]{1,0:T(8,128)(2,1)S(1)}, u32[]{:S(2)}, u32[]{:S(2)}) collective-permute-start(bf16[128,1024]{1,0:T(8,128)(2,1)S(1)} %get-tuple-element.107), channel_id=1, source_target_pairs={{0,2},{1,3},{2,0},{3,1},{4,6},{5,7},{6,4},{7,5},{8,10},{9,11},{10,... | collective-permute-start | bytes 786440 | tf_op jit(solution)/shard_map/ppermute | solution.py:32
  107.9 5.5 %block_grad_phase.1 = (f32[8,128,128]{2,1,0:T(8,128)}, f32[7,8,128,128]{3,2,1,0:T(8,128)}, f32[128,1024]{1,0:T(8,128)S(1)}) custom-call(s32[7,8]{1,0:T(8,128)S(1)} %copy-done.20, bf16[128,1024]{1,0:T(8,128)(2,1)S(1)} %copy-done.12, bf16[128,1024]{1,0:T(8,128)(2,1)S(1)} %get-tuple-element.103.mg, bf16[128,1024]{1,0:T(8,128)(2,1)S(1)} %copy-done.8, ...), custom_call_target="tpu_custom_call" | custom-call | flops 402653184 | bytes 12582912 | tf_op jit(solution)/shard_map/block_grad_phase/pallas_call | solution.py:714
  113.3 6.4 %down_grad_phase.1 = f32[1024,4096]{1,0:T(8,128)} custom-call(bf16[128,1024]{1,0:T(8,128)(2,1)S(1)} %get-tuple-element.109.mixed_ref, bf16[128,4224]{1,0:T(8,128)(2,1)S(1)} %constant_dynamic-update-slice_fusion.16.grad_ref), custom_call_target="tpu_custom_call" | custom-call | flops 1073741824 | bytes 16777216 | tf_op jit(solution)/shard_map/down_grad_phase/pallas_call | solution.py:756
  119.8 6.6 %up_grad_phase.1 = f32[4096,1024]{1,0:T(8,128)} custom-call(bf16[128,4096]{1,0:T(8,128)(2,1)S(1)} %copy-done.4, f32[128,1024]{1,0:T(8,128)S(1)} %copy-done.14, f32[128,1024]{1,0:T(8,128)S(1)} %get-tuple-element.104.grad_ref, bf16[128,1024]{1,0:T(8,128)(2,1)S(1)} %collective-permute-done.35.refs_0_, bf16[128,1024]{1,0:T(8,128)(2,1)S(1)} %collective-permute-done.36.refs_1_, ...), custom_call_target="tpu_custom_call" | custom-call | flops 1073741824 | bytes 16777216 | tf_op jit(solution)/shard_map/up_grad_phase/pallas_call | solution.py:800
  (67 shorter events, 0.3 us)
Async XLA Ops:
  0.6 11.3 %copy-start.27 = (s32[32,8]{0,1:T(8,128)S(1)}, s32[32,8]{0,1:T(8,128)}, u32[]{:S(2)}) copy-start(s32[32,8]{0,1:T(8,128)} %param.16) | copy-start | bytes 3076
  0.6 11.4 %copy-start.4 = (bf16[128,4096]{1,0:T(8,128)(2,1)S(1)}, bf16[128,4096]{1,0:T(8,128)(2,1)}, u32[]{:S(2)}) copy-start(bf16[128,4096]{1,0:T(8,128)(2,1)} %tok.3) | copy-start | bytes 3145732
  10.2 1.3 %copy-start.2 = (bf16[256,4096]{1,0:T(8,128)(2,1)}, bf16[256,4096]{1,0:T(8,128)(2,1)S(1)}, u32[]{:S(2)}) copy-start(bf16[256,4096]{1,0:T(8,128)(2,1)S(1)} %get-tuple-element.83.a) | copy-start | bytes 6291460
  11.5 14.3 %collective-permute-start.19 = (bf16[256,4096]{1,0:T(8,128)(2,1)}, bf16[256,4096]{1,0:T(8,128)(2,1)}, u32[]{:S(2)}, u32[]{:S(2)}) collective-permute-start(bf16[256,4096]{1,0:T(8,128)(2,1)} %get-tuple-element.84), channel_id=1, source_target_pairs={{0,1},{1,0},{2,3},{3,2},{4,5},{5,4},{6,7},{7,6},{8,9},{9,8},{10,11... | collective-permute-start | bytes 6291464 | tf_op jit(solution)/shard_map/ppermute | solution.py:32
  12.1 10.9 %copy-start = (bf16[7,8,128,128]{3,2,1,0:T(8,128)(2,1)S(1)}, bf16[7,8,128,128]{3,2,1,0:T(8,128)(2,1)}, u32[]{:S(2)}) copy-start(bf16[7,8,128,128]{3,2,1,0:T(8,128)(2,1)} %refs_5_.3) | copy-start | bytes 5505028
  12.1 10.9 %copy-start.9 = (bf16[8,128,128]{2,1,0:T(8,128)(2,1)S(1)}, bf16[8,128,128]{2,1,0:T(8,128)(2,1)}, u32[]{:S(2)}) copy-start(bf16[8,128,128]{2,1,0:T(8,128)(2,1)} %refs_4_.3) | copy-start | bytes 786436
  12.1 10.9 %copy-start.20 = (s32[7,8]{1,0:T(8,128)S(1)}, s32[7,8]{1,0:T(8,128)}, u32[]{:S(2)}) copy-start(s32[7,8]{1,0:T(8,128)} %pat.7) | copy-start | bytes 676
  16.2 7.9 %copy-start.11 = (bf16[128,1024]{1,0:T(8,128)(2,1)}, bf16[128,1024]{1,0:T(8,128)(2,1)S(1)}, u32[]{:S(2)}) copy-start(bf16[128,1024]{1,0:T(8,128)(2,1)S(1)} %get-tuple-element.82.act_ref) | copy-start | bytes 786436
  16.2 7.9 %copy-start.13 = (f32[128,1024]{1,0:T(8,128)}, f32[128,1024]{1,0:T(8,128)S(1)}, u32[]{:S(2)}) copy-start(f32[128,1024]{1,0:T(8,128)S(1)} %get-tuple-element.102.pre_ref) | copy-start | bytes 1572868
  16.2 9.6 %copy-start.3 = (bf16[256,4096]{1,0:T(8,128)(2,1)S(1)}, bf16[256,4096]{1,0:T(8,128)(2,1)}, u32[]{:S(2)}) copy-start(bf16[256,4096]{1,0:T(8,128)(2,1)} %copy-done.2) | copy-start | bytes 6291460
  16.2 9.6 %collective-permute-start.16 = (bf16[128,1024]{1,0:T(8,128)(2,1)S(1)}, bf16[128,1024]{1,0:T(8,128)(2,1)S(1)}, u32[]{:S(2)}, u32[]{:S(2)}) collective-permute-start(bf16[128,1024]{1,0:T(8,128)(2,1)S(1)} %get-tuple-element.82.act_ref), channel_id=1, source_target_pairs={{0,2},{1,3},{2,0},{3,1},{4,6},{5,7},{6,4},{7,5},{8,10},{9,11},{10,... | collective-permute-start | bytes 786440 | tf_op jit(solution)/shard_map/ppermute | solution.py:32
  18.8 15.1 %collective-permute-start.18 = (bf16[128,1024]{1,0:T(8,128)(2,1)S(1)}, bf16[128,1024]{1,0:T(8,128)(2,1)S(1)}, u32[]{:S(2)}, u32[]{:S(2)}) collective-permute-start(bf16[128,1024]{1,0:T(8,128)(2,1)S(1)} %get-tuple-element.82.act_ref), channel_id=1, source_target_pairs={{0,8},{1,9},{2,10},{3,11},{4,12},{5,13},{6,14},{7,15},{8,0},{9,1},... | collective-permute-start | bytes 786440 | tf_op jit(solution)/shard_map/ppermute | solution.py:32
  21.3 12.7 %collective-permute-start.17 = (bf16[128,1024]{1,0:T(8,128)(2,1)S(1)}, bf16[128,1024]{1,0:T(8,128)(2,1)S(1)}, u32[]{:S(2)}, u32[]{:S(2)}) collective-permute-start(bf16[128,1024]{1,0:T(8,128)(2,1)S(1)} %get-tuple-element.82.act_ref), channel_id=1, source_target_pairs={{0,4},{1,5},{2,6},{3,7},{4,0},{5,1},{6,2},{7,3},{8,12},{9,13},{10,... | collective-permute-start | bytes 786440 | tf_op jit(solution)/shard_map/ppermute | solution.py:32
  23.0 11.0 %collective-permute-start.15 = (bf16[128,1024]{1,0:T(8,128)(2,1)S(1)}, bf16[128,1024]{1,0:T(8,128)(2,1)S(1)}, u32[]{:S(2)}, u32[]{:S(2)}) collective-permute-start(bf16[128,1024]{1,0:T(8,128)(2,1)S(1)} %get-tuple-element.82.act_ref), channel_id=1, source_target_pairs={{0,1},{1,0},{2,3},{3,2},{4,5},{5,4},{6,7},{7,6},{8,9},{9,8},{10,11... | collective-permute-start | bytes 786440 | tf_op jit(solution)/shard_map/ppermute | solution.py:32
  27.6 6.5 %copy-start.21 = (s32[8,32]{1,0:T(8,128)S(1)}, s32[8,32]{1,0:T(8,128)}, u32[]{:S(2)}) copy-start(s32[8,32]{1,0:T(8,128)} %sc.2) | copy-start | bytes 3076
  27.6 14.2 %collective-permute-start.21 = (bf16[64,4096]{1,0:T(8,128)(2,1)S(1)}, bf16[64,4096]{1,0:T(8,128)(2,1)S(1)}, u32[]{:S(2)}, u32[]{:S(2)}) collective-permute-start(bf16[64,4096]{1,0:T(8,128)(2,1)S(1)} %add_phase.10.refs_0_), channel_id=1, source_target_pairs={{0,2},{1,3},{2,0},{3,1},{4,6},{5,7},{6,4},{7,5},{8,10},{9,11},{10,... | collective-permute-start | bytes 1572872 | tf_op jit(solution)/shard_map/ppermute | solution.py:32
  34.0 7.0 %copy-start.5 = (bf16[128,1024]{1,0:T(8,128)(2,1)}, bf16[128,1024]{1,0:T(8,128)(2,1)S(1)}, u32[]{:S(2)}) copy-start(bf16[128,1024]{1,0:T(8,128)(2,1)S(1)} %collective-permute-done.17.refs_2_) | copy-start | bytes 786436
  34.0 7.0 %copy-start.7 = (bf16[128,1024]{1,0:T(8,128)(2,1)}, bf16[128,1024]{1,0:T(8,128)(2,1)S(1)}, u32[]{:S(2)}) copy-start(bf16[128,1024]{1,0:T(8,128)(2,1)S(1)} %collective-permute-done.15.refs_0_) | copy-start | bytes 786436
  41.1 3.1 %collective-permute-start.20 = (bf16[64,4096]{1,0:T(8,128)(2,1)S(1)}, bf16[64,4096]{1,0:T(8,128)(2,1)S(1)}, u32[]{:S(2)}, u32[]{:S(2)}) collective-permute-start(bf16[64,4096]{1,0:T(8,128)(2,1)S(1)} %get-tuple-element.87), channel_id=1, source_target_pairs={{0,1},{1,0},{2,3},{3,2},{4,5},{5,4},{6,7},{7,6},{8,9},{9,8},{10,11... | collective-permute-start | bytes 1572872 | tf_op jit(solution)/shard_map/ppermute | solution.py:32
  41.1 15.1 %collective-permute-start.27 = (bf16[64,4096]{1,0:T(8,128)(2,1)}, bf16[64,4096]{1,0:T(8,128)(2,1)}, u32[]{:S(2)}, u32[]{:S(2)}) collective-permute-start(bf16[64,4096]{1,0:T(8,128)(2,1)} %get-tuple-element.85.refs_7_), channel_id=1, source_target_pairs={{0,2},{1,3},{2,0},{3,1},{4,6},{5,7},{6,4},{7,5},{8,10},{9,11},{10,... | collective-permute-start | bytes 1572872 | tf_op jit(solution)/shard_map/ppermute | solution.py:32
  41.9 3.1 %copy-start.17 = (bf16[32,4096]{1,0:T(8,128)(2,1)}, bf16[32,4096]{1,0:T(8,128)(2,1)S(1)}, u32[]{:S(2)}) copy-start(bf16[32,4096]{1,0:T(8,128)(2,1)S(1)} %get-tuple-element.90.refs_1_) | copy-start | bytes 786436
  41.9 21.4 %collective-permute-start.23 = (bf16[32,4096]{1,0:T(8,128)(2,1)S(1)}, bf16[32,4096]{1,0:T(8,128)(2,1)S(1)}, u32[]{:S(2)}, u32[]{:S(2)}) collective-permute-start(bf16[32,4096]{1,0:T(8,128)(2,1)S(1)} %get-tuple-element.89.refs_0_), channel_id=1, source_target_pairs={{0,8},{1,9},{2,10},{3,11},{4,12},{5,13},{6,14},{7,15},{8,0},{9,1},... | collective-permute-start | bytes 786440 | tf_op jit(solution)/shard_map/ppermute | solution.py:32
  45.0 0.7 copy-start.15
  45.7 17.6 %copy-start.16 = (bf16[32,4096]{1,0:T(8,128)(2,1)S(1)}, bf16[32,4096]{1,0:T(8,128)(2,1)}, u32[]{:S(2)}) copy-start(bf16[32,4096]{1,0:T(8,128)(2,1)} %copy-done.15) | copy-start | bytes 786436
  45.7 17.6 %collective-permute-start.22 = (bf16[32,4096]{1,0:T(8,128)(2,1)}, bf16[32,4096]{1,0:T(8,128)(2,1)S(1)}, u32[]{:S(2)}, u32[]{:S(2)}) collective-permute-start(bf16[32,4096]{1,0:T(8,128)(2,1)} %get-tuple-element.92), channel_id=1, source_target_pairs={{0,2},{1,3},{2,0},{3,1},{4,6},{5,7},{6,4},{7,5},{8,10},{9,11},{10,... | collective-permute-start | bytes 786440 | tf_op jit(solution)/shard_map/ppermute | solution.py:32
  47.1 18.3 %collective-permute-start.14 = (f32[8,128]{1,0:T(8,128)S(1)}, f32[8,128]{1,0:T(8,128)S(1)}, u32[]{:S(2)}, u32[]{:S(2)}) collective-permute-start(f32[8,128]{1,0:T(8,128)S(1)} %get-tuple-element.81.refs_0_), channel_id=1, source_target_pairs={{0,16},{16,0},{1,17},{17,1},{2,18},{18,2},{3,19},{19,3},{4,20},{20... | collective-permute-start | bytes 12296 | tf_op jit(solution)/shard_map/ppermute | solution.py:855
  48.7 24.4 %collective-permute-start.29 = (bf16[32,4096]{1,0:T(8,128)(2,1)}, bf16[32,4096]{1,0:T(8,128)(2,1)}, u32[]{:S(2)}, u32[]{:S(2)}) collective-permute-start(bf16[32,4096]{1,0:T(8,128)(2,1)} %copy-done.17), channel_id=1, source_target_pairs={{0,12},{1,13},{2,14},{3,15},{4,8},{5,9},{6,10},{7,11},{8,4},{9,5},... | collective-permute-start | bytes 786440 | tf_op jit(solution)/shard_map/ppermute | solution.py:32
  56.2 11.6 %copy-start.25 = (s32[128,8]{0,1:T(8,128)S(1)}, s32[128,8]{0,1:T(8,128)}, u32[]{:S(2)}) copy-start(s32[128,8]{0,1:T(8,128)} %param.24) | copy-start | bytes 12292
  56.3 11.7 %copy-start.26 = (f32[128,8]{0,1:T(8,128)S(1)}, f32[128,8]{0,1:T(8,128)}, u32[]{:S(2)}) copy-start(f32[128,8]{0,1:T(8,128)} %param.25) | copy-start | bytes 12292
  56.3 16.8 %copy-start.22 = (f32[4096]{0:T(1024)S(1)}, f32[4096]{0:T(1024)}, u32[]{:S(2)}) copy-start(f32[4096]{0:T(1024)} %param.22) | copy-start | bytes 49156
  58.1 9.7 %copy-start.18 = (bf16[32,4096]{1,0:T(8,128)(2,1)}, bf16[32,4096]{1,0:T(8,128)(2,1)S(1)}, u32[]{:S(2)}) copy-start(bf16[32,4096]{1,0:T(8,128)(2,1)S(1)} %get-tuple-element.98.refs_4_) | copy-start | bytes 786436
  58.1 14.9 %collective-permute-start.28 = (bf16[32,4096]{1,0:T(8,128)(2,1)}, bf16[32,4096]{1,0:T(8,128)(2,1)S(1)}, u32[]{:S(2)}, u32[]{:S(2)}) collective-permute-start(bf16[32,4096]{1,0:T(8,128)(2,1)} %get-tuple-element.99), channel_id=1, source_target_pairs={{0,4},{1,5},{2,6},{3,7},{4,0},{5,1},{6,2},{7,3},{8,12},{9,13},{10,... | collective-permute-start | bytes 786440 | tf_op jit(solution)/shard_map/ppermute | solution.py:32
  63.3 8.3 %collective-permute-start.24 = (bf16[8,4096]{1,0:T(8,128)(2,1)S(1)}, bf16[8,4096]{1,0:T(8,128)(2,1)S(1)}, u32[]{:S(2)}, u32[]{:S(2)}) collective-permute-start(bf16[8,4096]{1,0:T(8,128)(2,1)S(1)} %get-tuple-element.94), channel_id=1, source_target_pairs={{0,4},{1,5},{2,6},{3,7},{4,0},{5,1},{6,2},{7,3},{8,12},{9,13},{10,... | collective-permute-start | bytes 196616 | tf_op jit(solution)/shard_map/ppermute | solution.py:32
  63.4 9.6 %collective-permute-start.25 = (bf16[8,4096]{1,0:T(8,128)(2,1)S(1)}, bf16[8,4096]{1,0:T(8,128)(2,1)S(1)}, u32[]{:S(2)}, u32[]{:S(2)}) collective-permute-start(bf16[8,4096]{1,0:T(8,128)(2,1)S(1)} %get-tuple-element.95), channel_id=1, source_target_pairs={{0,8},{1,9},{2,10},{3,11},{4,12},{5,13},{6,14},{7,15},{8,0},{9,1},... | collective-permute-start | bytes 196616 | tf_op jit(solution)/shard_map/ppermute | solution.py:32
  65.5 7.6 %collective-permute-start.26 = (bf16[8,4096]{1,0:T(8,128)(2,1)S(1)}, bf16[8,4096]{1,0:T(8,128)(2,1)S(1)}, u32[]{:S(2)}, u32[]{:S(2)}) collective-permute-start(bf16[8,4096]{1,0:T(8,128)(2,1)S(1)} %get-tuple-element.96), channel_id=1, source_target_pairs={{0,12},{1,13},{2,14},{3,15},{4,8},{5,9},{6,10},{7,11},{8,4},{9,5},... | collective-permute-start | bytes 196616 | tf_op jit(solution)/shard_map/ppermute | solution.py:32
  73.1 1.0 copy-start.19
  76.5 6.9 %collective-permute-start.32 = (bf16[8,4224]{1,0:T(8,128)(2,1)S(1)}, bf16[8,4224]{1,0:T(8,128)(2,1)S(1)}, u32[]{:S(2)}, u32[]{:S(2)}) collective-permute-start(bf16[8,4224]{1,0:T(8,128)(2,1)S(1)} %get-tuple-element.142), channel_id=1, source_target_pairs={{0,12},{1,13},{2,14},{3,15},{4,8},{5,9},{6,10},{7,11},{8,4},{9,5},... | collective-permute-start | bytes 202760 | tf_op jit(solution)/shard_map/ppermute | solution.py:32
  78.1 7.1 %collective-permute-start.31 = (bf16[8,4224]{1,0:T(8,128)(2,1)S(1)}, bf16[8,4224]{1,0:T(8,128)(2,1)S(1)}, u32[]{:S(2)}, u32[]{:S(2)}) collective-permute-start(bf16[8,4224]{1,0:T(8,128)(2,1)S(1)} %get-tuple-element.142), channel_id=1, source_target_pairs={{0,8},{1,9},{2,10},{3,11},{4,12},{5,13},{6,14},{7,15},{8,0},{9,1},... | collective-permute-start | bytes 202760 | tf_op jit(solution)/shard_map/ppermute | solution.py:32
  79.3 5.9 %collective-permute-start.30 = (bf16[8,4224]{1,0:T(8,128)(2,1)S(1)}, bf16[8,4224]{1,0:T(8,128)(2,1)S(1)}, u32[]{:S(2)}, u32[]{:S(2)}) collective-permute-start(bf16[8,4224]{1,0:T(8,128)(2,1)S(1)} %get-tuple-element.142), channel_id=1, source_target_pairs={{0,4},{1,5},{2,6},{3,7},{4,0},{5,1},{6,2},{7,3},{8,12},{9,13},{10,... | collective-permute-start | bytes 202760 | tf_op jit(solution)/shard_map/ppermute | solution.py:32
  85.2 8.2 %collective-permute-start.33 = (bf16[32,4224]{1,0:T(8,128)(2,1)S(1)}, bf16[32,4224]{1,0:T(8,128)(2,1)S(1)}, u32[]{:S(2)}, u32[]{:S(2)}) collective-permute-start(bf16[32,4224]{1,0:T(8,128)(2,1)S(1)} %pad_maximum_fusion.1), channel_id=1, source_target_pairs={{0,2},{1,3},{2,0},{3,1},{4,6},{5,7},{6,4},{7,5},{8,10},{9,11},{10,... | collective-permute-start | bytes 811016 | tf_op jit(solution)/shard_map/ppermute | solution.py:32
  93.4 2.0 %collective-permute-start.34 = (bf16[64,4224]{1,0:T(8,128)(2,1)S(1)}, bf16[64,4224]{1,0:T(8,128)(2,1)S(1)}, u32[]{:S(2)}, u32[]{:S(2)}) collective-permute-start(bf16[64,4224]{1,0:T(8,128)(2,1)S(1)} %get-tuple-element.132), channel_id=1, source_target_pairs={{0,1},{1,0},{2,3},{3,2},{4,5},{5,4},{6,7},{7,6},{8,9},{9,8},{10,11... | collective-permute-start | bytes 1622024 | tf_op jit(solution)/shard_map/ppermute | solution.py:32
  95.5 12.4 %copy-start.1 = (bf16[7,8,128,128]{3,2,1,0:T(8,128)(2,1)S(1)}, bf16[7,8,128,128]{3,2,1,0:T(8,128)(2,1)}, u32[]{:S(2)}) copy-start(bf16[7,8,128,128]{3,2,1,0:T(8,128)(2,1)} %refs_5_.3) | copy-start | bytes 5505028
  95.5 12.4 %copy-start.6 = (bf16[128,1024]{1,0:T(8,128)(2,1)S(1)}, bf16[128,1024]{1,0:T(8,128)(2,1)}, u32[]{:S(2)}) copy-start(bf16[128,1024]{1,0:T(8,128)(2,1)} %copy-done.5) | copy-start | bytes 786436
  95.5 12.4 %copy-start.8 = (bf16[128,1024]{1,0:T(8,128)(2,1)S(1)}, bf16[128,1024]{1,0:T(8,128)(2,1)}, u32[]{:S(2)}) copy-start(bf16[128,1024]{1,0:T(8,128)(2,1)} %copy-done.7) | copy-start | bytes 786436
  95.5 12.4 %copy-start.10 = (bf16[8,128,128]{2,1,0:T(8,128)(2,1)S(1)}, bf16[8,128,128]{2,1,0:T(8,128)(2,1)}, u32[]{:S(2)}) copy-start(bf16[8,128,128]{2,1,0:T(8,128)(2,1)} %refs_4_.3) | copy-start | bytes 786436
  95.5 12.4 %copy-start.12 = (bf16[128,1024]{1,0:T(8,128)(2,1)S(1)}, bf16[128,1024]{1,0:T(8,128)(2,1)}, u32[]{:S(2)}) copy-start(bf16[128,1024]{1,0:T(8,128)(2,1)} %copy-done.11) | copy-start | bytes 786436
  103.1 16.6 %collective-permute-start.35 = (bf16[128,1024]{1,0:T(8,128)(2,1)S(1)}, bf16[128,1024]{1,0:T(8,128)(2,1)S(1)}, u32[]{:S(2)}, u32[]{:S(2)}) collective-permute-start(bf16[128,1024]{1,0:T(8,128)(2,1)S(1)} %get-tuple-element.105), channel_id=1, source_target_pairs={{0,8},{1,9},{2,10},{3,11},{4,12},{5,13},{6,14},{7,15},{8,0},{9,1},... | collective-permute-start | bytes 786440 | tf_op jit(solution)/shard_map/ppermute | solution.py:32
  103.5 16.3 %collective-permute-start.36 = (bf16[128,1024]{1,0:T(8,128)(2,1)S(1)}, bf16[128,1024]{1,0:T(8,128)(2,1)S(1)}, u32[]{:S(2)}, u32[]{:S(2)}) collective-permute-start(bf16[128,1024]{1,0:T(8,128)(2,1)S(1)} %get-tuple-element.106), channel_id=1, source_target_pairs={{0,4},{1,5},{2,6},{3,7},{4,0},{5,1},{6,2},{7,3},{8,12},{9,13},{10,... | collective-permute-start | bytes 786440 | tf_op jit(solution)/shard_map/ppermute | solution.py:32
  106.3 13.5 %collective-permute-start.37 = (bf16[128,1024]{1,0:T(8,128)(2,1)S(1)}, bf16[128,1024]{1,0:T(8,128)(2,1)S(1)}, u32[]{:S(2)}, u32[]{:S(2)}) collective-permute-start(bf16[128,1024]{1,0:T(8,128)(2,1)S(1)} %get-tuple-element.107), channel_id=1, source_target_pairs={{0,2},{1,3},{2,0},{3,1},{4,6},{5,7},{6,4},{7,5},{8,10},{9,11},{10,... | collective-permute-start | bytes 786440 | tf_op jit(solution)/shard_map/ppermute | solution.py:32
  107.9 11.9 %collective-permute-start.38 = (bf16[128,1024]{1,0:T(8,128)(2,1)S(1)}, bf16[128,1024]{1,0:T(8,128)(2,1)S(1)}, u32[]{:S(2)}, u32[]{:S(2)}) collective-permute-start(bf16[128,1024]{1,0:T(8,128)(2,1)S(1)} %get-tuple-element.108), channel_id=1, source_target_pairs={{0,1},{1,0},{2,3},{3,2},{4,5},{5,4},{6,7},{7,6},{8,9},{9,8},{10,11... | collective-permute-start | bytes 786440 | tf_op jit(solution)/shard_map/ppermute | solution.py:32
  113.3 6.4 %copy-start.14 = (f32[128,1024]{1,0:T(8,128)S(1)}, f32[128,1024]{1,0:T(8,128)}, u32[]{:S(2)}) copy-start(f32[128,1024]{1,0:T(8,128)} %copy-done.13) | copy-start | bytes 1572868
